TPU v7x, 256 devices: a whole 4x4x8 slice. The times are simulated.
256 devices in a mesh: fsdp: 16 (over y, x), ctx: 16 (over z, core).
Axes of the slice: x: 4, y: 4, z: 8, core: 2. Of those that a mesh axis runs over, the one named last changes fastest.
Arguments:
- queries: bfloat16 [32768, 2048], P(('fsdp', 'ctx')), may hold values from -80 to 80
- keys: bfloat16 [32768, 2048], P(('fsdp', 'ctx')), may hold values from -4 to 4
- values: bfloat16 [32768, 2048], P(('fsdp', 'ctx')), may hold values from -6 to 6
- out_weight: bfloat16 [2048, 4096], P('fsdp'), may hold values from -0.125 to 0.125
- sessions: int32 [16, 2048], P('fsdp'), may hold values from 0 to 2, never falling along the last dimension, each value on 1 to 1536 neighbouring positions
Outputs:
- output: bfloat16 [32768, 4096], P(('fsdp', 'ctx'))
Inputs may be any that keep to these rules, and one draw needn't show every extreme that they name: Along each slab the session number never falls; each of the 3 sessions holds 1 to 1536 tokens and one holds exactly 1536.
All inputs are finite; a program needn't handle non-finite values.
Results may differ from a plain program's by a relative error of at most 0.007.
Values may be sent and summed in bfloat16 or wider, within the bound.
No kernel may reach another device: no remote copies, remote signals or barrier semaphores. Data moves between devices by JAX's collectives and lax.ppermute only.
A program may use at most 128 MiB of HBM per device.

v0:
```python
import math

import jax
import jax.numpy as jnp
from jax import lax
from jax.sharding import PartitionSpec as P

HDIM = 128


def per_device(queries, keys, values, out_weight, sessions):
    tokens_here = queries.shape[0]
    width = queries.shape[1]
    heads_here = width // HDIM
    scale = 1.0 / math.sqrt(HDIM)
    slab_ids = sessions[0]
    first_token = lax.axis_index("ctx") * tokens_here
    my_positions = first_token + jnp.arange(tokens_here, dtype=jnp.int32)
    my_ids = lax.dynamic_slice_in_dim(slab_ids, first_token, tokens_here)
    query_heads = jnp.transpose(queries.reshape(tokens_here, heads_here, HDIM), (1, 0, 2))
    start_state = (
        jnp.full((heads_here, tokens_here), -1e30, jnp.float32),
        jnp.zeros((heads_here, tokens_here), jnp.float32),
        jnp.zeros((heads_here, tokens_here, HDIM), jnp.float32),
    )
    key_piece = lax.all_gather(keys, "ctx", axis=0, tiled=True)
    value_piece = lax.all_gather(values, "ctx", axis=0, tiled=True)
    count = key_piece.shape[0]
    key_positions = jnp.arange(count, dtype=jnp.int32)
    allowed = (my_ids[:, None] == slab_ids[None, :]) & (
        key_positions[None, :] <= my_positions[:, None]
    )

    def update(current):
        key_heads = jnp.transpose(key_piece.reshape(count, heads_here, HDIM), (1, 0, 2))
        value_heads = jnp.transpose(value_piece.reshape(count, heads_here, HDIM), (1, 0, 2))

        def one_head(operands):
            query_head, key_head, value_head, row_max, row_total, accum = operands
            scores = jnp.dot(query_head, key_head.T, preferred_element_type=jnp.float32) * scale
            scores = jnp.where(allowed, scores, jnp.float32(-1e30))
            new_max = jnp.maximum(row_max, jnp.max(scores, axis=1))
            weights = jnp.where(allowed, jnp.exp(scores - new_max[:, None]), jnp.float32(0.0))
            factor = jnp.exp(row_max - new_max)
            new_total = row_total * factor + jnp.sum(weights, axis=1)
            added = jnp.dot(
                weights.astype(jnp.bfloat16), value_head, preferred_element_type=jnp.float32
            )
            return (new_max, new_total, accum * factor[:, None] + added)

        return lax.map(one_head, (query_heads, key_heads, value_heads) + tuple(current))

    row_max, row_total, accum = lax.cond(
        jnp.any(allowed), update, lambda current: current, start_state
    )
    finished = accum / row_total[:, :, None]
    attended = jnp.transpose(finished, (1, 0, 2)).reshape(tokens_here, width).astype(jnp.bfloat16)
    piece = lax.all_gather(out_weight, "fsdp", axis=0, tiled=True)
    projected = jnp.dot(attended, piece, preferred_element_type=jnp.float32)
    return projected.astype(jnp.bfloat16)


def solution(mesh):
    return jax.shard_map(
        per_device,
        mesh=mesh,
        in_specs=(
            P(("fsdp", "ctx"), None),
            P(("fsdp", "ctx"), None),
            P(("fsdp", "ctx"), None),
            P("fsdp", None),
            P("fsdp", None),
        ),
        out_specs=P(("fsdp", "ctx"), None),
        check_vma=False,
    )
```

profile of v0, /device:TPU:1, one launch (start us, length us, event | category | flops | bytes accessed | tf_op | source)
XLA Modules:
  0.0 274.5 jit_solution(3808026801106439446)
XLA Ops:
  6.5 2.0 copy.8
  8.7 2.0 copy.9
  12.1 1.7 fusion.16
  14.4 1.3 copy.10
  15.7 63.8 %all-gather.4.cloned.1.call-done = bf16[2048,2048]{0,1:T(8,128)(2,1)} async-done(((bf16[128,2048]{0,1:T(8,128)(2,1)}), bf16[2048,2048]{0,1:T(8,128)(2,1)}) %all-gather.4.cloned.1.call-update) | async-done | bytes 8388624 | tf_op jit(solution)/shard_map/all_gather | solution.py:26
  79.5 64.4 %all-gather.6.cloned.1.call-done = bf16[2048,2048]{0,1:T(8,128)(2,1)} async-done(((bf16[128,2048]{0,1:T(8,128)(2,1)}), bf16[2048,2048]{0,1:T(8,128)(2,1)}) %all-gather.6.cloned.1.call-update) | async-done | bytes 8388624 | tf_op jit(solution)/shard_map/all_gather | solution.py:27
  143.9 86.1 %conditional.1 = (f32[16,128]{1,0:T(8,128)}, f32[16,128,128]{1,2,0:T(8,128)}) conditional(s32[]{:T(128)} %convert_element_type.18, () %tuple.17, (bf16[2048,2048]{0,1:T(8,128)(2,1)}, bf16[2048,2048]{0,1:T(8,128)(2,1)}, bf16[16,128,128]{1,2,0:T(8,128)(2,1)S(1)}, pred[128,2048]{1,0:T(32,128)(4,1)S(1)}) %tuple.49), branch_computations={%region_1.0_spmd, %region_2.7_spmd} | conditional | flops 136593792 | bytes 5349073 | solution.py:53
  143.9 86.1 %while.11 = (s32[]{:T(128)}, f32[16,128]{1,0:T(8,128)}, f32[16,128,128]{1,2,0:T(8,128)}, bf16[16,128,128]{1,2,0:T(8,128)(2,1)S(1)}, bf16[16,2048,128]{1,2,0:T(8,...) while((s32[]{:T(128)}, f32[16,128]{1,0:T(8,128)}, ...), condition=%wide.region_6.6_spmd, body=%wide.region_3.5_spmd.sunk | while | flops 136593792 | bytes 5348977 | solution.py:51
  143.9 1.5 fusion.28
  147.1 1.4 fusion.30
  149.3 1.5 fusion.28
  152.5 1.4 fusion.30
  154.7 1.5 fusion.28
  157.9 1.4 fusion.30
  160.1 1.5 fusion.28
  163.3 1.5 fusion.30
  165.5 1.5 fusion.28
  168.7 1.5 fusion.30
  170.9 1.5 fusion.28
  174.1 1.5 fusion.30
  176.2 1.5 fusion.28
  179.4 1.4 fusion.30
  181.6 1.5 fusion.28
  184.8 1.4 fusion.30
  187.0 1.5 fusion.28
  188.9 1.3 dynamic_update_slice.12
  190.2 1.5 fusion.30
  192.4 1.5 fusion.28
  194.2 1.3 dynamic_update_slice.12
  195.5 1.4 fusion.30
  197.7 1.5 fusion.28
  200.9 1.4 fusion.30
  203.1 1.5 fusion.28
  205.0 1.3 dynamic_update_slice.12
  206.3 1.4 fusion.30
  208.5 1.5 fusion.28
  211.7 1.4 fusion.30
  213.9 1.5 fusion.28
  215.8 1.3 dynamic_update_slice.12
  217.1 1.4 fusion.30
  219.3 1.5 fusion.28
  221.2 1.3 dynamic_update_slice.12
  222.5 1.4 fusion.30
  224.7 1.5 fusion.28
  227.9 1.4 fusion.30
  230.0 1.3 divide_convert_fusion
  231.4 27.4 %all-gather.8.cloned.1.call-done = bf16[2048,4096]{1,0:T(8,128)(2,1)} async-done(((bf16[128,4096]{1,0:T(8,128)(2,1)}), bf16[2048,4096]{1,0:T(8,128)(2,1)}) %all-gather.8.cloned.1.call-update) | async-done | bytes 16777232 | tf_op jit(solution)/shard_map/all_gather | solution.py:58
  258.8 9.1 %convolution_convert_fusion = bf16[128,4096]{1,0:T(8,128)(2,1)} fusion(bf16[128,2048]{0,1:T(8,128)(2,1)S(1)} %bitcast.45, bf16[2048,4096]{1,0:T(8,128)(2,1)} %all-gather.8.cloned.1.call-done), kind=kOutput, calls=%fused_computation.22 | convolution fusion | flops 2148007936 | bytes 18350080 | tf_op jit(solution)/shard_map/dot_general | solution.py:59
  (101 shorter events, 33.9 us)
Async XLA Ops:
  6.5 73.0 %all-gather.4.cloned.1.call-start = ((), (), s32[]{:S(2)}) async-start(), calls=%async_computation | async-start | bytes 8912896 | tf_op jit(solution)/shard_map/all_gather | solution.py:26
  8.6 135.3 %all-gather.6.cloned.1.call-start = ((), (), s32[]{:S(2)}) async-start(), calls=%async_computation.1 | async-start | bytes 8912896 | tf_op jit(solution)/shard_map/all_gather | solution.py:27
  10.7 248.1 %all-gather.8.cloned.1.call-start = ((), (), s32[]{:S(2)}) async-start(), calls=%async_computation.2 | async-start | bytes 17825792 | tf_op jit(solution)/shard_map/all_gather | solution.py:58
Sparse Core Ops, SparseCore 0:
  9.1 70.3 all-gather.3
  81.2 62.6 all-gather.5
  146.4 112.4 all-gather.7
where the time goes:
time: 277 us; the launch traced here: 274 us
  waiting for transfers between devices  156 us (56%)
  matrix products  56 us (20%)
  local copies, waits for them, and re-layouts  38.5 us (14%)
  between operations  13.7 us (5%)
  other arithmetic  9.54 us (3%)
    all_gather x1, waiting for transfers between devices, per_device(): value_piece = lax.all_gather(values, 'ctx', axis=0, tiled=True)  64.4 us
    all_gather x1, waiting for transfers between devices, per_device(): key_piece = lax.all_gather(keys, 'ctx', axis=0, tiled=True)  63.8 us
    dynamic_update_slice x48, local copies, waits for them, and re-layouts, update(): lax.map(one_head, (query_heads, key_heads, value_heads) + tuple(current))  32.4 us
    all_gather x1, waiting for transfers between devices, per_device(): piece = lax.all_gather(out_weight, 'fsdp', axis=0, tiled=True)  27.4 us
    dot_general x16, matrix products, one_head(): jnp.dot(query_head, key_head.T, preferred_element_type=jnp.float32) * scale  23.7 us
    dot_general x16, matrix products, one_head(): jnp.dot(weights.astype(jnp.bfloat16), value_head, preferred_element_type=...  23.2 us
    dot_general x1, matrix products, per_device(): projected = jnp.dot(attended, piece, preferred_element_type=jnp.float32)  9.1 us
    reduce_sum x16, other arithmetic, one_head(): new_total = row_total * factor + jnp.sum(weights, axis=1)  6.21 us
  transfers between devices with their start and end apart: 3, of which 3 were waited for; matrix products, arithmetic and copies ran while one was open for 34% of the time, Pallas kernels for 0%

commit v1 on v0

v1 whole, which is shorter than its diff:
```python
import math

import jax
import jax.numpy as jnp
from jax import lax
from jax.experimental import pallas as pl
from jax.experimental.pallas import tpu as pltpu
from jax.sharding import PartitionSpec as P

HDIM = 128
Q_TILE = 256
K_TILE = 512
MASKED = -1e30


def attention_kernel(bounds_ref, q_ref, k_ref, v_ref, out_ref):
    blocks, rows, _ = q_ref.shape
    first, second = bounds_ref[0], bounds_ref[1]
    factor = math.log2(math.e) / math.sqrt(HDIM)

    def start_of(position):
        return jnp.where(position >= second, second, jnp.where(position >= first, first, 0))

    for tile in range(blocks * rows // Q_TILE):
        q_blocks = slice(tile * Q_TILE // rows, (tile + 1) * Q_TILE // rows)
        q_tile = q_ref[q_blocks].reshape(Q_TILE, HDIM)
        q_pos = tile * Q_TILE + lax.broadcasted_iota(jnp.int32, (1, Q_TILE), 1)
        q_start = start_of(q_pos)
        low = start_of(jnp.int32(tile * Q_TILE)) // K_TILE
        high = (tile * Q_TILE + Q_TILE - 1) // K_TILE + 1

        def step(j, carry):
            row_max, total, accum = carry
            k_blocks = pl.ds(j * (K_TILE // rows), K_TILE // rows)
            k_tile = k_ref[k_blocks].reshape(K_TILE, HDIM)
            v_tile = v_ref[k_blocks].reshape(K_TILE, HDIM)
            scores = lax.dot_general(
                k_tile, q_tile, (((1,), (1,)), ((), ())), preferred_element_type=jnp.float32
            )
            k_pos = j * K_TILE + lax.broadcasted_iota(jnp.int32, (K_TILE, 1), 0)
            allowed = (k_pos >= q_start) & (k_pos <= q_pos)
            scores = jnp.where(allowed, scores, MASKED)
            new_max = jnp.maximum(row_max, jnp.max(scores, axis=0, keepdims=True))
            weights = jnp.where(allowed, jnp.exp2((scores - new_max) * factor), 0.0)
            rescale = jnp.exp2((row_max - new_max) * factor)
            new_total = total * rescale + jnp.sum(weights, axis=0, keepdims=True)
            added = lax.dot_general(
                v_tile,
                weights.astype(jnp.bfloat16),
                (((0,), (0,)), ((), ())),
                preferred_element_type=jnp.float32,
            )
            return new_max, new_total, accum * rescale + added

        start_state = (
            jnp.full((1, Q_TILE), MASKED, jnp.float32),
            jnp.zeros((1, Q_TILE), jnp.float32),
            jnp.zeros((HDIM, Q_TILE), jnp.float32),
        )
        _, total, accum = lax.fori_loop(low, high, step, start_state)
        finished = jnp.transpose(accum / total).astype(jnp.bfloat16)
        out_ref[q_blocks] = finished.reshape(Q_TILE // rows, rows, HDIM)


def head_attention(bounds, packed):
    blocks, _, rows, _ = packed.shape

    def part(index):
        return pl.BlockSpec((blocks, None, rows, HDIM), lambda i, b: (0, index, 0, 0))

    return pl.pallas_call(
        attention_kernel,
        out_shape=jax.ShapeDtypeStruct((blocks, rows, HDIM), jnp.bfloat16),
        grid_spec=pltpu.PrefetchScalarGridSpec(
            num_scalar_prefetch=1,
            grid=(1,),
            in_specs=[part(0), part(1), part(2)],
            out_specs=pl.BlockSpec((blocks, rows, HDIM), lambda i, b: (0, 0, 0)),
        ),
        compiler_params=pltpu.CompilerParams(vmem_limit_bytes=40 << 20),
        name="head_attention",
    )(bounds, packed, packed, packed)


def per_device(queries, keys, values, out_weight, sessions):
    rows, width = queries.shape
    heads = width // HDIM
    half = out_weight.shape[1] // 2
    core = lax.axis_index("ctx") % 2
    swap = [(i, i ^ 1) for i in range(lax.axis_size("ctx"))]
    my_columns = lax.dynamic_slice_in_dim(out_weight, core * half, half, 1)
    weight = lax.all_gather(my_columns, "fsdp", axis=0, tiled=True)
    bounds = jnp.stack([jnp.sum(sessions[0] < 1), jnp.sum(sessions[0] < 2)]).astype(jnp.int32)

    packed = jnp.concatenate([queries, keys, values], axis=0)
    packed = lax.all_to_all(packed, "ctx", 1, 0, tiled=True)
    attended = head_attention(bounds, packed.reshape(heads, 3, rows, HDIM))
    attended = lax.all_to_all(attended, "ctx", 0, 0, tiled=True)
    mine = jnp.transpose(attended, (1, 0, 2)).reshape(rows, width)
    theirs = lax.ppermute(mine, "ctx", swap)
    projected = jnp.dot(
        jnp.concatenate([mine, theirs], axis=0), weight, preferred_element_type=jnp.float32
    ).astype(jnp.bfloat16)
    kept = projected[:rows]
    got = lax.ppermute(projected[rows:], "ctx", swap)
    left = jnp.where(core == 0, kept, got)
    right = jnp.where(core == 0, got, kept)
    return jnp.concatenate([left, right], axis=1)


def solution(mesh):
    return jax.shard_map(
        per_device,
        mesh=mesh,
        in_specs=(
            P(("fsdp", "ctx"), None),
            P(("fsdp", "ctx"), None),
            P(("fsdp", "ctx"), None),
            P("fsdp", None),
            P("fsdp", None),
        ),
        out_specs=P(("fsdp", "ctx"), None),
        check_vma=False,
    )
```

time: 277 us -> 113 us (0.41)
  the two profiles are of different devices: /device:TPU:1 before, /device:TPU:13 now
where the time goes in v1:
time: 113 us; the launch traced here: 111 us
  waiting for transfers between devices  40.2 us (36%)
  blocking collectives  21.4 us (19%)
  between operations  13.4 us (12%)
  Pallas kernels  12 us (11%)
  starting transfers between devices  9.6 us (8%)
  other arithmetic  6.07 us (5%)
  matrix products  5.72 us (5%)
  local copies, waits for them, and re-layouts  2.39 us (2%)
    all_to_all x1, waiting for transfers between devices, per_device(): packed = lax.all_to_all(packed, 'ctx', 1, 0, tiled=True)  36.5 us
    all_to_all x1, blocking collectives, per_device(): attended = lax.all_to_all(attended, 'ctx', 0, 0, tiled=True)  21.4 us
    pallas_call x1, Pallas kernels, head_attention(): pl.pallas_call(attention_kernel, out_shape=jax.ShapeDtypeStruct((blocks,...  12 us
    all_to_all x1, starting transfers between devices, per_device(): packed = lax.all_to_all(packed, 'ctx', 1, 0, tiled=True)  9.28 us
    dot_general x1, matrix products, per_device(): jnp.dot(jnp.concatenate([mine, theirs], axis=0), weight, preferred_elemen...  5.72 us
    all_to_all x1, other arithmetic, per_device(): packed = lax.all_to_all(packed, 'ctx', 1, 0, tiled=True)  2.99 us
  transfers between devices with their start and end apart: 4, of which 3 were waited for; matrix products, arithmetic and copies ran while one was open for 5% of the time, Pallas kernels for 11%

profile of v1, /device:TPU:13, one launch (start us, length us, event | category | flops | bytes accessed | tf_op | source)
XLA Modules:
  0.0 110.8 jit_solution(13107386097235752978)
XLA Ops:
  6.5 0.0 copy-start
  6.5 0.0 all-gather.2.cloned.1.call-start
  6.5 1.2 %copy-done = bf16[128,4096]{1,0:T(8,128)(2,1)S(1)} copy-done((bf16[128,4096]{1,0:T(8,128)(2,1)S(1)}, bf16[128,4096]{1,0:T(8,128)(2,1)}, u32[]{:S(2)}) %copy-start) | copy-done | bytes 1048600
  7.8 0.8 constant_dynamic-slice_fusion
  8.6 0.0 all-gather.2.cloned.1.call-update
  8.6 3.0 %copy_bitcast_fusion = bf16[384,16,128]{2,0,1:T(8,128)(2,1)} fusion(bf16[128,2048]{1,0:T(8,128)(2,1)} %param.7, bf16[128,2048]{1,0:T(8,128)(2,1)} %param.6, bf16[128,2048]{1,0:T(8,128)(2,1)} %param.5), kind=kLoop, calls=%fused_computation.1 | loop fusion | flops 4718592 | bytes 3145728 | tf_op jit(solution)/shard_map/all_to_all | solution.py:96
  11.6 0.0 copy-start.1
  11.6 9.3 %all-to-all-start = ((bf16[384,16,128]{2,0,1:T(8,128)(2,1)}), bf16[384,16,128]{2,0,1:T(8,128)(2,1)S(1)}, u32[]{:S(2)}, u32[]{:S(2)}) async-start(bf16[384,16,128]{2,0,1:T(8,128)(2,1)} %copy_bitcast_fusion), calls=%async_computation | async-start | bytes 3145728 | tf_op jit(solution)/shard_map/all_to_all | solution.py:96
  20.9 0.0 copy-done.1
  20.9 0.7 fusion.3
  21.6 1.3 %pad_add_fusion.bounds_ref = s32[2]{0:T(128)S(1)} fusion(s32[1]{0:T(128)} %bitcast.1, s32[1]{0:T(128)} %bitcast), kind=kLoop, calls=%fused_computation.13 | loop fusion | flops 2 | bytes 16 | tf_op jit(solution)/shard_map/stack | solution.py:93
  22.9 36.5 %all-to-all-done = bf16[384,16,128]{2,0,1:T(8,128)(2,1)S(1)} async-done(((bf16[384,16,128]{2,0,1:T(8,128)(2,1)}), bf16[384,16,128]{2,0,1:T(8,128)(2,1)S(1)}, u32[]{:S(2)}, u32[]{:S(2)}) %all-to-all-start) | async-done | bytes 1572896 | tf_op jit(solution)/shard_map/all_to_all | solution.py:96
  59.3 12.0 %head_attention.1 = bf16[16,128,128]{2,1,0:T(8,128)(2,1)S(1)} custom-call(s32[2]{0:T(128)S(1)} %pad_add_fusion.bounds_ref, bf16[16,3,128,128]{3,2,1,0:T(8,128)(2,1)S(1)} %bitcast.13, bf16[16,3,128,128]{3,2,1,0:T(8,128)(2,1)S(1)} %bitcast.14, bf16[16,3,128,128]{3,2,1,0:T(8,128)(2,1)S(1)} %bitcast.15), custom_call_target="tpu_custom_call" | custom-call | tf_op jit(solution)/shard_map/head_attention/pallas_call | solution.py:71
  71.4 21.4 %all_to_all.21 = bf16[16,128,128]{2,1,0:T(8,128)(2,1)S(1)} all-to-all(bf16[16,128,128]{2,1,0:T(8,128)(2,1)S(1)} %head_attention.1), channel_id=1, replica_groups=mesh['fsdp'=16,'ctx'=16] {'ctx'}, dimensions={0} | all-to-all | bytes 1048576 | tf_op jit(solution)/shard_map/all_to_all | solution.py:98
  92.7 0.3 copy.8
  93.0 0.1 collective-permute-start
  93.1 1.9 %collective-permute-done = bf16[128,2048]{0,1:T(8,128)(2,1)S(1)} collective-permute-done((bf16[128,2048]{0,1:T(8,128)(2,1)S(1)}, bf16[128,2048]{0,1:T(8,128)(2,1)S(1)}, u32[]{:S(2)}, u32[]{:S(2)}) %collective-permute-start) | collective-permute-done | bytes 524320 | tf_op jit(solution)/shard_map/ppermute | solution.py:100
  95.0 0.0 all-gather.2.cloned.1.call-done
  95.0 5.7 %convolution_convert_fusion = bf16[256,2048]{1,0:T(8,128)(2,1)S(1)} fusion(bf16[2048,2048]{1,0:T(8,128)(2,1)} %all-gather.2.cloned.1.call-done, bf16[128,2048]{0,1:T(8,128)(2,1)S(1)} %collective-permute-done, bf16[128,2048]{0,1:T(8,128)(2,1)S(1)} %bitcast.17), kind=kOutput, calls=%fused_computation | convolution fusion | flops 2150105088 | bytes 10485760 | tf_op jit(solution)/shard_map/dot_general | solution.py:101
  100.8 0.2 collective-permute-start.1
  101.0 1.8 %collective-permute-done.1 = bf16[128,2048]{1,0:T(8,128)(2,1)S(1)} collective-permute-done((bf16[128,2048]{1,0:T(8,128)(2,1)S(1)}, bf16[128,2048]{1,0:T(8,128)(2,1)S(1)}, u32[]{:S(2)}, u32[]{:S(2)}) %collective-permute-start.1) | collective-permute-done | bytes 524320 | tf_op jit(solution)/shard_map/ppermute | solution.py:105
  102.8 0.1 broadcast_select_fusion.1
  102.9 1.1 pad_maximum_fusion
  (1 shorter events, 0.0 us)
Async XLA Ops:
  6.5 1.2 %copy-start = (bf16[128,4096]{1,0:T(8,128)(2,1)S(1)}, bf16[128,4096]{1,0:T(8,128)(2,1)}, u32[]{:S(2)}) copy-start(bf16[128,4096]{1,0:T(8,128)(2,1)} %param.8) | copy-start | bytes 3145732
  6.5 88.5 %all-gather.2.cloned.1.call-start = ((), (), s32[]{:S(2)}) async-start(), calls=%async_computation.2 | async-start | bytes 8912896 | tf_op jit(solution)/shard_map/all_gather | solution.py:92
  11.6 9.3 %copy-start.1 = (s32[1,2048]{1,0:T(1,128)S(1)}, s32[1,2048]{1,0:T(1,128)}, u32[]{:S(2)}) copy-start(s32[1,2048]{1,0:T(1,128)} %param.9) | copy-start | bytes 24580
  11.6 47.7 %all-to-all-start = ((bf16[384,16,128]{2,0,1:T(8,128)(2,1)}), bf16[384,16,128]{2,0,1:T(8,128)(2,1)S(1)}, u32[]{:S(2)}, u32[]{:S(2)}) async-start(bf16[384,16,128]{2,0,1:T(8,128)(2,1)} %copy_bitcast_fusion), calls=%async_computation | async-start | bytes 3145728 | tf_op jit(solution)/shard_map/all_to_all | solution.py:96
  93.0 2.0 %collective-permute-start = (bf16[128,2048]{0,1:T(8,128)(2,1)S(1)}, bf16[128,2048]{0,1:T(8,128)(2,1)S(1)}, u32[]{:S(2)}, u32[]{:S(2)}) collective-permute-start(bf16[128,2048]{0,1:T(8,128)(2,1)S(1)} %bitcast.16), channel_id=1, source_target_pairs={{0,1},{1,0},{2,3},{3,2},{4,5},{5,4},{6,7},{7,6},{8,9},{9,8},{10,11... | collective-permute-start | bytes 1572872 | tf_op jit(solution)/shard_map/ppermute | solution.py:100
  100.8 2.0 %collective-permute-start.1 = (bf16[128,2048]{1,0:T(8,128)(2,1)S(1)}, bf16[128,2048]{1,0:T(8,128)(2,1)S(1)}, u32[]{:S(2)}, u32[]{:S(2)}) collective-permute-start(bf16[128,2048]{1,0:T(8,128)(2,1)S(1)} %slice.9), channel_id=1, source_target_pairs={{0,1},{1,0},{2,3},{3,2},{4,5},{5,4},{6,7},{7,6},{8,9},{9,8},{10,11... | collective-permute-start | bytes 1572872 | tf_op jit(solution)/shard_map/ppermute | solution.py:105
Sparse Core Ops, SparseCore 0:
  9.8 77.3 all-gather.1

commit v2 on v1

--- a/solution.py
+++ b/solution.py
@@ -1,3 +1,4 @@
+import functools
 import math
 
 import jax
@@ -11,6 +12,8 @@
 Q_TILE = 256
 K_TILE = 512
 MASKED = -1e30
+SIDE = 4
+NEAR = (0, 1, 3, 2)
 
 
 def attention_kernel(bounds_ref, q_ref, k_ref, v_ref, out_ref):
@@ -62,6 +65,21 @@
         out_ref[q_blocks] = finished.reshape(Q_TILE // rows, rows, HDIM)
 
 
+def pack_kernel(queries_ref, keys_ref, values_ref, out_ref):
+    for index, ref in enumerate((queries_ref, keys_ref, values_ref)):
+        for head in range(out_ref.shape[0]):
+            out_ref[head, index] = ref[:, head * HDIM:(head + 1) * HDIM]
+
+
+def pack(queries, keys, values):
+    rows, width = queries.shape
+    return pl.pallas_call(
+        pack_kernel,
+        out_shape=jax.ShapeDtypeStruct((width // HDIM, 3, rows, HDIM), queries.dtype),
+        name="pack",
+    )(queries, keys, values)
+
+
 def head_attention(bounds, packed):
     blocks, _, rows, _ = packed.shape
 
@@ -77,32 +95,98 @@
             in_specs=[part(0), part(1), part(2)],
             out_specs=pl.BlockSpec((blocks, rows, HDIM), lambda i, b: (0, 0, 0)),
         ),
-        compiler_params=pltpu.CompilerParams(vmem_limit_bytes=40 << 20),
+        compiler_params=pltpu.CompilerParams(vmem_limit_bytes=12 << 20),
         name="head_attention",
     )(bounds, packed, packed, packed)
 
 
+def projection_kernel(offsets, place_ref, mine_ref, theirs_ref, *rest):
+    pieces, (kept_ref, sent_ref, left_ref) = list(rest[:-3]), rest[-3:]
+    rows = mine_ref.shape[1]
+    columns = pieces[0].shape[2]
+    y, x = place_ref[0], place_ref[1]
+    for side, lists in enumerate(offsets):
+        accum = None
+        start = 0
+        for places in lists:
+            for dy, dx in places:
+                head = ((y + dy + SIDE) % SIDE) * SIDE + (x + dx + SIDE) % SIDE
+                left_ref[:rows, start:start + HDIM] = mine_ref[head]
+                left_ref[rows:, start:start + HDIM] = theirs_ref[head]
+                start += HDIM
+        start = 0
+        for places in lists:
+            depth = len(places) * HDIM
+            piece = pieces.pop(0)[...].reshape(depth, columns)
+            added = jnp.dot(left_ref[:, start:start + depth], piece, preferred_element_type=jnp.float32)
+            accum = added if accum is None else accum + added
+            start += depth
+        result = accum.astype(jnp.bfloat16)
+        kept_ref[:, side * columns:(side + 1) * columns] = result[:rows]
+        sent_ref[:, side * columns:(side + 1) * columns] = result[rows:]
+
+
+def project(place, mine, theirs, pieces, offsets):
+    heads, rows, _ = mine.shape
+    columns = 2 * pieces[0].shape[2]
+    vmem = pl.BlockSpec(memory_space=pltpu.VMEM)
+    out = jax.ShapeDtypeStruct((rows, columns), jnp.bfloat16)
+    return pl.pallas_call(
+        functools.partial(projection_kernel, offsets),
+        out_shape=(out, out),
+        in_specs=[pl.BlockSpec(memory_space=pltpu.SMEM)] + [vmem] * (2 + len(pieces)),
+        out_specs=(vmem, vmem),
+        scratch_shapes=[pltpu.VMEM((2 * rows, heads * HDIM), jnp.bfloat16)],
+        compiler_params=pltpu.CompilerParams(vmem_limit_bytes=10 << 20),
+        name="project",
+    )(place, mine, theirs, *pieces)
+
+
+def fetch(piece, dy, dx):
+    pairs = [
+        (SIDE * ((y + dy + SIDE) % SIDE) + (x + dx) % SIDE, SIDE * y + x)
+        for y in range(SIDE)
+        for x in range(SIDE)
+    ]
+    return lax.ppermute(piece, "fsdp", pairs)
+
+
 def per_device(queries, keys, values, out_weight, sessions):
-    rows, width = queries.shape
-    heads = width // HDIM
-    half = out_weight.shape[1] // 2
     core = lax.axis_index("ctx") % 2
     swap = [(i, i ^ 1) for i in range(lax.axis_size("ctx"))]
-    my_columns = lax.dynamic_slice_in_dim(out_weight, core * half, half, 1)
-    weight = lax.all_gather(my_columns, "fsdp", axis=0, tiled=True)
     bounds = jnp.stack([jnp.sum(sessions[0] < 1), jnp.sum(sessions[0] < 2)]).astype(jnp.int32)
-
-    packed = jnp.concatenate([queries, keys, values], axis=0)
-    packed = lax.all_to_all(packed, "ctx", 1, 0, tiled=True)
-    attended = head_attention(bounds, packed.reshape(heads, 3, rows, HDIM))
-    attended = lax.all_to_all(attended, "ctx", 0, 0, tiled=True)
-    mine = jnp.transpose(attended, (1, 0, 2)).reshape(rows, width)
+    place = lax.axis_index("fsdp")
+    place = jnp.stack([place // SIDE, place % SIDE]).astype(jnp.int32)
+
+    packed = lax.all_to_all(pack(queries, keys, values), "ctx", 0, 0, tiled=True)
+
+    half = out_weight.shape[1] // 2
+    first = lax.dynamic_slice_in_dim(out_weight, core * half, half // 2, 1)
+    second = lax.dynamic_slice_in_dim(out_weight, core * half + half // 2, half // 2, 1)
+    first = jnp.stack([first] + [fetch(first, 0, step) for step in NEAR[1:]])
+    second = jnp.stack([second] + [fetch(second, step, 0) for step in NEAR[1:]])
+    packed, _, _ = lax.optimization_barrier((packed, first, second))
+    beside = [fetch(first, 1, 0), fetch(first, -1, 0), fetch(second, 0, 1), fetch(second, 0, -1)]
+
+    attended = head_attention(bounds, packed)
+    attended, *_ = lax.optimization_barrier((attended, *beside))
+    far = [
+        fetch(beside[0][:2], 1, 0),
+        fetch(beside[1][2:], -1, 0),
+        fetch(beside[2][:2], 0, 1),
+        fetch(beside[3][2:], 0, -1),
+    ]
+    pieces = [first, beside[0], beside[1], far[0], far[1], second, beside[2], beside[3], far[2], far[3]]
+    steps = [(0, NEAR), (1, NEAR), (-1, NEAR), (2, NEAR[:2]), (2, NEAR[2:])]
+    offsets = (
+        [[(dy, dx) for dx in near] for dy, near in steps],
+        [[(dy, dx) for dy in near] for dx, near in steps],
+    )
+
+    mine = lax.all_to_all(attended, "ctx", 0, 0, tiled=True)
     theirs = lax.ppermute(mine, "ctx", swap)
-    projected = jnp.dot(
-        jnp.concatenate([mine, theirs], axis=0), weight, preferred_element_type=jnp.float32
-    ).astype(jnp.bfloat16)
-    kept = projected[:rows]
-    got = lax.ppermute(projected[rows:], "ctx", swap)
+    kept, sent = project(place, mine, theirs, pieces, offsets)
+    got = lax.ppermute(sent, "ctx", swap)
     left = jnp.where(core == 0, kept, got)
     right = jnp.where(core == 0, got, kept)
     return jnp.concatenate([left, right], axis=1)

time: 113 us -> 109 us (0.965)
  the two profiles are of different devices: /device:TPU:13 before, /device:TPU:1 now
where the time goes in v2:
time: 109 us; the launch traced here: 107 us
  starting transfers between devices  35.7 us (33%)
  waiting for transfers between devices  35.6 us (33%)
  Pallas kernels  21.9 us (20%)
  local copies, waits for them, and re-layouts  8.34 us (8%)
  other arithmetic  5.55 us (5%)
    ppermute x14, starting transfers between devices, fetch(): return lax.ppermute(piece, 'fsdp', pairs)  19.7 us
    ppermute x14, waiting for transfers between devices, fetch(): return lax.ppermute(piece, 'fsdp', pairs)  15.7 us
    all_to_all x1, waiting for transfers between devices, per_device(): lax.all_to_all(pack(queries, keys, values), 'ctx', 0, 0, tiled=True)  13.7 us
    pallas_call x1, Pallas kernels, head_attention(): pl.pallas_call(attention_kernel, out_shape=jax.ShapeDtypeStruct((blocks,...  13 us
    all_to_all x1, starting transfers between devices, per_device(): lax.all_to_all(pack(queries, keys, values), 'ctx', 0, 0, tiled=True)  10.1 us
    pallas_call x1, Pallas kernels, project(): pl.pallas_call(functools.partial(projection_kernel, offsets), out_shape=(...  6.13 us
    all_to_all x1, starting transfers between devices, per_device(): mine = lax.all_to_all(attended, 'ctx', 0, 0, tiled=True)  4.67 us
    all_to_all x1, waiting for transfers between devices, per_device(): mine = lax.all_to_all(attended, 'ctx', 0, 0, tiled=True)  4.4 us
  transfers between devices with their start and end apart: 18, of which 9 were waited for; matrix products, arithmetic and copies ran while one was open for 10% of the time, Pallas kernels for 12%

profile of v2, /device:TPU:1, one launch (start us, length us, event | category | flops | bytes accessed | tf_op | source)
XLA Modules:
  0.0 107.2 jit_solution(12977505712963299514)
XLA Ops:
  0.0 2.8 %pack.1 = bf16[16,3,128,128]{3,2,1,0:T(8,128)(2,1)} custom-call(bf16[128,2048]{1,0:T(8,128)(2,1)} %queries_ref.1, bf16[128,2048]{1,0:T(8,128)(2,1)} %keys_ref.1, bf16[128,2048]{1,0:T(8,128)(2,1)} %values_ref.1), custom_call_target="tpu_custom_call" | custom-call | tf_op jit(solution)/shard_map/pack/pallas_call | solution.py:76
  2.8 10.1 %all-to-all-start = ((bf16[16,3,128,128]{3,2,1,0:T(8,128)(2,1)}), bf16[16,3,128,128]{3,2,1,0:T(8,128)(2,1)S(1)}, u32[]{:S(2)}, u32[]{:S(2)}) async-start(bf16[16,3,128,128]{3,2,1,0:T(8,128)(2,1)} %pack.1), calls=%async_computation | async-start | bytes 3145728 | tf_op jit(solution)/shard_map/all_to_all | solution.py:161
  13.0 1.4 %collective-permute-start.4 = (bf16[128,1024]{1,0:T(8,128)(2,1)S(1)}, bf16[128,1024]{1,0:T(8,128)(2,1)S(1)}, u32[]{:S(2)}, u32[]{:S(2)}) collective-permute-start(bf16[128,1024]{1,0:T(8,128)(2,1)S(1)} %get-tuple-element.17), channel_id=1, source_target_pairs={{192,0},{208,16},{224,32},{240,48},{0,64},{16,80},{32,96},{48,112}... | collective-permute-start | bytes 786440 | tf_op jit(solution)/shard_map/ppermute | solution.py:151
  14.3 2.6 %collective-permute-start.5 = (bf16[128,1024]{1,0:T(8,128)(2,1)S(1)}, bf16[128,1024]{1,0:T(8,128)(2,1)S(1)}, u32[]{:S(2)}, u32[]{:S(2)}) collective-permute-start(bf16[128,1024]{1,0:T(8,128)(2,1)S(1)} %get-tuple-element.17), channel_id=1, source_target_pairs={{128,0},{144,16},{160,32},{176,48},{192,64},{208,80},{224,96},{240... | collective-permute-start | bytes 786440 | tf_op jit(solution)/shard_map/ppermute | solution.py:151
  17.0 1.1 collective-permute-start.3
  18.0 2.5 %collective-permute-start = (bf16[128,1024]{1,0:T(8,128)(2,1)S(1)}, bf16[128,1024]{1,0:T(8,128)(2,1)S(1)}, u32[]{:S(2)}, u32[]{:S(2)}) collective-permute-start(bf16[128,1024]{1,0:T(8,128)(2,1)S(1)} %get-tuple-element.18), channel_id=1, source_target_pairs={{16,0},{32,16},{48,32},{0,48},{80,64},{96,80},{112,96},{64,112},{1... | collective-permute-start | bytes 786440 | tf_op jit(solution)/shard_map/ppermute | solution.py:151
  20.5 1.6 %collective-permute-done.4 = bf16[128,1024]{1,0:T(8,128)(2,1)S(1)} collective-permute-done((bf16[128,1024]{1,0:T(8,128)(2,1)S(1)}, bf16[128,1024]{1,0:T(8,128)(2,1)S(1)}, u32[]{:S(2)}, u32[]{:S(2)}) %collective-permute-start.4) | collective-permute-done | bytes 262176 | tf_op jit(solution)/shard_map/ppermute | solution.py:151
  22.2 2.7 %collective-permute-start.2 = (bf16[128,1024]{1,0:T(8,128)(2,1)S(1)}, bf16[128,1024]{1,0:T(8,128)(2,1)S(1)}, u32[]{:S(2)}, u32[]{:S(2)}) collective-permute-start(bf16[128,1024]{1,0:T(8,128)(2,1)S(1)} %get-tuple-element.18), channel_id=1, source_target_pairs={{32,0},{48,16},{0,32},{16,48},{96,64},{112,80},{64,96},{80,112},{1... | collective-permute-start | bytes 786440 | tf_op jit(solution)/shard_map/ppermute | solution.py:151
  24.9 4.0 %collective-permute-done.5 = bf16[128,1024]{1,0:T(8,128)(2,1)S(1)} collective-permute-done((bf16[128,1024]{1,0:T(8,128)(2,1)S(1)}, bf16[128,1024]{1,0:T(8,128)(2,1)S(1)}, u32[]{:S(2)}, u32[]{:S(2)}) %collective-permute-start.5) | collective-permute-done | bytes 262176 | tf_op jit(solution)/shard_map/ppermute | solution.py:151
  28.9 0.0 collective-permute-done.3
  28.9 0.1 pad_maximum_fusion.1.rest_5_
  29.0 0.0 copy-start.2
  29.0 2.6 %collective-permute-start.8 = (bf16[4,128,1024]{2,1,0:T(8,128)(2,1)S(1)}, bf16[4,128,1024]{2,1,0:T(8,128)(2,1)}, u32[]{:S(2)}, u32[]{:S(2)}) collective-permute-start(bf16[4,128,1024]{2,1,0:T(8,128)(2,1)S(1)} %pad_maximum_fusion.1.rest_5_), channel_id=1, source_target_pairs={{16,0},{32,16},{48,32},{0,48},{80,64},{96,80},{112,96},{64,112},{1... | collective-permute-start | bytes 3145736 | tf_op jit(solution)/shard_map/ppermute | solution.py:151
  31.6 0.0 collective-permute-start.9
  31.6 0.0 collective-permute-done
  31.6 0.0 collective-permute-done.1
  31.6 1.4 %collective-permute-done.2 = bf16[128,1024]{1,0:T(8,128)(2,1)S(1)} collective-permute-done((bf16[128,1024]{1,0:T(8,128)(2,1)S(1)}, bf16[128,1024]{1,0:T(8,128)(2,1)S(1)}, u32[]{:S(2)}, u32[]{:S(2)}) %collective-permute-start.2) | collective-permute-done | bytes 262176 | tf_op jit(solution)/shard_map/ppermute | solution.py:151
  33.0 1.1 %pad_maximum_fusion.rest_0_ = bf16[4,128,1024]{2,1,0:T(8,128)(2,1)} fusion(bf16[1,128,1024]{2,1,0:T(8,128)(2,1)S(1)} %bitcast.17, bf16[1,128,1024]{2,1,0:T(8,128)(2,1)S(1)} %bitcast.15, bf16[1,128,1024]{2,1,0:T(8,128)(2,1)S(1)} %bitcast.14, bf16[1,128,1024]{2,1,0:T(8,128)(2,1)S(1)} %bitcast.12), kind=kLoop, calls=%fused_computation | loop fusion | flops 1572864 | bytes 2097152 | tf_op jit(solution)/shard_map/stack | solution.py:166
  34.1 1.0 collective-permute-start.6
  35.1 0.5 collective-permute-start.7
  35.5 0.7 fusion
  36.3 1.3 %pad_add_fusion.1.bounds_ref = s32[2]{0:T(128)S(1)} fusion(s32[1]{0:T(128)} %bitcast.3, s32[1]{0:T(128)} %bitcast.2), kind=kLoop, calls=%fused_computation.10 | loop fusion | flops 2 | bytes 16 | tf_op jit(solution)/shard_map/stack | solution.py:157
  37.6 13.7 %all-to-all-done.q_ref.k_ref.v_ref = bf16[16,3,128,128]{3,2,1,0:T(8,128)(2,1)S(1)} async-done(((bf16[16,3,128,128]{3,2,1,0:T(8,128)(2,1)}), bf16[16,3,128,128]{3,2,1,0:T(8,128)(2,1)S(1)}, u32[]{:S(2)}, u32[]{:S(2)}) %all-to-all-start) | async-done | bytes 1572896 | tf_op jit(solution)/shard_map/all_to_all | solution.py:161
  51.3 13.0 %head_attention.1 = bf16[16,128,128]{2,1,0:T(8,128)(2,1)} custom-call(s32[2]{0:T(128)S(1)} %pad_add_fusion.1.bounds_ref, bf16[16,3,128,128]{3,2,1,0:T(8,128)(2,1)S(1)} %all-to-all-done.q_ref.k_ref.v_ref, bf16[16,3,128,128]{3,2,1,0:T(8,128)(2,1)S(1)} %all-to-all-done.q_ref.k_ref.v_ref, bf16[16,3,128,128]{3,2,1,0:T(8,128)(2,1)S(1)} %all-to-all-done.q_ref.k_ref.v_ref), custom_call_target="tpu_custom_call" | custom-call | tf_op jit(solution)/shard_map/head_attention/pallas_call | solution.py:89
  64.3 0.0 collective-permute-done.8.rest_6_
  64.3 0.0 collective-permute-done.9.rest_7_
  64.3 0.0 collective-permute-done.6.rest_1_
  64.3 0.0 collective-permute-done.7.rest_2_
  64.4 4.7 %all-to-all-start.1 = ((bf16[16,128,128]{2,1,0:T(8,128)(2,1)}), bf16[16,128,128]{2,1,0:T(8,128)(2,1)S(1)}, u32[]{:S(2)}, u32[]{:S(2)}) async-start(bf16[16,128,128]{2,1,0:T(8,128)(2,1)} %head_attention.1), calls=%async_computation.1 | async-start | bytes 1048576 | tf_op jit(solution)/shard_map/all_to_all | solution.py:186
  69.0 1.9 %slice.18 = bf16[2,128,1024]{2,1,0:T(8,128)(2,1)} slice(bf16[4,128,1024]{2,1,0:T(8,128)(2,1)} %collective-permute-done.8.rest_6_), slice={[0:2], [0:128], [0:1024]} | slice | bytes 1048576 | tf_op jit(solution)/shard_map/slice | solution.py:176
  70.9 3.9 %collective-permute-start.13 = (bf16[2,128,1024]{2,1,0:T(8,128)(2,1)}, bf16[2,128,1024]{2,1,0:T(8,128)(2,1)S(1)}, u32[]{:S(2)}, u32[]{:S(2)}) collective-permute-start(bf16[2,128,1024]{2,1,0:T(8,128)(2,1)} %slice.18), channel_id=1, source_target_pairs={{16,0},{32,16},{48,32},{0,48},{80,64},{96,80},{112,96},{64,112},{1... | collective-permute-start | bytes 1572872 | tf_op jit(solution)/shard_map/ppermute | solution.py:151
  74.8 1.9 %slice.19 = bf16[2,128,1024]{2,1,0:T(8,128)(2,1)} slice(bf16[4,128,1024]{2,1,0:T(8,128)(2,1)} %collective-permute-done.9.rest_7_), slice={[2:4], [0:128], [0:1024]} | slice | bytes 1048576 | tf_op jit(solution)/shard_map/slice | solution.py:177
  76.7 1.9 %slice.16 = bf16[2,128,1024]{2,1,0:T(8,128)(2,1)} slice(bf16[4,128,1024]{2,1,0:T(8,128)(2,1)} %collective-permute-done.6.rest_1_), slice={[0:2], [0:128], [0:1024]} | slice | bytes 1048576 | tf_op jit(solution)/shard_map/slice | solution.py:174
  78.6 1.9 %slice.17 = bf16[2,128,1024]{2,1,0:T(8,128)(2,1)} slice(bf16[4,128,1024]{2,1,0:T(8,128)(2,1)} %collective-permute-done.7.rest_2_), slice={[2:4], [0:128], [0:1024]} | slice | bytes 1048576 | tf_op jit(solution)/shard_map/slice | solution.py:175
  80.5 1.5 %collective-permute-start.12 = (bf16[2,128,1024]{2,1,0:T(8,128)(2,1)}, bf16[2,128,1024]{2,1,0:T(8,128)(2,1)}, u32[]{:S(2)}, u32[]{:S(2)}) collective-permute-start(bf16[2,128,1024]{2,1,0:T(8,128)(2,1)} %slice.17), channel_id=1, source_target_pairs={{192,0},{208,16},{224,32},{240,48},{0,64},{16,80},{32,96},{48,112}... | collective-permute-start | bytes 1572872 | tf_op jit(solution)/shard_map/ppermute | solution.py:151
  81.9 4.4 %all-to-all-done.1.mine_ref = bf16[16,128,128]{2,1,0:T(8,128)(2,1)S(1)} async-done(((bf16[16,128,128]{2,1,0:T(8,128)(2,1)}), bf16[16,128,128]{2,1,0:T(8,128)(2,1)S(1)}, u32[]{:S(2)}, u32[]{:S(2)}) %all-to-all-start.1) | async-done | bytes 524320 | tf_op jit(solution)/shard_map/all_to_all | solution.py:186
  86.3 0.0 collective-permute-start.10
  86.4 0.1 pad_add_fusion.place_ref
  86.4 0.0 collective-permute-done.13.rest_8_
  86.4 5.0 %collective-permute-done.14.rest_9_ = bf16[2,128,1024]{2,1,0:T(8,128)(2,1)S(1)} collective-permute-done((bf16[2,128,1024]{2,1,0:T(8,128)(2,1)}, bf16[2,128,1024]{2,1,0:T(8,128)(2,1)S(1)}, u32[]{:S(2)}, u32[]{:S(2)}) %collective-permute-start.14) | collective-permute-done | bytes 524320 | tf_op jit(solution)/shard_map/ppermute | solution.py:151
  91.4 0.7 collective-permute-done.11.rest_3_
  92.1 3.1 %collective-permute-done.12.rest_4_ = bf16[2,128,1024]{2,1,0:T(8,128)(2,1)} collective-permute-done((bf16[2,128,1024]{2,1,0:T(8,128)(2,1)}, bf16[2,128,1024]{2,1,0:T(8,128)(2,1)}, u32[]{:S(2)}, u32[]{:S(2)}) %collective-permute-start.12) | collective-permute-done | bytes 524320 | tf_op jit(solution)/shard_map/ppermute | solution.py:151
  95.2 6.1 %project.1 = (bf16[128,2048]{1,0:T(8,128)(2,1)S(1)}, bf16[128,2048]{1,0:T(8,128)(2,1)}) custom-call(s32[2]{0:T(128)S(1)} %pad_add_fusion.place_ref, bf16[16,128,128]{2,1,0:T(8,128)(2,1)S(1)} %all-to-all-done.1.mine_ref, bf16[16,128,128]{2,1,0:T(8,128)(2,1)} %collective-permute-done.10.theirs_ref, bf16[4,128,1024]{2,1,0:T(8,128)(2,1)} %pad_maximum_fusion.rest_0_, ...), custom_call_target="tpu_custom_call" | custom-call | tf_op jit(solution)/shard_map/project/pallas_call | solution.py:134
  101.3 0.8 copy-done
  102.1 1.2 %collective-permute-start.15 = (bf16[128,2048]{1,0:T(8,128)(2,1)}, bf16[128,2048]{1,0:T(8,128)(2,1)S(1)}, u32[]{:S(2)}, u32[]{:S(2)}) collective-permute-start(bf16[128,2048]{1,0:T(8,128)(2,1)} %get-tuple-element.12), channel_id=1, source_target_pairs={{0,1},{1,0},{2,3},{3,2},{4,5},{5,4},{6,7},{7,6},{8,9},{9,8},{10,11... | collective-permute-start | bytes 1572872 | tf_op jit(solution)/shard_map/ppermute | solution.py:189
  103.3 1.7 %collective-permute-done.15 = bf16[128,2048]{1,0:T(8,128)(2,1)S(1)} collective-permute-done((bf16[128,2048]{1,0:T(8,128)(2,1)}, bf16[128,2048]{1,0:T(8,128)(2,1)S(1)}, u32[]{:S(2)}, u32[]{:S(2)}) %collective-permute-start.15) | collective-permute-done | bytes 524320 | tf_op jit(solution)/shard_map/ppermute | solution.py:189
  105.0 1.1 %broadcast_select_fusion.1 = (bf16[128,2048]{1,0:T(8,128)(2,1)S(1)}, bf16[128,2048]{1,0:T(8,128)(2,1)S(1)}) fusion(bf16[128,2048]{1,0:T(8,128)(2,1)} %copy-done, bf16[128,2048]{1,0:T(8,128)(2,1)S(1)} %collective-permute-done.15, pred[]{:T(512)S(6)} %eq.7), kind=kLoop, calls=%fused_computation.4 | loop fusion | flops 524288 | bytes 2097153 | tf_op jit(solution)/shard_map/jit(_where)/select_n | solution.py:190
  106.1 1.1 pad_maximum_fusion.2
  (9 shorter events, 0.1 us)
Async XLA Ops:
  2.8 10.1 %copy-start.1 = (bf16[128,4096]{1,0:T(8,128)(2,1)S(1)}, bf16[128,4096]{1,0:T(8,128)(2,1)}, u32[]{:S(2)}) copy-start(bf16[128,4096]{1,0:T(8,128)(2,1)} %param.8) | copy-start | bytes 3145732
  2.8 48.5 %all-to-all-start = ((bf16[16,3,128,128]{3,2,1,0:T(8,128)(2,1)}), bf16[16,3,128,128]{3,2,1,0:T(8,128)(2,1)S(1)}, u32[]{:S(2)}, u32[]{:S(2)}) async-start(bf16[16,3,128,128]{3,2,1,0:T(8,128)(2,1)} %pack.1), calls=%async_computation | async-start | bytes 3145728 | tf_op jit(solution)/shard_map/all_to_all | solution.py:161
  13.0 9.2 %collective-permute-start.4 = (bf16[128,1024]{1,0:T(8,128)(2,1)S(1)}, bf16[128,1024]{1,0:T(8,128)(2,1)S(1)}, u32[]{:S(2)}, u32[]{:S(2)}) collective-permute-start(bf16[128,1024]{1,0:T(8,128)(2,1)S(1)} %get-tuple-element.17), channel_id=1, source_target_pairs={{192,0},{208,16},{224,32},{240,48},{0,64},{16,80},{32,96},{48,112}... | collective-permute-start | bytes 786440 | tf_op jit(solution)/shard_map/ppermute | solution.py:151
  14.3 14.5 %collective-permute-start.5 = (bf16[128,1024]{1,0:T(8,128)(2,1)S(1)}, bf16[128,1024]{1,0:T(8,128)(2,1)S(1)}, u32[]{:S(2)}, u32[]{:S(2)}) collective-permute-start(bf16[128,1024]{1,0:T(8,128)(2,1)S(1)} %get-tuple-element.17), channel_id=1, source_target_pairs={{128,0},{144,16},{160,32},{176,48},{192,64},{208,80},{224,96},{240... | collective-permute-start | bytes 786440 | tf_op jit(solution)/shard_map/ppermute | solution.py:151
  17.0 11.9 %collective-permute-start.3 = (bf16[128,1024]{1,0:T(8,128)(2,1)S(1)}, bf16[128,1024]{1,0:T(8,128)(2,1)S(1)}, u32[]{:S(2)}, u32[]{:S(2)}) collective-permute-start(bf16[128,1024]{1,0:T(8,128)(2,1)S(1)} %get-tuple-element.17), channel_id=1, source_target_pairs={{64,0},{80,16},{96,32},{112,48},{128,64},{144,80},{160,96},{176,11... | collective-permute-start | bytes 786440 | tf_op jit(solution)/shard_map/ppermute | solution.py:151
  18.0 13.6 %collective-permute-start = (bf16[128,1024]{1,0:T(8,128)(2,1)S(1)}, bf16[128,1024]{1,0:T(8,128)(2,1)S(1)}, u32[]{:S(2)}, u32[]{:S(2)}) collective-permute-start(bf16[128,1024]{1,0:T(8,128)(2,1)S(1)} %get-tuple-element.18), channel_id=1, source_target_pairs={{16,0},{32,16},{48,32},{0,48},{80,64},{96,80},{112,96},{64,112},{1... | collective-permute-start | bytes 786440 | tf_op jit(solution)/shard_map/ppermute | solution.py:151
  20.5 11.1 %collective-permute-start.1 = (bf16[128,1024]{1,0:T(8,128)(2,1)S(1)}, bf16[128,1024]{1,0:T(8,128)(2,1)S(1)}, u32[]{:S(2)}, u32[]{:S(2)}) collective-permute-start(bf16[128,1024]{1,0:T(8,128)(2,1)S(1)} %get-tuple-element.18), channel_id=1, source_target_pairs={{48,0},{0,16},{16,32},{32,48},{112,64},{64,80},{80,96},{96,112},{1... | collective-permute-start | bytes 786440 | tf_op jit(solution)/shard_map/ppermute | solution.py:151
  22.2 10.8 %collective-permute-start.2 = (bf16[128,1024]{1,0:T(8,128)(2,1)S(1)}, bf16[128,1024]{1,0:T(8,128)(2,1)S(1)}, u32[]{:S(2)}, u32[]{:S(2)}) collective-permute-start(bf16[128,1024]{1,0:T(8,128)(2,1)S(1)} %get-tuple-element.18), channel_id=1, source_target_pairs={{32,0},{48,16},{0,32},{16,48},{96,64},{112,80},{64,96},{80,112},{1... | collective-permute-start | bytes 786440 | tf_op jit(solution)/shard_map/ppermute | solution.py:151
  29.0 6.5 %copy-start.2 = (s32[1,2048]{1,0:T(1,128)S(1)}, s32[1,2048]{1,0:T(1,128)}, u32[]{:S(2)}) copy-start(s32[1,2048]{1,0:T(1,128)} %param.9) | copy-start | bytes 24580
  29.0 35.3 %collective-permute-start.8 = (bf16[4,128,1024]{2,1,0:T(8,128)(2,1)S(1)}, bf16[4,128,1024]{2,1,0:T(8,128)(2,1)}, u32[]{:S(2)}, u32[]{:S(2)}) collective-permute-start(bf16[4,128,1024]{2,1,0:T(8,128)(2,1)S(1)} %pad_maximum_fusion.1.rest_5_), channel_id=1, source_target_pairs={{16,0},{32,16},{48,32},{0,48},{80,64},{96,80},{112,96},{64,112},{1... | collective-permute-start | bytes 3145736 | tf_op jit(solution)/shard_map/ppermute | solution.py:151
  31.6 32.7 %collective-permute-start.9 = (bf16[4,128,1024]{2,1,0:T(8,128)(2,1)S(1)}, bf16[4,128,1024]{2,1,0:T(8,128)(2,1)}, u32[]{:S(2)}, u32[]{:S(2)}) collective-permute-start(bf16[4,128,1024]{2,1,0:T(8,128)(2,1)S(1)} %pad_maximum_fusion.1.rest_5_), channel_id=1, source_target_pairs={{48,0},{0,16},{16,32},{32,48},{112,64},{64,80},{80,96},{96,112},{1... | collective-permute-start | bytes 3145736 | tf_op jit(solution)/shard_map/ppermute | solution.py:151
  34.1 30.3 %collective-permute-start.6 = (bf16[4,128,1024]{2,1,0:T(8,128)(2,1)}, bf16[4,128,1024]{2,1,0:T(8,128)(2,1)}, u32[]{:S(2)}, u32[]{:S(2)}) collective-permute-start(bf16[4,128,1024]{2,1,0:T(8,128)(2,1)} %pad_maximum_fusion.rest_0_), channel_id=1, source_target_pairs={{64,0},{80,16},{96,32},{112,48},{128,64},{144,80},{160,96},{176,11... | collective-permute-start | bytes 3145736 | tf_op jit(solution)/shard_map/ppermute | solution.py:151
  35.1 29.3 %collective-permute-start.7 = (bf16[4,128,1024]{2,1,0:T(8,128)(2,1)}, bf16[4,128,1024]{2,1,0:T(8,128)(2,1)}, u32[]{:S(2)}, u32[]{:S(2)}) collective-permute-start(bf16[4,128,1024]{2,1,0:T(8,128)(2,1)} %pad_maximum_fusion.rest_0_), channel_id=1, source_target_pairs={{192,0},{208,16},{224,32},{240,48},{0,64},{16,80},{32,96},{48,112}... | collective-permute-start | bytes 3145736 | tf_op jit(solution)/shard_map/ppermute | solution.py:151
  64.4 22.0 %all-to-all-start.1 = ((bf16[16,128,128]{2,1,0:T(8,128)(2,1)}), bf16[16,128,128]{2,1,0:T(8,128)(2,1)S(1)}, u32[]{:S(2)}, u32[]{:S(2)}) async-start(bf16[16,128,128]{2,1,0:T(8,128)(2,1)} %head_attention.1), calls=%async_computation.1 | async-start | bytes 1048576 | tf_op jit(solution)/shard_map/all_to_all | solution.py:186
  70.9 15.5 %collective-permute-start.13 = (bf16[2,128,1024]{2,1,0:T(8,128)(2,1)}, bf16[2,128,1024]{2,1,0:T(8,128)(2,1)S(1)}, u32[]{:S(2)}, u32[]{:S(2)}) collective-permute-start(bf16[2,128,1024]{2,1,0:T(8,128)(2,1)} %slice.18), channel_id=1, source_target_pairs={{16,0},{32,16},{48,32},{0,48},{80,64},{96,80},{112,96},{64,112},{1... | collective-permute-start | bytes 1572872 | tf_op jit(solution)/shard_map/ppermute | solution.py:151
  76.7 14.7 %collective-permute-start.14 = (bf16[2,128,1024]{2,1,0:T(8,128)(2,1)}, bf16[2,128,1024]{2,1,0:T(8,128)(2,1)S(1)}, u32[]{:S(2)}, u32[]{:S(2)}) collective-permute-start(bf16[2,128,1024]{2,1,0:T(8,128)(2,1)} %slice.19), channel_id=1, source_target_pairs={{48,0},{0,16},{16,32},{32,48},{112,64},{64,80},{80,96},{96,112},{1... | collective-permute-start | bytes 1572872 | tf_op jit(solution)/shard_map/ppermute | solution.py:151
  78.6 13.5 %collective-permute-start.11 = (bf16[2,128,1024]{2,1,0:T(8,128)(2,1)}, bf16[2,128,1024]{2,1,0:T(8,128)(2,1)S(1)}, u32[]{:S(2)}, u32[]{:S(2)}) collective-permute-start(bf16[2,128,1024]{2,1,0:T(8,128)(2,1)} %slice.16), channel_id=1, source_target_pairs={{64,0},{80,16},{96,32},{112,48},{128,64},{144,80},{160,96},{176,11... | collective-permute-start | bytes 1572872 | tf_op jit(solution)/shard_map/ppermute | solution.py:151
  80.5 14.7 %collective-permute-start.12 = (bf16[2,128,1024]{2,1,0:T(8,128)(2,1)}, bf16[2,128,1024]{2,1,0:T(8,128)(2,1)}, u32[]{:S(2)}, u32[]{:S(2)}) collective-permute-start(bf16[2,128,1024]{2,1,0:T(8,128)(2,1)} %slice.17), channel_id=1, source_target_pairs={{192,0},{208,16},{224,32},{240,48},{0,64},{16,80},{32,96},{48,112}... | collective-permute-start | bytes 1572872 | tf_op jit(solution)/shard_map/ppermute | solution.py:151
  86.3 8.8 %collective-permute-start.10 = (bf16[16,128,128]{2,1,0:T(8,128)(2,1)S(1)}, bf16[16,128,128]{2,1,0:T(8,128)(2,1)}, u32[]{:S(2)}, u32[]{:S(2)}) collective-permute-start(bf16[16,128,128]{2,1,0:T(8,128)(2,1)S(1)} %all-to-all-done.1.mine_ref), channel_id=1, source_target_pairs={{0,1},{1,0},{2,3},{3,2},{4,5},{5,4},{6,7},{7,6},{8,9},{9,8},{10,11... | collective-permute-start | bytes 1572872 | tf_op jit(solution)/shard_map/ppermute | solution.py:187
  101.3 0.8 copy-start
  102.1 2.9 %collective-permute-start.15 = (bf16[128,2048]{1,0:T(8,128)(2,1)}, bf16[128,2048]{1,0:T(8,128)(2,1)S(1)}, u32[]{:S(2)}, u32[]{:S(2)}) collective-permute-start(bf16[128,2048]{1,0:T(8,128)(2,1)} %get-tuple-element.12), channel_id=1, source_target_pairs={{0,1},{1,0},{2,3},{3,2},{4,5},{5,4},{6,7},{7,6},{8,9},{9,8},{10,11... | collective-permute-start | bytes 1572872 | tf_op jit(solution)/shard_map/ppermute | solution.py:189

commit v3 on v2

v3 whole, which is shorter than its diff:
```python
import functools
import math

import jax
import jax.numpy as jnp
from jax import lax
from jax.experimental import pallas as pl
from jax.experimental.pallas import tpu as pltpu
from jax.sharding import PartitionSpec as P

HDIM = 128
TILE = 512
CHAIN = 256
MASKED = -1e30
SIDE = 4
NEAR = (0, 1, 3, 2)


def attention_kernel(bounds_ref, packed_ref, out_ref, vt_ref):
    blocks, _, rows, _ = packed_ref.shape
    slab = blocks * rows
    first, second = bounds_ref[0], bounds_ref[1]
    factor = math.log2(math.e) / math.sqrt(HDIM)
    chains = TILE // CHAIN

    def start_of(position):
        return jnp.where(position >= second, second, jnp.where(position >= first, first, 0))

    def tokens(index, start, count):
        return packed_ref[pl.ds(start // rows, count // rows), index].reshape(count, HDIM)

    for block in range(blocks):
        vt_ref[block] = jnp.transpose(packed_ref[block, 2])

    def values_t(start, count):
        part = vt_ref[pl.ds(start // rows, count // rows)]
        return jnp.concatenate([part[i] for i in range(count // rows)], axis=1)

    def attend(state, query, keys, v_t, mask):
        scores = lax.dot_general(keys, query, (((1,), (1,)), ((), ())), preferred_element_type=jnp.float32)
        if mask is not None:
            scores = jnp.where(mask, scores, MASKED)
        top = jnp.max(scores, axis=0, keepdims=True)
        if state is not None:
            top = jnp.maximum(state[0], top)
        weights = jnp.exp2((scores - top) * factor)
        total = jnp.sum(weights, axis=0, keepdims=True)
        accum = jnp.dot(v_t, weights.astype(jnp.bfloat16), preferred_element_type=jnp.float32)
        if state is not None:
            rescale = jnp.exp2((state[0] - top) * factor)
            total = total + state[1] * rescale
            accum = accum + state[2] * rescale
        return top, total, accum

    for tile in range(slab // TILE):
        base = tile * TILE
        queries, positions, starts, states = [], [], [], []
        for chain in range(chains):
            at = base + chain * CHAIN
            queries.append(tokens(0, at, CHAIN))
            position = at + lax.broadcasted_iota(jnp.int32, (1, CHAIN), 1)
            starts.append(start_of(position))
            count = (chain + 1) * CHAIN
            key_pos = base + lax.broadcasted_iota(jnp.int32, (count, 1), 0)
            mask = (key_pos <= position) & (key_pos >= starts[-1])
            states.append(attend(None, queries[-1], tokens(1, base, count), values_t(base, count), mask))
        if tile:
            low = start_of(jnp.int32(base)) // TILE
            full = jnp.minimum((start_of(jnp.int32(base + TILE - 1)) + TILE - 1) // TILE, tile)

            def step(masked, j, states):
                start = pl.multiple_of(j * TILE, TILE)
                keys, v_t = tokens(1, start, TILE), values_t(start, TILE)
                out = []
                for chain in range(chains):
                    mask = None
                    if masked:
                        mask = start + lax.broadcasted_iota(jnp.int32, (TILE, 1), 0) >= starts[chain]
                    out.append(attend(states[chain], queries[chain], keys, v_t, mask))
                return tuple(out)

            states = lax.fori_loop(full, tile, lambda j, s: step(False, j, s), tuple(states))
            states = lax.fori_loop(low, full, lambda j, s: step(True, j, s), states)
        for chain in range(chains):
            _, total, accum = states[chain]
            finished = jnp.transpose((accum / total).astype(jnp.bfloat16))
            at = (base + chain * CHAIN) // rows
            out_ref[at:at + CHAIN // rows] = finished.reshape(CHAIN // rows, rows, HDIM)


def pack_kernel(queries_ref, keys_ref, values_ref, out_ref, semaphores):
    copies = []
    for head in range(out_ref.shape[0]):
        for index, ref in enumerate((queries_ref, keys_ref, values_ref)):
            source = ref.at[:, head * HDIM:(head + 1) * HDIM]
            copies.append(
                pltpu.make_async_copy(source, out_ref.at[head, index], semaphores.at[head, index])
            )
    for copy in copies:
        copy.start()
    for copy in copies:
        copy.wait()


def pack(queries, keys, values):
    rows, width = queries.shape
    hbm = pl.BlockSpec(memory_space=pl.ANY)
    return pl.pallas_call(
        pack_kernel,
        out_shape=jax.ShapeDtypeStruct((width // HDIM, 3, rows, HDIM), queries.dtype),
        in_specs=[hbm] * 3,
        out_specs=hbm,
        scratch_shapes=[pltpu.SemaphoreType.DMA((width // HDIM, 3))],
        name="pack",
    )(queries, keys, values)


def head_attention(bounds, packed):
    blocks, _, rows, _ = packed.shape
    vmem = pl.BlockSpec(memory_space=pltpu.VMEM)
    return pl.pallas_call(
        attention_kernel,
        out_shape=jax.ShapeDtypeStruct((blocks, rows, HDIM), jnp.bfloat16),
        in_specs=[pl.BlockSpec(memory_space=pltpu.SMEM), vmem],
        out_specs=vmem,
        scratch_shapes=[pltpu.VMEM((blocks, HDIM, rows), jnp.bfloat16)],
        compiler_params=pltpu.CompilerParams(vmem_limit_bytes=16 << 20),
        name="head_attention",
    )(bounds, packed)


def projection_kernel(offsets, place_ref, mine_ref, theirs_ref, *rest):
    pieces, (out_ref, sent_ref, kept_ref, left_ref, weight_ref, semaphores) = rest[:-6], rest[-6:]
    columns = pieces[0].shape[2]
    rows = mine_ref.shape[1]
    y, x, core = place_ref[0], place_ref[1], place_ref[2]
    copies, kept_copies = [], []
    at = 0
    for index, piece in enumerate(pieces):
        steps = piece.shape[0]
        copies.append(
            pltpu.make_async_copy(piece, weight_ref.at[pl.ds(at, steps)], semaphores.at[index])
        )
        copies[-1].start()
        at += steps
    at = 0
    for side, lists in enumerate(offsets):
        accum = None
        start = 0
        for places in lists:
            for dy, dx in places:
                head = ((y + dy + SIDE) % SIDE) * SIDE + (x + dx + SIDE) % SIDE
                left_ref[:rows, start:start + HDIM] = mine_ref[head]
                left_ref[rows:, start:start + HDIM] = theirs_ref[head]
                start += HDIM
        start = 0
        for places in lists:
            depth = len(places) * HDIM
            copies.pop(0).wait()
            piece = weight_ref[at:at + len(places)].reshape(depth, columns)
            added = jnp.dot(left_ref[:, start:start + depth], piece, preferred_element_type=jnp.float32)
            accum = added if accum is None else accum + added
            start += depth
            at += len(places)
        result = accum.astype(jnp.bfloat16)
        sent_ref[:, side * columns:(side + 1) * columns] = result[rows:]
        kept_ref[side] = result[:rows]
        target = out_ref.at[:, pl.ds(pl.multiple_of((2 * core + side) * columns, columns), columns)]
        kept_copies.append(
            pltpu.make_async_copy(kept_ref.at[side], target, semaphores.at[len(pieces) + side])
        )
        kept_copies[-1].start()
    for copy in kept_copies:
        copy.wait()


def project(place, mine, theirs, pieces, offsets):
    heads, rows, _ = mine.shape
    columns = pieces[0].shape[2]
    vmem = pl.BlockSpec(memory_space=pltpu.VMEM)
    hbm = pl.BlockSpec(memory_space=pltpu.HBM)
    return pl.pallas_call(
        functools.partial(projection_kernel, offsets),
        out_shape=(
            jax.ShapeDtypeStruct((rows, 4 * columns), jnp.bfloat16),
            jax.ShapeDtypeStruct((rows, 2 * columns), jnp.bfloat16),
        ),
        in_specs=[pl.BlockSpec(memory_space=pltpu.SMEM), vmem, vmem]
        + [hbm] * len(pieces),
        out_specs=(hbm, vmem),
        scratch_shapes=[
            pltpu.VMEM((2, rows, columns), jnp.bfloat16),
            pltpu.VMEM((2 * rows, heads * HDIM), jnp.bfloat16),
            pltpu.VMEM((2 * heads, HDIM, columns), jnp.bfloat16),
            pltpu.SemaphoreType.DMA((len(pieces) + 2,)),
        ],
        compiler_params=pltpu.CompilerParams(vmem_limit_bytes=20 << 20),
        name="project",
    )(place, mine, theirs, *[pltpu.with_memory_space_constraint(piece, pltpu.HBM) for piece in pieces])


def join_kernel(place_ref, got_ref, part_ref, out_ref, semaphore):
    half = got_ref.shape[1]
    other = pl.multiple_of((1 - place_ref[2]) * half, half)
    copy = pltpu.make_async_copy(got_ref, out_ref.at[:, pl.ds(other, half)], semaphore)
    copy.start()
    copy.wait()


def join(place, got, part):
    hbm = pl.BlockSpec(memory_space=pltpu.HBM)
    return pl.pallas_call(
        join_kernel,
        out_shape=jax.ShapeDtypeStruct(part.shape, part.dtype),
        in_specs=[pl.BlockSpec(memory_space=pltpu.SMEM), pl.BlockSpec(memory_space=pltpu.VMEM), hbm],
        out_specs=hbm,
        input_output_aliases={2: 0},
        scratch_shapes=[pltpu.SemaphoreType.DMA],
        name="join",
    )(place, pltpu.with_memory_space_constraint(got, pltpu.VMEM), part)


def fetch(piece, dy, dx):
    pairs = [
        (SIDE * ((y + dy + SIDE) % SIDE) + (x + dx) % SIDE, SIDE * y + x)
        for y in range(SIDE)
        for x in range(SIDE)
    ]
    return lax.ppermute(piece, "fsdp", pairs)


def per_device(queries, keys, values, out_weight, sessions):
    core = lax.axis_index("ctx") % 2
    swap = [(i, i ^ 1) for i in range(lax.axis_size("ctx"))]
    bounds = jnp.stack([jnp.sum(sessions[0] < 1), jnp.sum(sessions[0] < 2)]).astype(jnp.int32)
    place = lax.axis_index("fsdp")
    place = jnp.stack([place // SIDE, place % SIDE, core]).astype(jnp.int32)

    packed = lax.all_to_all(pack(queries, keys, values), "ctx", 0, 0, tiled=True)

    half = out_weight.shape[1] // 2
    first = lax.dynamic_slice_in_dim(out_weight, core * half, half // 2, 1)
    second = lax.dynamic_slice_in_dim(out_weight, core * half + half // 2, half // 2, 1)
    first = jnp.stack([first] + [fetch(first, 0, step) for step in NEAR[1:]])
    second = jnp.stack([second] + [fetch(second, step, 0) for step in NEAR[1:]])
    packed, _, _ = lax.optimization_barrier((packed, first, second))
    passed = [
        fetch(first[:2], 1, 0),
        fetch(first[2:], -1, 0),
        fetch(second[:2], 0, 1),
        fetch(second[2:], 0, -1),
    ]
    beside = [
        fetch(first[2:], 1, 0),
        fetch(first[:2], -1, 0),
        fetch(second[2:], 0, 1),
        fetch(second[:2], 0, -1),
    ]
    packed, *_ = lax.optimization_barrier((packed, *passed))
    far = [
        fetch(passed[0], 1, 0),
        fetch(passed[1], -1, 0),
        fetch(passed[2], 0, 1),
        fetch(passed[3], 0, -1),
    ]
    attended = head_attention(bounds, packed)
    attended, *_ = lax.optimization_barrier((attended, *beside))
    steps = [1, -1, 1, -1, 2, 2]
    lists = [NEAR[:2], NEAR[2:], NEAR[2:], NEAR[:2], NEAR[:2], NEAR[2:]]
    offsets = (
        [[(0, dx) for dx in NEAR]] + [[(dy, dx) for dx in near] for dy, near in zip(steps, lists)],
        [[(dy, 0) for dy in NEAR]] + [[(dy, dx) for dy in near] for dx, near in zip(steps, lists)],
    )
    pieces = [first, *passed[:2], *beside[:2], *far[:2], second, *passed[2:], *beside[2:], *far[2:]]

    mine = lax.all_to_all(attended, "ctx", 0, 0, tiled=True)
    theirs = lax.ppermute(mine, "ctx", swap)
    part, sent = project(place, mine, theirs, pieces, offsets)
    got = lax.ppermute(sent, "ctx", swap)
    return join(place, got, part)


def solution(mesh):
    return jax.shard_map(
        per_device,
        mesh=mesh,
        in_specs=(
            P(("fsdp", "ctx"), None),
            P(("fsdp", "ctx"), None),
            P(("fsdp", "ctx"), None),
            P("fsdp", None),
            P("fsdp", None),
        ),
        out_specs=P(("fsdp", "ctx"), None),
        check_vma=False,
    )
```

time: 109 us -> 163 us (1.50)
  Pallas kernels: 21.9 us -> 64.2 us
  starting transfers between devices: 35.7 us -> 50.1 us
  local copies, waits for them, and re-layouts: 8.34 us -> 0.07 us
  waiting for transfers between devices: 35.6 us -> 39.6 us
  other arithmetic: 5.55 us -> 7.72 us
    pallas_call x1, Pallas kernels: 2.8 us -> 49.2 us  [pack(): pl.pallas_call(pack_kernel, out_shape=jax.ShapeDtypeStruct((width // HDIM...]
    ppermute x14 -> x18, waiting for transfers between devices: 15.7 us -> 29.9 us  [fetch(): return lax.ppermute(piece, 'fsdp', pairs)]
    all_to_all x1, waiting for transfers between devices: 13.7 us -> 0.01 us  [per_device(): lax.all_to_all(pack(queries, keys, values), 'ctx', 0, 0, tiled=True)]
    ppermute x14 -> x18, starting transfers between devices: 19.7 us -> 28.3 us  [fetch(): return lax.ppermute(piece, 'fsdp', pairs)]
    slice x4 -> x0, local copies, waits for them, and re-layouts: 7.5 us -> none  [the longest x1 1.88 us: per_device(): beside[1][2:]]
    pallas_call x1, Pallas kernels: 13 us -> 7.47 us  [head_attention(): pl.pallas_call(attention_kernel, out_shape=jax.ShapeDtypeStruct((blocks,...]
    all_to_all x1, starting transfers between devices: 4.67 us -> 10.1 us  [per_device(): mine = lax.all_to_all(attended, 'ctx', 0, 0, tiled=True)]
    all_to_all x1, waiting for transfers between devices: 4.4 us -> 8.19 us  [per_device(): mine = lax.all_to_all(attended, 'ctx', 0, 0, tiled=True)]
  transfers between devices with their start and end apart: 18 -> 22, of which waited for: 9 -> 10; matrix products, arithmetic and copies ran while one was open for 10% -> 5% of each run, Pallas kernels for 12% -> 5%
where the time goes in v3:
time: 163 us; the launch traced here: 162 us
  Pallas kernels  64.2 us (39%)
  starting transfers between devices  50.1 us (31%)
  waiting for transfers between devices  39.6 us (24%)
  other arithmetic  7.72 us (5%)
    pallas_call x1, Pallas kernels, pack(): pl.pallas_call(pack_kernel, out_shape=jax.ShapeDtypeStruct((width // HDIM...  49.2 us
    ppermute x18, waiting for transfers between devices, fetch(): return lax.ppermute(piece, 'fsdp', pairs)  29.9 us
    ppermute x18, starting transfers between devices, fetch(): return lax.ppermute(piece, 'fsdp', pairs)  28.3 us
    all_to_all x1, starting transfers between devices, per_device(): lax.all_to_all(pack(queries, keys, values), 'ctx', 0, 0, tiled=True)  10.1 us
    all_to_all x1, starting transfers between devices, per_device(): mine = lax.all_to_all(attended, 'ctx', 0, 0, tiled=True)  10.1 us
    all_to_all x1, waiting for transfers between devices, per_device(): mine = lax.all_to_all(attended, 'ctx', 0, 0, tiled=True)  8.19 us
    pallas_call x1, Pallas kernels, head_attention(): pl.pallas_call(attention_kernel, out_shape=jax.ShapeDtypeStruct((blocks,...  7.47 us
    pallas_call x1, Pallas kernels, project(): pl.pallas_call(functools.partial(projection_kernel, offsets), out_shape=(...  6.07 us
  transfers between devices with their start and end apart: 22, of which 10 were waited for; matrix products, arithmetic and copies ran while one was open for 5% of the time, Pallas kernels for 5%

profile of v3, /device:TPU:1, one launch (start us, length us, event | category | flops | bytes accessed | tf_op | source)
XLA Modules:
  0.0 162.0 jit_solution(15129871928948461953)
XLA Ops:
  0.0 49.2 %pack.1 = bf16[16,3,128,128]{3,2,1,0:T(8,128)(2,1)} custom-call(bf16[128,2048]{1,0:T(8,128)(2,1)} %queries_ref.1, bf16[128,2048]{1,0:T(8,128)(2,1)} %keys_ref.1, bf16[128,2048]{1,0:T(8,128)(2,1)} %values_ref.1), custom_call_target="tpu_custom_call" | custom-call | tf_op jit(solution)/shard_map/pack/pallas_call | solution.py:108
  49.2 0.0 copy-start.5
  49.2 10.1 %all-to-all-start = ((bf16[16,3,128,128]{3,2,1,0:T(8,128)(2,1)}), bf16[16,3,128,128]{3,2,1,0:T(8,128)(2,1)S(1)}, u32[]{:S(2)}, u32[]{:S(2)}) async-start(bf16[16,3,128,128]{3,2,1,0:T(8,128)(2,1)} %pack.1), calls=%async_computation | async-start | bytes 3145728 | tf_op jit(solution)/shard_map/all_to_all | solution.py:239
  59.4 1.3 collective-permute-start.1
  60.7 2.5 %collective-permute-start.2 = (bf16[128,1024]{1,0:T(8,128)(2,1)S(1)}, bf16[128,1024]{1,0:T(8,128)(2,1)S(1)}, u32[]{:S(2)}, u32[]{:S(2)}) collective-permute-start(bf16[128,1024]{1,0:T(8,128)(2,1)S(1)} %get-tuple-element.18), channel_id=1, source_target_pairs={{32,0},{48,16},{0,32},{16,48},{96,64},{112,80},{64,96},{80,112},{1... | collective-permute-start | bytes 786440 | tf_op jit(solution)/shard_map/ppermute | solution.py:229
  63.1 1.3 collective-permute-start.4
  64.4 2.6 %collective-permute-start.5 = (bf16[128,1024]{1,0:T(8,128)(2,1)S(1)}, bf16[128,1024]{1,0:T(8,128)(2,1)S(1)}, u32[]{:S(2)}, u32[]{:S(2)}) collective-permute-start(bf16[128,1024]{1,0:T(8,128)(2,1)S(1)} %get-tuple-element.17), channel_id=1, source_target_pairs={{128,0},{144,16},{160,32},{176,48},{192,64},{208,80},{224,96},{240... | collective-permute-start | bytes 786440 | tf_op jit(solution)/shard_map/ppermute | solution.py:229
  67.0 1.2 collective-permute-start
  68.2 0.2 collective-permute-done.1
  68.4 6.6 %collective-permute-done.2 = bf16[128,1024]{1,0:T(8,128)(2,1)S(1)} collective-permute-done((bf16[128,1024]{1,0:T(8,128)(2,1)S(1)}, bf16[128,1024]{1,0:T(8,128)(2,1)S(1)}, u32[]{:S(2)}, u32[]{:S(2)}) %collective-permute-start.2) | collective-permute-done | bytes 262176 | tf_op jit(solution)/shard_map/ppermute | solution.py:229
  75.0 0.9 pad_maximum_fusion.3
  76.0 1.3 collective-permute-start.7
  77.3 0.0 collective-permute-done.4
  77.3 1.1 collective-permute-done.5
  78.3 0.8 pad_maximum_fusion.5
  79.2 0.0 collective-permute-start.9
  79.2 0.0 collective-permute-done
  79.2 0.9 pad_maximum_fusion.2
  80.1 0.4 collective-permute-start.6
  80.5 1.5 collective-permute-start.3
  81.9 14.7 %collective-permute-done.3 = bf16[128,1024]{1,0:T(8,128)(2,1)S(1)} collective-permute-done((bf16[128,1024]{1,0:T(8,128)(2,1)S(1)}, bf16[128,1024]{1,0:T(8,128)(2,1)S(1)}, u32[]{:S(2)}, u32[]{:S(2)}) %collective-permute-start.3) | collective-permute-done | bytes 262176 | tf_op jit(solution)/shard_map/ppermute | solution.py:229
  96.6 0.8 pad_maximum_fusion.4
  97.5 3.5 %collective-permute-start.8 = (bf16[2,128,1024]{2,1,0:T(8,128)(2,1)}, bf16[2,128,1024]{2,1,0:T(8,128)(2,1)}, u32[]{:S(2)}, u32[]{:S(2)}) collective-permute-start(bf16[2,128,1024]{2,1,0:T(8,128)(2,1)} %pad_maximum_fusion.4), channel_id=1, source_target_pairs={{16,0},{32,16},{48,32},{0,48},{80,64},{96,80},{112,96},{64,112},{1... | collective-permute-start | bytes 1572872 | tf_op jit(solution)/shard_map/ppermute | solution.py:229
  101.0 2.0 %collective-permute-start.10 = (bf16[2,128,1024]{2,1,0:T(8,128)(2,1)}, bf16[2,128,1024]{2,1,0:T(8,128)(2,1)}, u32[]{:S(2)}, u32[]{:S(2)}) collective-permute-start(bf16[2,128,1024]{2,1,0:T(8,128)(2,1)} %pad_maximum_fusion.3), channel_id=1, source_target_pairs={{64,0},{80,16},{96,32},{112,48},{128,64},{144,80},{160,96},{176,11... | collective-permute-start | bytes 1572872 | tf_op jit(solution)/shard_map/ppermute | solution.py:229
  103.0 0.0 collective-permute-done.7.rest_2_
  103.0 0.0 collective-permute-start.12
  103.0 0.1 collective-permute-start.11
  103.1 1.6 collective-permute-start.13
  104.8 0.7 fusion
  105.4 1.3 pad_add_fusion.1.bounds_ref
  106.7 1.1 pad_maximum_fusion.1.rest_7_
  107.8 1.1 pad_maximum_fusion.rest_0_
  108.9 0.8 collective-permute-done.8.rest_8_
  109.7 7.5 %head_attention.1 = bf16[16,128,128]{2,1,0:T(8,128)(2,1)} custom-call(s32[2]{0:T(128)S(1)} %pad_add_fusion.1.bounds_ref, bf16[16,3,128,128]{3,2,1,0:T(8,128)(2,1)S(1)} %all-to-all-done.packed_ref), custom_call_target="tpu_custom_call" | custom-call | tf_op jit(solution)/shard_map/head_attention/pallas_call | solution.py:121
  117.2 3.8 %collective-permute-done.12.rest_10_ = bf16[2,128,1024]{2,1,0:T(8,128)(2,1)} collective-permute-done((bf16[2,128,1024]{2,1,0:T(8,128)(2,1)}, bf16[2,128,1024]{2,1,0:T(8,128)(2,1)}, u32[]{:S(2)}, u32[]{:S(2)}) %collective-permute-start.12) | collective-permute-done | bytes 524320 | tf_op jit(solution)/shard_map/ppermute | solution.py:229
  121.0 10.1 %all-to-all-start.1 = ((bf16[16,128,128]{2,1,0:T(8,128)(2,1)}), bf16[16,128,128]{2,1,0:T(8,128)(2,1)S(1)}, u32[]{:S(2)}, u32[]{:S(2)}) async-start(bf16[16,128,128]{2,1,0:T(8,128)(2,1)} %head_attention.1), calls=%async_computation.1 | async-start | bytes 1048576 | tf_op jit(solution)/shard_map/all_to_all | solution.py:276
  131.1 0.7 collective-permute-start.16
  131.8 2.2 %collective-permute-start.18 = (bf16[2,128,1024]{2,1,0:T(8,128)(2,1)S(1)}, bf16[2,128,1024]{2,1,0:T(8,128)(2,1)}, u32[]{:S(2)}, u32[]{:S(2)}) collective-permute-start(bf16[2,128,1024]{2,1,0:T(8,128)(2,1)S(1)} %collective-permute-done.9.rest_9_), channel_id=1, source_target_pairs={{48,0},{0,16},{16,32},{32,48},{112,64},{64,80},{80,96},{96,112},{1... | collective-permute-start | bytes 1572872 | tf_op jit(solution)/shard_map/ppermute | solution.py:229
  134.0 6.2 %collective-permute-start.17 = (bf16[2,128,1024]{2,1,0:T(8,128)(2,1)}, bf16[2,128,1024]{2,1,0:T(8,128)(2,1)}, u32[]{:S(2)}, u32[]{:S(2)}) collective-permute-start(bf16[2,128,1024]{2,1,0:T(8,128)(2,1)} %collective-permute-done.8.rest_8_), channel_id=1, source_target_pairs={{16,0},{32,16},{48,32},{0,48},{80,64},{96,80},{112,96},{64,112},{1... | collective-permute-start | bytes 1572872 | tf_op jit(solution)/shard_map/ppermute | solution.py:229
  140.2 8.2 %all-to-all-done.1.mine_ref = bf16[16,128,128]{2,1,0:T(8,128)(2,1)S(1)} async-done(((bf16[16,128,128]{2,1,0:T(8,128)(2,1)}), bf16[16,128,128]{2,1,0:T(8,128)(2,1)S(1)}, u32[]{:S(2)}, u32[]{:S(2)}) %all-to-all-start.1) | async-done | bytes 524320 | tf_op jit(solution)/shard_map/all_to_all | solution.py:276
  148.4 0.0 collective-permute-start.14
  148.4 0.1 pad_add_fusion.place_ref
  148.5 1.3 collective-permute-done.18.rest_13_
  149.8 1.4 collective-permute-done.17.rest_12_
  151.1 6.1 %project.1 = (bf16[128,4096]{1,0:T(8,128)(2,1)}, bf16[128,2048]{1,0:T(8,128)(2,1)S(1)}) custom-call(s32[3]{0:T(128)S(1)} %pad_add_fusion.place_ref, bf16[16,128,128]{2,1,0:T(8,128)(2,1)S(1)} %all-to-all-done.1.mine_ref, bf16[16,128,128]{2,1,0:T(8,128)(2,1)S(1)} %collective-permute-done.14.theirs_ref, bf16[4,128,1024]{2,1,0:T(8,128)(2,1)} %pad_maximum_fusion.rest_0_, ...), custom_call_target="tpu_custom_call" | custom-call | tf_op jit(solution)/shard_map/project/pallas_call | solution.py:182
  157.2 1.6 collective-permute-start.19
  158.8 1.5 collective-permute-done.19.got_ref
  160.4 1.5 join.1
  (24 shorter events, 0.1 us)
Async XLA Ops:
  49.2 10.1 %copy-start.5 = (bf16[128,4096]{1,0:T(8,128)(2,1)S(1)}, bf16[128,4096]{1,0:T(8,128)(2,1)}, u32[]{:S(2)}) copy-start(bf16[128,4096]{1,0:T(8,128)(2,1)} %param.8) | copy-start | bytes 3145732
  49.2 59.7 %all-to-all-start = ((bf16[16,3,128,128]{3,2,1,0:T(8,128)(2,1)}), bf16[16,3,128,128]{3,2,1,0:T(8,128)(2,1)S(1)}, u32[]{:S(2)}, u32[]{:S(2)}) async-start(bf16[16,3,128,128]{3,2,1,0:T(8,128)(2,1)} %pack.1), calls=%async_computation | async-start | bytes 3145728 | tf_op jit(solution)/shard_map/all_to_all | solution.py:239
  59.4 9.1 %collective-permute-start.1 = (bf16[128,1024]{1,0:T(8,128)(2,1)S(1)}, bf16[128,1024]{1,0:T(8,128)(2,1)S(1)}, u32[]{:S(2)}, u32[]{:S(2)}) collective-permute-start(bf16[128,1024]{1,0:T(8,128)(2,1)S(1)} %get-tuple-element.18), channel_id=1, source_target_pairs={{48,0},{0,16},{16,32},{32,48},{112,64},{64,80},{80,96},{96,112},{1... | collective-permute-start | bytes 786440 | tf_op jit(solution)/shard_map/ppermute | solution.py:229
  60.7 14.4 %collective-permute-start.2 = (bf16[128,1024]{1,0:T(8,128)(2,1)S(1)}, bf16[128,1024]{1,0:T(8,128)(2,1)S(1)}, u32[]{:S(2)}, u32[]{:S(2)}) collective-permute-start(bf16[128,1024]{1,0:T(8,128)(2,1)S(1)} %get-tuple-element.18), channel_id=1, source_target_pairs={{32,0},{48,16},{0,32},{16,48},{96,64},{112,80},{64,96},{80,112},{1... | collective-permute-start | bytes 786440 | tf_op jit(solution)/shard_map/ppermute | solution.py:229
  63.1 14.1 %collective-permute-start.4 = (bf16[128,1024]{1,0:T(8,128)(2,1)S(1)}, bf16[128,1024]{1,0:T(8,128)(2,1)S(1)}, u32[]{:S(2)}, u32[]{:S(2)}) collective-permute-start(bf16[128,1024]{1,0:T(8,128)(2,1)S(1)} %get-tuple-element.17), channel_id=1, source_target_pairs={{192,0},{208,16},{224,32},{240,48},{0,64},{16,80},{32,96},{48,112}... | collective-permute-start | bytes 786440 | tf_op jit(solution)/shard_map/ppermute | solution.py:229
  64.4 13.9 %collective-permute-start.5 = (bf16[128,1024]{1,0:T(8,128)(2,1)S(1)}, bf16[128,1024]{1,0:T(8,128)(2,1)S(1)}, u32[]{:S(2)}, u32[]{:S(2)}) collective-permute-start(bf16[128,1024]{1,0:T(8,128)(2,1)S(1)} %get-tuple-element.17), channel_id=1, source_target_pairs={{128,0},{144,16},{160,32},{176,48},{192,64},{208,80},{224,96},{240... | collective-permute-start | bytes 786440 | tf_op jit(solution)/shard_map/ppermute | solution.py:229
  67.0 12.1 %collective-permute-start = (bf16[128,1024]{1,0:T(8,128)(2,1)S(1)}, bf16[128,1024]{1,0:T(8,128)(2,1)S(1)}, u32[]{:S(2)}, u32[]{:S(2)}) collective-permute-start(bf16[128,1024]{1,0:T(8,128)(2,1)S(1)} %get-tuple-element.18), channel_id=1, source_target_pairs={{16,0},{32,16},{48,32},{0,48},{80,64},{96,80},{112,96},{64,112},{1... | collective-permute-start | bytes 786440 | tf_op jit(solution)/shard_map/ppermute | solution.py:229
  76.0 27.0 %collective-permute-start.7 = (bf16[2,128,1024]{2,1,0:T(8,128)(2,1)}, bf16[2,128,1024]{2,1,0:T(8,128)(2,1)S(1)}, u32[]{:S(2)}, u32[]{:S(2)}) collective-permute-start(bf16[2,128,1024]{2,1,0:T(8,128)(2,1)} %pad_maximum_fusion.3), channel_id=1, source_target_pairs={{192,0},{208,16},{224,32},{240,48},{0,64},{16,80},{32,96},{48,112}... | collective-permute-start | bytes 1572872 | tf_op jit(solution)/shard_map/ppermute | solution.py:229
  78.3 26.4 %copy-start.6 = (s32[1,2048]{1,0:T(1,128)S(1)}, s32[1,2048]{1,0:T(1,128)}, u32[]{:S(2)}) copy-start(s32[1,2048]{1,0:T(1,128)} %param.9) | copy-start | bytes 24580
  79.2 23.8 %collective-permute-start.9 = (bf16[2,128,1024]{2,1,0:T(8,128)(2,1)}, bf16[2,128,1024]{2,1,0:T(8,128)(2,1)S(1)}, u32[]{:S(2)}, u32[]{:S(2)}) collective-permute-start(bf16[2,128,1024]{2,1,0:T(8,128)(2,1)} %pad_maximum_fusion.5), channel_id=1, source_target_pairs={{48,0},{0,16},{16,32},{32,48},{112,64},{64,80},{80,96},{96,112},{1... | collective-permute-start | bytes 1572872 | tf_op jit(solution)/shard_map/ppermute | solution.py:229
  80.1 23.0 %collective-permute-start.6 = (bf16[2,128,1024]{2,1,0:T(8,128)(2,1)}, bf16[2,128,1024]{2,1,0:T(8,128)(2,1)S(1)}, u32[]{:S(2)}, u32[]{:S(2)}) collective-permute-start(bf16[2,128,1024]{2,1,0:T(8,128)(2,1)} %pad_maximum_fusion.2), channel_id=1, source_target_pairs={{64,0},{80,16},{96,32},{112,48},{128,64},{144,80},{160,96},{176,11... | collective-permute-start | bytes 1572872 | tf_op jit(solution)/shard_map/ppermute | solution.py:229
  80.5 16.2 %collective-permute-start.3 = (bf16[128,1024]{1,0:T(8,128)(2,1)S(1)}, bf16[128,1024]{1,0:T(8,128)(2,1)S(1)}, u32[]{:S(2)}, u32[]{:S(2)}) collective-permute-start(bf16[128,1024]{1,0:T(8,128)(2,1)S(1)} %get-tuple-element.17), channel_id=1, source_target_pairs={{64,0},{80,16},{96,32},{112,48},{128,64},{144,80},{160,96},{176,11... | collective-permute-start | bytes 786440 | tf_op jit(solution)/shard_map/ppermute | solution.py:229
  97.5 12.2 %collective-permute-start.8 = (bf16[2,128,1024]{2,1,0:T(8,128)(2,1)}, bf16[2,128,1024]{2,1,0:T(8,128)(2,1)}, u32[]{:S(2)}, u32[]{:S(2)}) collective-permute-start(bf16[2,128,1024]{2,1,0:T(8,128)(2,1)} %pad_maximum_fusion.4), channel_id=1, source_target_pairs={{16,0},{32,16},{48,32},{0,48},{80,64},{96,80},{112,96},{64,112},{1... | collective-permute-start | bytes 1572872 | tf_op jit(solution)/shard_map/ppermute | solution.py:229
  101.0 16.2 %collective-permute-start.10 = (bf16[2,128,1024]{2,1,0:T(8,128)(2,1)}, bf16[2,128,1024]{2,1,0:T(8,128)(2,1)}, u32[]{:S(2)}, u32[]{:S(2)}) collective-permute-start(bf16[2,128,1024]{2,1,0:T(8,128)(2,1)} %pad_maximum_fusion.3), channel_id=1, source_target_pairs={{64,0},{80,16},{96,32},{112,48},{128,64},{144,80},{160,96},{176,11... | collective-permute-start | bytes 1572872 | tf_op jit(solution)/shard_map/ppermute | solution.py:229
  103.0 28.1 %copy-start.1 = (bf16[2,128,1024]{2,1,0:T(8,128)(2,1)}, bf16[2,128,1024]{2,1,0:T(8,128)(2,1)S(1)}, u32[]{:S(2)}) copy-start(bf16[2,128,1024]{2,1,0:T(8,128)(2,1)S(1)} %collective-permute-done.7.rest_2_) | copy-start | bytes 1572868
  103.0 18.0 %collective-permute-start.12 = (bf16[2,128,1024]{2,1,0:T(8,128)(2,1)}, bf16[2,128,1024]{2,1,0:T(8,128)(2,1)}, u32[]{:S(2)}, u32[]{:S(2)}) collective-permute-start(bf16[2,128,1024]{2,1,0:T(8,128)(2,1)} %pad_maximum_fusion.5), channel_id=1, source_target_pairs={{16,0},{32,16},{48,32},{0,48},{80,64},{96,80},{112,96},{64,112},{1... | collective-permute-start | bytes 1572872 | tf_op jit(solution)/shard_map/ppermute | solution.py:229
  103.0 28.7 %copy-start.2 = (bf16[2,128,1024]{2,1,0:T(8,128)(2,1)}, bf16[2,128,1024]{2,1,0:T(8,128)(2,1)S(1)}, u32[]{:S(2)}) copy-start(bf16[2,128,1024]{2,1,0:T(8,128)(2,1)S(1)} %collective-permute-done.9.rest_9_) | copy-start | bytes 1572868
  103.0 17.9 %collective-permute-start.11 = (bf16[2,128,1024]{2,1,0:T(8,128)(2,1)}, bf16[2,128,1024]{2,1,0:T(8,128)(2,1)}, u32[]{:S(2)}, u32[]{:S(2)}) collective-permute-start(bf16[2,128,1024]{2,1,0:T(8,128)(2,1)} %pad_maximum_fusion.2), channel_id=1, source_target_pairs={{192,0},{208,16},{224,32},{240,48},{0,64},{16,80},{32,96},{48,112}... | collective-permute-start | bytes 1572872 | tf_op jit(solution)/shard_map/ppermute | solution.py:229
  103.1 30.8 %copy-start.3 = (bf16[2,128,1024]{2,1,0:T(8,128)(2,1)}, bf16[2,128,1024]{2,1,0:T(8,128)(2,1)S(1)}, u32[]{:S(2)}) copy-start(bf16[2,128,1024]{2,1,0:T(8,128)(2,1)S(1)} %collective-permute-done.6.rest_1_) | copy-start | bytes 1572868
  103.1 17.8 %collective-permute-start.13 = (bf16[2,128,1024]{2,1,0:T(8,128)(2,1)}, bf16[2,128,1024]{2,1,0:T(8,128)(2,1)}, u32[]{:S(2)}, u32[]{:S(2)}) collective-permute-start(bf16[2,128,1024]{2,1,0:T(8,128)(2,1)} %pad_maximum_fusion.4), channel_id=1, source_target_pairs={{48,0},{0,16},{16,32},{32,48},{112,64},{64,80},{80,96},{96,112},{1... | collective-permute-start | bytes 1572872 | tf_op jit(solution)/shard_map/ppermute | solution.py:229
  121.0 27.4 %all-to-all-start.1 = ((bf16[16,128,128]{2,1,0:T(8,128)(2,1)}), bf16[16,128,128]{2,1,0:T(8,128)(2,1)S(1)}, u32[]{:S(2)}, u32[]{:S(2)}) async-start(bf16[16,128,128]{2,1,0:T(8,128)(2,1)} %head_attention.1), calls=%async_computation.1 | async-start | bytes 1048576 | tf_op jit(solution)/shard_map/all_to_all | solution.py:276
  131.1 17.4 %collective-permute-start.16 = (bf16[2,128,1024]{2,1,0:T(8,128)(2,1)S(1)}, bf16[2,128,1024]{2,1,0:T(8,128)(2,1)S(1)}, u32[]{:S(2)}, u32[]{:S(2)}) collective-permute-start(bf16[2,128,1024]{2,1,0:T(8,128)(2,1)S(1)} %collective-permute-done.7.rest_2_), channel_id=1, source_target_pairs={{192,0},{208,16},{224,32},{240,48},{0,64},{16,80},{32,96},{48,112}... | collective-permute-start | bytes 1572872 | tf_op jit(solution)/shard_map/ppermute | solution.py:229
  131.8 18.0 %collective-permute-start.18 = (bf16[2,128,1024]{2,1,0:T(8,128)(2,1)S(1)}, bf16[2,128,1024]{2,1,0:T(8,128)(2,1)}, u32[]{:S(2)}, u32[]{:S(2)}) collective-permute-start(bf16[2,128,1024]{2,1,0:T(8,128)(2,1)S(1)} %collective-permute-done.9.rest_9_), channel_id=1, source_target_pairs={{48,0},{0,16},{16,32},{32,48},{112,64},{64,80},{80,96},{96,112},{1... | collective-permute-start | bytes 1572872 | tf_op jit(solution)/shard_map/ppermute | solution.py:229
  134.0 15.8 %collective-permute-start.15 = (bf16[2,128,1024]{2,1,0:T(8,128)(2,1)S(1)}, bf16[2,128,1024]{2,1,0:T(8,128)(2,1)}, u32[]{:S(2)}, u32[]{:S(2)}) collective-permute-start(bf16[2,128,1024]{2,1,0:T(8,128)(2,1)S(1)} %collective-permute-done.6.rest_1_), channel_id=1, source_target_pairs={{64,0},{80,16},{96,32},{112,48},{128,64},{144,80},{160,96},{176,11... | collective-permute-start | bytes 1572872 | tf_op jit(solution)/shard_map/ppermute | solution.py:229
  134.0 17.2 %collective-permute-start.17 = (bf16[2,128,1024]{2,1,0:T(8,128)(2,1)}, bf16[2,128,1024]{2,1,0:T(8,128)(2,1)}, u32[]{:S(2)}, u32[]{:S(2)}) collective-permute-start(bf16[2,128,1024]{2,1,0:T(8,128)(2,1)} %collective-permute-done.8.rest_8_), channel_id=1, source_target_pairs={{16,0},{32,16},{48,32},{0,48},{80,64},{96,80},{112,96},{64,112},{1... | collective-permute-start | bytes 1572872 | tf_op jit(solution)/shard_map/ppermute | solution.py:229
  148.4 2.8 %collective-permute-start.14 = (bf16[16,128,128]{2,1,0:T(8,128)(2,1)S(1)}, bf16[16,128,128]{2,1,0:T(8,128)(2,1)S(1)}, u32[]{:S(2)}, u32[]{:S(2)}) collective-permute-start(bf16[16,128,128]{2,1,0:T(8,128)(2,1)S(1)} %all-to-all-done.1.mine_ref), channel_id=1, source_target_pairs={{0,1},{1,0},{2,3},{3,2},{4,5},{5,4},{6,7},{7,6},{8,9},{9,8},{10,11... | collective-permute-start | bytes 1572872 | tf_op jit(solution)/shard_map/ppermute | solution.py:277
  148.5 8.8 %copy-start = (s32[3]{0:T(128)}, s32[3]{0:T(128)S(1)}, u32[]{:S(2)}) copy-start(s32[3]{0:T(128)S(1)} %pad_add_fusion.place_ref) | copy-start | bytes 40
  148.5 2.7 %copy-start.4 = (bf16[2,128,1024]{2,1,0:T(8,128)(2,1)}, bf16[2,128,1024]{2,1,0:T(8,128)(2,1)S(1)}, u32[]{:S(2)}) copy-start(bf16[2,128,1024]{2,1,0:T(8,128)(2,1)S(1)} %collective-permute-done.16.rest_6_) | copy-start | bytes 1572868
  157.2 3.1 %collective-permute-start.19 = (bf16[128,2048]{1,0:T(8,128)(2,1)S(1)}, bf16[128,2048]{1,0:T(8,128)(2,1)S(1)}, u32[]{:S(2)}, u32[]{:S(2)}) collective-permute-start(bf16[128,2048]{1,0:T(8,128)(2,1)S(1)} %get-tuple-element.13), channel_id=1, source_target_pairs={{0,1},{1,0},{2,3},{3,2},{4,5},{5,4},{6,7},{7,6},{8,9},{9,8},{10,11... | collective-permute-start | bytes 1572872 | tf_op jit(solution)/shard_map/ppermute | solution.py:279

commit v4 on v3

--- a/solution.py
+++ b/solution.py
@@ -1,4 +1,3 @@
-import functools
 import math
 
 import jax
@@ -14,6 +13,7 @@
 MASKED = -1e30
 SIDE = 4
 NEAR = (0, 1, 3, 2)
+STRIP = 512
 
 
 def attention_kernel(bounds_ref, packed_ref, out_ref, vt_ref):
@@ -88,29 +88,22 @@
             out_ref[at:at + CHAIN // rows] = finished.reshape(CHAIN // rows, rows, HDIM)
 
 
-def pack_kernel(queries_ref, keys_ref, values_ref, out_ref, semaphores):
-    copies = []
-    for head in range(out_ref.shape[0]):
-        for index, ref in enumerate((queries_ref, keys_ref, values_ref)):
-            source = ref.at[:, head * HDIM:(head + 1) * HDIM]
-            copies.append(
-                pltpu.make_async_copy(source, out_ref.at[head, index], semaphores.at[head, index])
-            )
-    for copy in copies:
-        copy.start()
-    for copy in copies:
-        copy.wait()
+def pack_kernel(queries_ref, keys_ref, values_ref, out_ref):
+    for index, ref in enumerate((queries_ref, keys_ref, values_ref)):
+        for head in range(out_ref.shape[0]):
+            out_ref[head, index] = ref[:, head * HDIM:(head + 1) * HDIM]
 
 
 def pack(queries, keys, values):
     rows, width = queries.shape
-    hbm = pl.BlockSpec(memory_space=pl.ANY)
+    heads = width // HDIM
+    half = pl.BlockSpec((rows, width // 2), lambda i: (0, i))
     return pl.pallas_call(
         pack_kernel,
-        out_shape=jax.ShapeDtypeStruct((width // HDIM, 3, rows, HDIM), queries.dtype),
-        in_specs=[hbm] * 3,
-        out_specs=hbm,
-        scratch_shapes=[pltpu.SemaphoreType.DMA((width // HDIM, 3))],
+        out_shape=jax.ShapeDtypeStruct((heads, 3, rows, HDIM), queries.dtype),
+        grid=(2,),
+        in_specs=[half] * 3,
+        out_specs=pl.BlockSpec((heads // 2, 3, rows, HDIM), lambda i: (i, 0, 0, 0)),
         name="pack",
     )(queries, keys, values)
 
@@ -129,74 +122,76 @@
     )(bounds, packed)
 
 
-def projection_kernel(offsets, place_ref, mine_ref, theirs_ref, *rest):
-    pieces, (out_ref, sent_ref, kept_ref, left_ref, weight_ref, semaphores) = rest[:-6], rest[-6:]
+def projection_kernel(place_ref, mine_ref, theirs_ref, *rest):
+    pieces = rest[:SIDE]
+    out_ref, sent_ref, kept_ref, left_ref, weight_ref, weight_semaphores, semaphores = rest[SIDE:]
     columns = pieces[0].shape[2]
     rows = mine_ref.shape[1]
+    depth = SIDE * HDIM
+    loads = []
+    for strip in range(columns // STRIP):
+        for i, piece in enumerate(pieces):
+            source = piece.at[:, :, strip * STRIP:(strip + 1) * STRIP]
+            loads.append(
+                pltpu.make_async_copy(source, weight_ref.at[strip, i], weight_semaphores.at[strip, i])
+            )
+            loads[-1].start()
     y, x, core = place_ref[0], place_ref[1], place_ref[2]
-    copies, kept_copies = [], []
-    at = 0
-    for index, piece in enumerate(pieces):
-        steps = piece.shape[0]
+    for i, far in enumerate(NEAR):
+        for j, near in enumerate(NEAR):
+            dy = jnp.where(core == 0, far, near)
+            dx = jnp.where(core == 0, near, far)
+            head = ((y + dy) % SIDE) * SIDE + (x + dx) % SIDE
+            at = slice(i * depth + j * HDIM, i * depth + (j + 1) * HDIM)
+            left_ref[:rows, at] = mine_ref[head]
+            left_ref[rows:, at] = theirs_ref[head]
+    copies = []
+    for strip in range(columns // STRIP):
+        at = slice(strip * STRIP, (strip + 1) * STRIP)
+        for load in loads[strip * SIDE:(strip + 1) * SIDE]:
+            load.wait()
+        result = jnp.dot(
+            left_ref[...],
+            weight_ref[strip].reshape(SIDE * depth, STRIP),
+            preferred_element_type=jnp.float32,
+        ).astype(jnp.bfloat16)
+        sent_ref[:, at] = result[rows:]
+        kept_ref[strip] = result[:rows]
+        target = pl.multiple_of(core * columns + strip * STRIP, STRIP)
         copies.append(
-            pltpu.make_async_copy(piece, weight_ref.at[pl.ds(at, steps)], semaphores.at[index])
+            pltpu.make_async_copy(
+                kept_ref.at[strip], out_ref.at[:, pl.ds(target, STRIP)], semaphores.at[strip]
+            )
         )
         copies[-1].start()
-        at += steps
-    at = 0
-    for side, lists in enumerate(offsets):
-        accum = None
-        start = 0
-        for places in lists:
-            for dy, dx in places:
-                head = ((y + dy + SIDE) % SIDE) * SIDE + (x + dx + SIDE) % SIDE
-                left_ref[:rows, start:start + HDIM] = mine_ref[head]
-                left_ref[rows:, start:start + HDIM] = theirs_ref[head]
-                start += HDIM
-        start = 0
-        for places in lists:
-            depth = len(places) * HDIM
-            copies.pop(0).wait()
-            piece = weight_ref[at:at + len(places)].reshape(depth, columns)
-            added = jnp.dot(left_ref[:, start:start + depth], piece, preferred_element_type=jnp.float32)
-            accum = added if accum is None else accum + added
-            start += depth
-            at += len(places)
-        result = accum.astype(jnp.bfloat16)
-        sent_ref[:, side * columns:(side + 1) * columns] = result[rows:]
-        kept_ref[side] = result[:rows]
-        target = out_ref.at[:, pl.ds(pl.multiple_of((2 * core + side) * columns, columns), columns)]
-        kept_copies.append(
-            pltpu.make_async_copy(kept_ref.at[side], target, semaphores.at[len(pieces) + side])
-        )
-        kept_copies[-1].start()
-    for copy in kept_copies:
+    for copy in copies:
         copy.wait()
 
 
-def project(place, mine, theirs, pieces, offsets):
+def project(place, mine, theirs, pieces):
     heads, rows, _ = mine.shape
     columns = pieces[0].shape[2]
     vmem = pl.BlockSpec(memory_space=pltpu.VMEM)
     hbm = pl.BlockSpec(memory_space=pltpu.HBM)
-    return pl.pallas_call(
-        functools.partial(projection_kernel, offsets),
+    pieces = [pltpu.with_memory_space_constraint(piece, pltpu.HBM) for piece in pieces]
+    return pl.pallas_call(
+        projection_kernel,
         out_shape=(
-            jax.ShapeDtypeStruct((rows, 4 * columns), jnp.bfloat16),
             jax.ShapeDtypeStruct((rows, 2 * columns), jnp.bfloat16),
+            jax.ShapeDtypeStruct((rows, columns), jnp.bfloat16),
         ),
-        in_specs=[pl.BlockSpec(memory_space=pltpu.SMEM), vmem, vmem]
-        + [hbm] * len(pieces),
+        in_specs=[pl.BlockSpec(memory_space=pltpu.SMEM), vmem, vmem] + [hbm] * SIDE,
         out_specs=(hbm, vmem),
         scratch_shapes=[
-            pltpu.VMEM((2, rows, columns), jnp.bfloat16),
+            pltpu.VMEM((columns // STRIP, rows, STRIP), jnp.bfloat16),
             pltpu.VMEM((2 * rows, heads * HDIM), jnp.bfloat16),
-            pltpu.VMEM((2 * heads, HDIM, columns), jnp.bfloat16),
-            pltpu.SemaphoreType.DMA((len(pieces) + 2,)),
+            pltpu.VMEM((columns // STRIP, SIDE, SIDE, HDIM, STRIP), jnp.bfloat16),
+            pltpu.SemaphoreType.DMA((columns // STRIP, SIDE)),
+            pltpu.SemaphoreType.DMA((columns // STRIP,)),
         ],
         compiler_params=pltpu.CompilerParams(vmem_limit_bytes=20 << 20),
         name="project",
-    )(place, mine, theirs, *[pltpu.with_memory_space_constraint(piece, pltpu.HBM) for piece in pieces])
+    )(place, mine, theirs, *pieces)
 
 
 def join_kernel(place_ref, got_ref, part_ref, out_ref, semaphore):
@@ -220,13 +215,19 @@
     )(place, pltpu.with_memory_space_constraint(got, pltpu.VMEM), part)
 
 
-def fetch(piece, dy, dx):
-    pairs = [
-        (SIDE * ((y + dy + SIDE) % SIDE) + (x + dx) % SIDE, SIDE * y + x)
-        for y in range(SIDE)
-        for x in range(SIDE)
-    ]
-    return lax.ppermute(piece, "fsdp", pairs)
+def fetch(piece, step, near):
+    count = lax.axis_size("ctx")
+    pairs = []
+    for y in range(SIDE):
+        for x in range(SIDE):
+            for place in range(count):
+                along_x = (place % 2 == 0) == near
+                source_y = y if along_x else (y + step) % SIDE
+                source_x = (x + step) % SIDE if along_x else x
+                pairs.append(
+                    ((SIDE * source_y + source_x) * count + place, (SIDE * y + x) * count + place)
+                )
+    return lax.ppermute(piece, ("fsdp", "ctx"), pairs)
 
 
 def per_device(queries, keys, values, out_weight, sessions):
@@ -239,43 +240,15 @@
     packed = lax.all_to_all(pack(queries, keys, values), "ctx", 0, 0, tiled=True)
 
     half = out_weight.shape[1] // 2
-    first = lax.dynamic_slice_in_dim(out_weight, core * half, half // 2, 1)
-    second = lax.dynamic_slice_in_dim(out_weight, core * half + half // 2, half // 2, 1)
-    first = jnp.stack([first] + [fetch(first, 0, step) for step in NEAR[1:]])
-    second = jnp.stack([second] + [fetch(second, step, 0) for step in NEAR[1:]])
-    packed, _, _ = lax.optimization_barrier((packed, first, second))
-    passed = [
-        fetch(first[:2], 1, 0),
-        fetch(first[2:], -1, 0),
-        fetch(second[:2], 0, 1),
-        fetch(second[2:], 0, -1),
-    ]
-    beside = [
-        fetch(first[2:], 1, 0),
-        fetch(first[:2], -1, 0),
-        fetch(second[2:], 0, 1),
-        fetch(second[:2], 0, -1),
-    ]
-    packed, *_ = lax.optimization_barrier((packed, *passed))
-    far = [
-        fetch(passed[0], 1, 0),
-        fetch(passed[1], -1, 0),
-        fetch(passed[2], 0, 1),
-        fetch(passed[3], 0, -1),
-    ]
+    own = lax.dynamic_slice_in_dim(out_weight, core * half, half, 1)
+    line = jnp.stack([own] + [fetch(own, step, True) for step in NEAR[1:]])
+    packed, _ = lax.optimization_barrier((packed, line))
+    pieces = [line] + [fetch(line, step, False) for step in NEAR[1:]]
+
     attended = head_attention(bounds, packed)
-    attended, *_ = lax.optimization_barrier((attended, *beside))
-    steps = [1, -1, 1, -1, 2, 2]
-    lists = [NEAR[:2], NEAR[2:], NEAR[2:], NEAR[:2], NEAR[:2], NEAR[2:]]
-    offsets = (
-        [[(0, dx) for dx in NEAR]] + [[(dy, dx) for dx in near] for dy, near in zip(steps, lists)],
-        [[(dy, 0) for dy in NEAR]] + [[(dy, dx) for dy in near] for dx, near in zip(steps, lists)],
-    )
-    pieces = [first, *passed[:2], *beside[:2], *far[:2], second, *passed[2:], *beside[2:], *far[2:]]
-
     mine = lax.all_to_all(attended, "ctx", 0, 0, tiled=True)
     theirs = lax.ppermute(mine, "ctx", swap)
-    part, sent = project(place, mine, theirs, pieces, offsets)
+    part, sent = project(place, mine, theirs, pieces)
     got = lax.ppermute(sent, "ctx", swap)
     return join(place, got, part)
 

time: 163 us -> 92.7 us (0.57)
  Pallas kernels: 64.2 us -> 16.4 us
  starting transfers between devices: 50.1 us -> 21.1 us
  blocking collectives: 0 us -> 21.4 us
  waiting for transfers between devices: 39.6 us -> 28.2 us
  other arithmetic: 7.72 us -> 3.67 us
    pallas_call x2, Pallas kernels: 55.2 us -> 8.25 us  [the longest x1 5.71 us: project(): pl.pallas_call(projection_kernel, out_shape=(jax.ShapeDtypeStruct((rows,...]
    all_to_all x0 -> x1, blocking collectives: none -> 21.4 us  [per_device(): mine = lax.all_to_all(attended, 'ctx', 0, 0, tiled=True)]
    ppermute x18 -> x6, starting transfers between devices: 28.3 us -> 9.88 us  [fetch(): return lax.ppermute(piece, ('fsdp', 'ctx'), pairs)]
    ppermute x18 -> x6, waiting for transfers between devices: 29.9 us -> 13.1 us  [fetch(): return lax.ppermute(piece, ('fsdp', 'ctx'), pairs)]
    all_to_all x1, waiting for transfers between devices: 0.01 us -> 12.9 us  [per_device(): lax.all_to_all(pack(queries, keys, values), 'ctx', 0, 0, tiled=True)]
    all_to_all x1 -> x0, starting transfers between devices: 10.1 us -> none  [per_device(): mine = lax.all_to_all(attended, 'ctx', 0, 0, tiled=True)]
    all_to_all x1 -> x0, waiting for transfers between devices: 8.19 us -> none  [per_device(): mine = lax.all_to_all(attended, 'ctx', 0, 0, tiled=True)]
    another operation x6 -> x1, other arithmetic: 5.73 us -> 1.6 us  [per_device(): line = jnp.stack([own] + [fetch(own, step, True) for step in NEAR[1:]])]
  transfers between devices with their start and end apart: 22 -> 9, of which waited for: 10 -> 8; matrix products, arithmetic and copies ran while one was open for 5% -> 4% of each run, Pallas kernels for 5% -> 7%
where the time goes in v4:
time: 92.7 us; the launch traced here: 91.1 us
  waiting for transfers between devices  28.2 us (30%)
  blocking collectives  21.4 us (23%)
  starting transfers between devices  21.1 us (23%)
  Pallas kernels  16.4 us (18%)
  other arithmetic  3.67 us (4%)
    all_to_all x1, blocking collectives, per_device(): mine = lax.all_to_all(attended, 'ctx', 0, 0, tiled=True)  21.4 us
    ppermute x6, waiting for transfers between devices, fetch(): return lax.ppermute(piece, ('fsdp', 'ctx'), pairs)  13.1 us
    all_to_all x1, waiting for transfers between devices, per_device(): lax.all_to_all(pack(queries, keys, values), 'ctx', 0, 0, tiled=True)  12.9 us
    all_to_all x1, starting transfers between devices, per_device(): lax.all_to_all(pack(queries, keys, values), 'ctx', 0, 0, tiled=True)  9.98 us
    ppermute x6, starting transfers between devices, fetch(): return lax.ppermute(piece, ('fsdp', 'ctx'), pairs)  9.88 us
    pallas_call x1, Pallas kernels, head_attention(): pl.pallas_call(attention_kernel, out_shape=jax.ShapeDtypeStruct((blocks,...  6.69 us
    pallas_call x1, Pallas kernels, project(): pl.pallas_call(projection_kernel, out_shape=(jax.ShapeDtypeStruct((rows,...  5.71 us
    pallas_call x1, Pallas kernels, pack(): pl.pallas_call(pack_kernel, out_shape=jax.ShapeDtypeStruct((heads, 3, row...  2.54 us
  transfers between devices with their start and end apart: 9, of which 8 were waited for; matrix products, arithmetic and copies ran while one was open for 4% of the time, Pallas kernels for 7%

profile of v4, /device:TPU:1, one launch (start us, length us, event | category | flops | bytes accessed | tf_op | source)
XLA Modules:
  0.0 91.1 jit_solution(8958754683736027631)
XLA Ops:
  0.0 0.0 copy-start
  0.0 2.5 %pack.1 = bf16[16,3,128,128]{3,2,1,0:T(8,128)(2,1)} custom-call(bf16[128,2048]{1,0:T(8,128)(2,1)} %queries_ref.1, bf16[128,2048]{1,0:T(8,128)(2,1)} %keys_ref.1, bf16[128,2048]{1,0:T(8,128)(2,1)} %values_ref.1), custom_call_target="tpu_custom_call" | custom-call | tf_op jit(solution)/shard_map/pack/pallas_call | solution.py:101
  2.5 10.0 %all-to-all-start = ((bf16[16,3,128,128]{3,2,1,0:T(8,128)(2,1)}), bf16[16,3,128,128]{3,2,1,0:T(8,128)(2,1)S(1)}, u32[]{:S(2)}, u32[]{:S(2)}) async-start(bf16[16,3,128,128]{3,2,1,0:T(8,128)(2,1)} %pack.1), calls=%async_computation | async-start | bytes 3145728 | tf_op jit(solution)/shard_map/all_to_all | solution.py:240
  12.5 0.0 copy-done
  12.6 1.4 %collective-permute-start.1 = (bf16[128,2048]{1,0:T(8,128)(2,1)S(1)}, bf16[128,2048]{1,0:T(8,128)(2,1)S(1)}, u32[]{:S(2)}, u32[]{:S(2)}) collective-permute-start(bf16[128,2048]{1,0:T(8,128)(2,1)S(1)} %constant_dynamic-slice_fusion), channel_id=1, source_target_pairs={{48,0},{193,1},{50,2},{195,3},{52,4},{197,5},{54,6},{199,7},{56,8}... | collective-permute-start | bytes 1572872 | tf_op jit(solution)/shard_map/ppermute | solution.py:230
  14.0 1.5 %collective-permute-start = (bf16[128,2048]{1,0:T(8,128)(2,1)S(1)}, bf16[128,2048]{1,0:T(8,128)(2,1)S(1)}, u32[]{:S(2)}, u32[]{:S(2)}) collective-permute-start(bf16[128,2048]{1,0:T(8,128)(2,1)S(1)} %constant_dynamic-slice_fusion), channel_id=1, source_target_pairs={{16,0},{65,1},{18,2},{67,3},{20,4},{69,5},{22,6},{71,7},{24,8},{73... | collective-permute-start | bytes 1572872 | tf_op jit(solution)/shard_map/ppermute | solution.py:230
  15.5 1.6 %collective-permute-start.2 = (bf16[128,2048]{1,0:T(8,128)(2,1)S(1)}, bf16[128,2048]{1,0:T(8,128)(2,1)S(1)}, u32[]{:S(2)}, u32[]{:S(2)}) collective-permute-start(bf16[128,2048]{1,0:T(8,128)(2,1)S(1)} %constant_dynamic-slice_fusion), channel_id=1, source_target_pairs={{32,0},{129,1},{34,2},{131,3},{36,4},{133,5},{38,6},{135,7},{40,8}... | collective-permute-start | bytes 1572872 | tf_op jit(solution)/shard_map/ppermute | solution.py:230
  17.1 5.2 %collective-permute-done.1 = bf16[128,2048]{1,0:T(8,128)(2,1)S(1)} collective-permute-done((bf16[128,2048]{1,0:T(8,128)(2,1)S(1)}, bf16[128,2048]{1,0:T(8,128)(2,1)S(1)}, u32[]{:S(2)}, u32[]{:S(2)}) %collective-permute-start.1) | collective-permute-done | bytes 524320 | tf_op jit(solution)/shard_map/ppermute | solution.py:230
  22.3 5.0 %collective-permute-done = bf16[128,2048]{1,0:T(8,128)(2,1)S(1)} collective-permute-done((bf16[128,2048]{1,0:T(8,128)(2,1)S(1)}, bf16[128,2048]{1,0:T(8,128)(2,1)S(1)}, u32[]{:S(2)}, u32[]{:S(2)}) %collective-permute-start) | collective-permute-done | bytes 524320 | tf_op jit(solution)/shard_map/ppermute | solution.py:230
  27.2 1.8 %collective-permute-done.2 = bf16[128,2048]{1,0:T(8,128)(2,1)S(1)} collective-permute-done((bf16[128,2048]{1,0:T(8,128)(2,1)S(1)}, bf16[128,2048]{1,0:T(8,128)(2,1)S(1)}, u32[]{:S(2)}, u32[]{:S(2)}) %collective-permute-start.2) | collective-permute-done | bytes 524320 | tf_op jit(solution)/shard_map/ppermute | solution.py:230
  29.1 0.0 copy-start.2
  29.1 1.6 %pad_maximum_fusion.rest_0_ = bf16[4,128,2048]{2,1,0:T(8,128)(2,1)} fusion(bf16[1,128,2048]{2,1,0:T(8,128)(2,1)S(1)} %bitcast.12, bf16[1,128,2048]{2,1,0:T(8,128)(2,1)S(1)} %bitcast.10, bf16[1,128,2048]{2,1,0:T(8,128)(2,1)S(1)} %bitcast.11, bf16[1,128,2048]{2,1,0:T(8,128)(2,1)S(1)} %fusion.2), kind=kLoop, calls=%fused_computation | loop fusion | flops 3145728 | bytes 4194304 | tf_op jit(solution)/shard_map/stack | solution.py:244
  30.7 2.7 %collective-permute-start.6 = (bf16[4,128,2048]{2,1,0:T(8,128)(2,1)}, bf16[4,128,2048]{2,1,0:T(8,128)(2,1)}, u32[]{:S(2)}, u32[]{:S(2)}) collective-permute-start(bf16[4,128,2048]{2,1,0:T(8,128)(2,1)} %pad_maximum_fusion.rest_0_), channel_id=1, source_target_pairs={{128,0},{33,1},{130,2},{35,3},{132,4},{37,5},{134,6},{39,7},{136,8... | collective-permute-start | bytes 6291464 | tf_op jit(solution)/shard_map/ppermute | solution.py:230
  33.4 0.3 collective-permute-start.5
  33.7 2.4 %collective-permute-start.4 = (bf16[4,128,2048]{2,1,0:T(8,128)(2,1)}, bf16[4,128,2048]{2,1,0:T(8,128)(2,1)}, u32[]{:S(2)}, u32[]{:S(2)}) collective-permute-start(bf16[4,128,2048]{2,1,0:T(8,128)(2,1)} %pad_maximum_fusion.rest_0_), channel_id=1, source_target_pairs={{64,0},{17,1},{66,2},{19,3},{68,4},{21,5},{70,6},{23,7},{72,8},{25... | collective-permute-start | bytes 6291464 | tf_op jit(solution)/shard_map/ppermute | solution.py:230
  36.1 0.0 copy-done.2
  36.1 0.7 fusion
  36.8 1.3 %pad_add_fusion.1.bounds_ref = s32[2]{0:T(128)S(1)} fusion(s32[1]{0:T(128)} %bitcast.4, s32[1]{0:T(128)} %bitcast.3), kind=kLoop, calls=%fused_computation.6 | loop fusion | flops 2 | bytes 16 | tf_op jit(solution)/shard_map/stack | solution.py:236
  38.1 12.9 %all-to-all-done.packed_ref = bf16[16,3,128,128]{3,2,1,0:T(8,128)(2,1)S(1)} async-done(((bf16[16,3,128,128]{3,2,1,0:T(8,128)(2,1)}), bf16[16,3,128,128]{3,2,1,0:T(8,128)(2,1)S(1)}, u32[]{:S(2)}, u32[]{:S(2)}) %all-to-all-start) | async-done | bytes 1572896 | tf_op jit(solution)/shard_map/all_to_all | solution.py:240
  51.0 6.7 %head_attention.1 = bf16[16,128,128]{2,1,0:T(8,128)(2,1)S(1)} custom-call(s32[2]{0:T(128)S(1)} %pad_add_fusion.1.bounds_ref, bf16[16,3,128,128]{3,2,1,0:T(8,128)(2,1)S(1)} %all-to-all-done.packed_ref), custom_call_target="tpu_custom_call" | custom-call | tf_op jit(solution)/shard_map/head_attention/pallas_call | solution.py:114
  57.7 21.4 %all_to_all.10.mine_ref = bf16[16,128,128]{2,1,0:T(8,128)(2,1)S(1)} all-to-all(bf16[16,128,128]{2,1,0:T(8,128)(2,1)S(1)} %head_attention.1), channel_id=1, replica_groups=mesh['fsdp'=16,'ctx'=16] {'ctx'}, dimensions={0} | all-to-all | bytes 1048576 | tf_op jit(solution)/shard_map/all_to_all | solution.py:249
  79.0 0.0 collective-permute-start.3
  79.0 0.1 pad_add_fusion.place_ref
  79.1 0.0 copy-start.1
  79.1 0.0 collective-permute-done.6.rest_3_
  79.1 1.0 %collective-permute-done.5.rest_2_ = bf16[4,128,2048]{2,1,0:T(8,128)(2,1)} collective-permute-done((bf16[4,128,2048]{2,1,0:T(8,128)(2,1)}, bf16[4,128,2048]{2,1,0:T(8,128)(2,1)}, u32[]{:S(2)}, u32[]{:S(2)}) %collective-permute-start.5) | collective-permute-done | bytes 2097184 | tf_op jit(solution)/shard_map/ppermute | solution.py:230
  80.1 0.1 collective-permute-done.4.rest_1_
  80.3 0.7 collective-permute-done.3.theirs_ref
  80.9 5.7 %project.1 = (bf16[128,4096]{1,0:T(8,128)(2,1)}, bf16[128,2048]{1,0:T(8,128)(2,1)S(1)}) custom-call(s32[3]{0:T(128)S(1)} %pad_add_fusion.place_ref, bf16[16,128,128]{2,1,0:T(8,128)(2,1)S(1)} %all_to_all.10.mine_ref, bf16[16,128,128]{2,1,0:T(8,128)(2,1)S(1)} %collective-permute-done.3.theirs_ref, bf16[4,128,2048]{2,1,0:T(8,128)(2,1)} %pad_maximum_fusion.rest_0_, ...), custom_call_target="tpu_custom_call" | custom-call | tf_op jit(solution)/shard_map/project/pallas_call | solution.py:177
  86.7 0.0 copy-done.1
  86.7 1.2 %collective-permute-start.7 = (bf16[128,2048]{1,0:T(8,128)(2,1)S(1)}, bf16[128,2048]{1,0:T(8,128)(2,1)S(1)}, u32[]{:S(2)}, u32[]{:S(2)}) collective-permute-start(bf16[128,2048]{1,0:T(8,128)(2,1)S(1)} %get-tuple-element.9), channel_id=1, source_target_pairs={{0,1},{1,0},{2,3},{3,2},{4,5},{5,4},{6,7},{7,6},{8,9},{9,8},{10,11... | collective-permute-start | bytes 1572872 | tf_op jit(solution)/shard_map/ppermute | solution.py:252
  87.9 1.5 %collective-permute-done.7.got_ref = bf16[128,2048]{1,0:T(8,128)(2,1)S(1)} collective-permute-done((bf16[128,2048]{1,0:T(8,128)(2,1)S(1)}, bf16[128,2048]{1,0:T(8,128)(2,1)S(1)}, u32[]{:S(2)}, u32[]{:S(2)}) %collective-permute-start.7) | collective-permute-done | bytes 524320 | tf_op jit(solution)/shard_map/ppermute | solution.py:252
  89.4 1.5 %join.1 = bf16[128,4096]{1,0:T(8,128)(2,1)} custom-call(s32[3]{0:T(128)} %copy-done.1, bf16[128,2048]{1,0:T(8,128)(2,1)S(1)} %collective-permute-done.7.got_ref, bf16[128,4096]{1,0:T(8,128)(2,1)} %get-tuple-element.10.part_ref), custom_call_target="tpu_custom_call", output_to_operand_aliasing={{}: (2, {})} | custom-call | tf_op jit(solution)/shard_map/join/pallas_call | solution.py:207
  (2 shorter events, 0.1 us)
Async XLA Ops:
  0.0 12.5 %copy-start = (bf16[128,4096]{1,0:T(8,128)(2,1)S(1)}, bf16[128,4096]{1,0:T(8,128)(2,1)}, u32[]{:S(2)}) copy-start(bf16[128,4096]{1,0:T(8,128)(2,1)} %param.8) | copy-start | bytes 3145732
  2.5 48.4 %all-to-all-start = ((bf16[16,3,128,128]{3,2,1,0:T(8,128)(2,1)}), bf16[16,3,128,128]{3,2,1,0:T(8,128)(2,1)S(1)}, u32[]{:S(2)}, u32[]{:S(2)}) async-start(bf16[16,3,128,128]{3,2,1,0:T(8,128)(2,1)} %pack.1), calls=%async_computation | async-start | bytes 3145728 | tf_op jit(solution)/shard_map/all_to_all | solution.py:240
  12.6 9.7 %collective-permute-start.1 = (bf16[128,2048]{1,0:T(8,128)(2,1)S(1)}, bf16[128,2048]{1,0:T(8,128)(2,1)S(1)}, u32[]{:S(2)}, u32[]{:S(2)}) collective-permute-start(bf16[128,2048]{1,0:T(8,128)(2,1)S(1)} %constant_dynamic-slice_fusion), channel_id=1, source_target_pairs={{48,0},{193,1},{50,2},{195,3},{52,4},{197,5},{54,6},{199,7},{56,8}... | collective-permute-start | bytes 1572872 | tf_op jit(solution)/shard_map/ppermute | solution.py:230
  14.0 13.3 %collective-permute-start = (bf16[128,2048]{1,0:T(8,128)(2,1)S(1)}, bf16[128,2048]{1,0:T(8,128)(2,1)S(1)}, u32[]{:S(2)}, u32[]{:S(2)}) collective-permute-start(bf16[128,2048]{1,0:T(8,128)(2,1)S(1)} %constant_dynamic-slice_fusion), channel_id=1, source_target_pairs={{16,0},{65,1},{18,2},{67,3},{20,4},{69,5},{22,6},{71,7},{24,8},{73... | collective-permute-start | bytes 1572872 | tf_op jit(solution)/shard_map/ppermute | solution.py:230
  15.5 13.6 %collective-permute-start.2 = (bf16[128,2048]{1,0:T(8,128)(2,1)S(1)}, bf16[128,2048]{1,0:T(8,128)(2,1)S(1)}, u32[]{:S(2)}, u32[]{:S(2)}) collective-permute-start(bf16[128,2048]{1,0:T(8,128)(2,1)S(1)} %constant_dynamic-slice_fusion), channel_id=1, source_target_pairs={{32,0},{129,1},{34,2},{131,3},{36,4},{133,5},{38,6},{135,7},{40,8}... | collective-permute-start | bytes 1572872 | tf_op jit(solution)/shard_map/ppermute | solution.py:230
  29.1 7.0 %copy-start.2 = (s32[1,2048]{1,0:T(1,128)S(1)}, s32[1,2048]{1,0:T(1,128)}, u32[]{:S(2)}) copy-start(s32[1,2048]{1,0:T(1,128)} %param.9) | copy-start | bytes 24580
  30.7 48.5 %collective-permute-start.6 = (bf16[4,128,2048]{2,1,0:T(8,128)(2,1)}, bf16[4,128,2048]{2,1,0:T(8,128)(2,1)}, u32[]{:S(2)}, u32[]{:S(2)}) collective-permute-start(bf16[4,128,2048]{2,1,0:T(8,128)(2,1)} %pad_maximum_fusion.rest_0_), channel_id=1, source_target_pairs={{128,0},{33,1},{130,2},{35,3},{132,4},{37,5},{134,6},{39,7},{136,8... | collective-permute-start | bytes 6291464 | tf_op jit(solution)/shard_map/ppermute | solution.py:230
  33.4 46.7 %collective-permute-start.5 = (bf16[4,128,2048]{2,1,0:T(8,128)(2,1)}, bf16[4,128,2048]{2,1,0:T(8,128)(2,1)}, u32[]{:S(2)}, u32[]{:S(2)}) collective-permute-start(bf16[4,128,2048]{2,1,0:T(8,128)(2,1)} %pad_maximum_fusion.rest_0_), channel_id=1, source_target_pairs={{192,0},{49,1},{194,2},{51,3},{196,4},{53,5},{198,6},{55,7},{200,8... | collective-permute-start | bytes 6291464 | tf_op jit(solution)/shard_map/ppermute | solution.py:230
  33.7 46.5 %collective-permute-start.4 = (bf16[4,128,2048]{2,1,0:T(8,128)(2,1)}, bf16[4,128,2048]{2,1,0:T(8,128)(2,1)}, u32[]{:S(2)}, u32[]{:S(2)}) collective-permute-start(bf16[4,128,2048]{2,1,0:T(8,128)(2,1)} %pad_maximum_fusion.rest_0_), channel_id=1, source_target_pairs={{64,0},{17,1},{66,2},{19,3},{68,4},{21,5},{70,6},{23,7},{72,8},{25... | collective-permute-start | bytes 6291464 | tf_op jit(solution)/shard_map/ppermute | solution.py:230
  79.0 1.9 %collective-permute-start.3 = (bf16[16,128,128]{2,1,0:T(8,128)(2,1)S(1)}, bf16[16,128,128]{2,1,0:T(8,128)(2,1)S(1)}, u32[]{:S(2)}, u32[]{:S(2)}) collective-permute-start(bf16[16,128,128]{2,1,0:T(8,128)(2,1)S(1)} %all_to_all.10.mine_ref), channel_id=1, source_target_pairs={{0,1},{1,0},{2,3},{3,2},{4,5},{5,4},{6,7},{7,6},{8,9},{9,8},{10,11... | collective-permute-start | bytes 1572872 | tf_op jit(solution)/shard_map/ppermute | solution.py:250
  79.1 7.5 %copy-start.1 = (s32[3]{0:T(128)}, s32[3]{0:T(128)S(1)}, u32[]{:S(2)}) copy-start(s32[3]{0:T(128)S(1)} %pad_add_fusion.place_ref) | copy-start | bytes 40
  86.7 2.8 %collective-permute-start.7 = (bf16[128,2048]{1,0:T(8,128)(2,1)S(1)}, bf16[128,2048]{1,0:T(8,128)(2,1)S(1)}, u32[]{:S(2)}, u32[]{:S(2)}) collective-permute-start(bf16[128,2048]{1,0:T(8,128)(2,1)S(1)} %get-tuple-element.9), channel_id=1, source_target_pairs={{0,1},{1,0},{2,3},{3,2},{4,5},{5,4},{6,7},{7,6},{8,9},{9,8},{10,11... | collective-permute-start | bytes 1572872 | tf_op jit(solution)/shard_map/ppermute | solution.py:252

commit v5 on v4

--- a/solution.py
+++ b/solution.py
@@ -1,3 +1,4 @@
+import functools
 import math
 
 import jax
@@ -9,10 +10,9 @@
 
 HDIM = 128
 TILE = 512
-CHAIN = 256
+CHAIN = 512
 MASKED = -1e30
 SIDE = 4
-NEAR = (0, 1, 3, 2)
 STRIP = 512
 
 
@@ -122,37 +122,36 @@
     )(bounds, packed)
 
 
-def projection_kernel(place_ref, mine_ref, theirs_ref, *rest):
-    pieces = rest[:SIDE]
-    out_ref, sent_ref, kept_ref, left_ref, weight_ref, weight_semaphores, semaphores = rest[SIDE:]
-    columns = pieces[0].shape[2]
+def projection_kernel(places, place_ref, mine_ref, theirs_ref, *rest):
+    pieces = rest[:-7]
+    out_ref, sent_ref, kept_ref, left_ref, weight_ref, weight_semaphores, semaphores = rest[-7:]
+    columns = sent_ref.shape[1]
     rows = mine_ref.shape[1]
-    depth = SIDE * HDIM
     loads = []
     for strip in range(columns // STRIP):
+        at = 0
         for i, piece in enumerate(pieces):
+            count = piece.shape[0]
             source = piece.at[:, :, strip * STRIP:(strip + 1) * STRIP]
-            loads.append(
-                pltpu.make_async_copy(source, weight_ref.at[strip, i], weight_semaphores.at[strip, i])
-            )
+            target = weight_ref.at[strip, pl.ds(at, count)]
+            loads.append(pltpu.make_async_copy(source, target, weight_semaphores.at[strip, i]))
             loads[-1].start()
+            at += count
     y, x, core = place_ref[0], place_ref[1], place_ref[2]
-    for i, far in enumerate(NEAR):
-        for j, near in enumerate(NEAR):
-            dy = jnp.where(core == 0, far, near)
-            dx = jnp.where(core == 0, near, far)
-            head = ((y + dy) % SIDE) * SIDE + (x + dx) % SIDE
-            at = slice(i * depth + j * HDIM, i * depth + (j + 1) * HDIM)
-            left_ref[:rows, at] = mine_ref[head]
-            left_ref[rows:, at] = theirs_ref[head]
+    for i, (far, near) in enumerate(places):
+        dy = jnp.where(core == 0, far, near)
+        dx = jnp.where(core == 0, near, far)
+        head = ((y + dy) % SIDE) * SIDE + (x + dx) % SIDE
+        left_ref[:rows, i * HDIM:(i + 1) * HDIM] = mine_ref[head]
+        left_ref[rows:, i * HDIM:(i + 1) * HDIM] = theirs_ref[head]
     copies = []
     for strip in range(columns // STRIP):
         at = slice(strip * STRIP, (strip + 1) * STRIP)
-        for load in loads[strip * SIDE:(strip + 1) * SIDE]:
+        for load in loads[strip * len(pieces):(strip + 1) * len(pieces)]:
             load.wait()
         result = jnp.dot(
             left_ref[...],
-            weight_ref[strip].reshape(SIDE * depth, STRIP),
+            weight_ref[strip].reshape(len(places) * HDIM, STRIP),
             preferred_element_type=jnp.float32,
         ).astype(jnp.bfloat16)
         sent_ref[:, at] = result[rows:]
@@ -168,51 +167,31 @@
         copy.wait()
 
 
-def project(place, mine, theirs, pieces):
+def project(place, mine, theirs, pieces, places):
     heads, rows, _ = mine.shape
     columns = pieces[0].shape[2]
+    strips = columns // STRIP
     vmem = pl.BlockSpec(memory_space=pltpu.VMEM)
     hbm = pl.BlockSpec(memory_space=pltpu.HBM)
     pieces = [pltpu.with_memory_space_constraint(piece, pltpu.HBM) for piece in pieces]
     return pl.pallas_call(
-        projection_kernel,
+        functools.partial(projection_kernel, places),
         out_shape=(
             jax.ShapeDtypeStruct((rows, 2 * columns), jnp.bfloat16),
             jax.ShapeDtypeStruct((rows, columns), jnp.bfloat16),
         ),
-        in_specs=[pl.BlockSpec(memory_space=pltpu.SMEM), vmem, vmem] + [hbm] * SIDE,
+        in_specs=[pl.BlockSpec(memory_space=pltpu.SMEM), vmem, vmem] + [hbm] * len(pieces),
         out_specs=(hbm, vmem),
         scratch_shapes=[
-            pltpu.VMEM((columns // STRIP, rows, STRIP), jnp.bfloat16),
+            pltpu.VMEM((strips, rows, STRIP), jnp.bfloat16),
             pltpu.VMEM((2 * rows, heads * HDIM), jnp.bfloat16),
-            pltpu.VMEM((columns // STRIP, SIDE, SIDE, HDIM, STRIP), jnp.bfloat16),
-            pltpu.SemaphoreType.DMA((columns // STRIP, SIDE)),
-            pltpu.SemaphoreType.DMA((columns // STRIP,)),
+            pltpu.VMEM((strips, heads, HDIM, STRIP), jnp.bfloat16),
+            pltpu.SemaphoreType.DMA((strips, len(pieces))),
+            pltpu.SemaphoreType.DMA((strips,)),
         ],
         compiler_params=pltpu.CompilerParams(vmem_limit_bytes=20 << 20),
         name="project",
     )(place, mine, theirs, *pieces)
-
-
-def join_kernel(place_ref, got_ref, part_ref, out_ref, semaphore):
-    half = got_ref.shape[1]
-    other = pl.multiple_of((1 - place_ref[2]) * half, half)
-    copy = pltpu.make_async_copy(got_ref, out_ref.at[:, pl.ds(other, half)], semaphore)
-    copy.start()
-    copy.wait()
-
-
-def join(place, got, part):
-    hbm = pl.BlockSpec(memory_space=pltpu.HBM)
-    return pl.pallas_call(
-        join_kernel,
-        out_shape=jax.ShapeDtypeStruct(part.shape, part.dtype),
-        in_specs=[pl.BlockSpec(memory_space=pltpu.SMEM), pl.BlockSpec(memory_space=pltpu.VMEM), hbm],
-        out_specs=hbm,
-        input_output_aliases={2: 0},
-        scratch_shapes=[pltpu.SemaphoreType.DMA],
-        name="join",
-    )(place, pltpu.with_memory_space_constraint(got, pltpu.VMEM), part)
 
 
 def fetch(piece, step, near):
@@ -241,16 +220,23 @@
 
     half = out_weight.shape[1] // 2
     own = lax.dynamic_slice_in_dim(out_weight, core * half, half, 1)
-    line = jnp.stack([own] + [fetch(own, step, True) for step in NEAR[1:]])
-    packed, _ = lax.optimization_barrier((packed, line))
-    pieces = [line] + [fetch(line, step, False) for step in NEAR[1:]]
+    low = jnp.stack([own, fetch(own, 1, True)])
+    high = jnp.stack([fetch(own, -1, True), fetch(own, 2, True)])
+    after = fetch(low, 1, False)
+    before = fetch(high, -1, False)
+    right = fetch(jnp.concatenate([high, after]), 1, False)
+    left = fetch(jnp.concatenate([low, before]), -1, False)
+    pieces = [low, high, after, before, right, left]
+    places = [(0, 0), (0, 1), (0, 3), (0, 2), (1, 0), (1, 1), (3, 3), (3, 2)]
+    places += [(1, 3), (1, 2), (2, 0), (2, 1), (3, 0), (3, 1), (2, 3), (2, 2)]
+    packed, *_ = lax.optimization_barrier((packed, after, before))
 
     attended = head_attention(bounds, packed)
     mine = lax.all_to_all(attended, "ctx", 0, 0, tiled=True)
     theirs = lax.ppermute(mine, "ctx", swap)
-    part, sent = project(place, mine, theirs, pieces)
+    part, sent = project(place, mine, theirs, pieces, places)
     got = lax.ppermute(sent, "ctx", swap)
-    return join(place, got, part)
+    return lax.dynamic_update_slice(part, got, (0, (1 - core) * half))
 
 
 def solution(mesh):

time: 92.7 us -> 96.3 us (1.039); the launches traced: 91.1 us -> 96.1 us
  local copies, waits for them, and re-layouts: 0.09 us -> 3.91 us
  other arithmetic: 3.67 us -> 5.64 us
  blocking collectives: 21.4 us -> 22.7 us
  starting transfers between devices: 21.1 us -> 19.9 us
  Pallas kernels: 16.4 us -> 15.4 us
    all_to_all x1, waiting for transfers between devices: 12.9 us -> 3.73 us  [per_device(): lax.all_to_all(pack(queries, keys, values), 'ctx', 0, 0, tiled=True)]
    ppermute x6 -> x7, waiting for transfers between devices: 13.1 us -> 21.1 us  [fetch(): return lax.ppermute(piece, ('fsdp', 'ctx'), pairs)]
    concatenate x0 -> x2, other arithmetic: none -> 3.37 us  [the longest x1 1.69 us: per_device(): left = fetch(jnp.concatenate([low, before]), -1, False)]
    unnamed x6 -> x12, local copies, waits for them, and re-layouts: 0.01 us -> 2.21 us
    another operation x1 -> x2, other arithmetic: 1.6 us -> 0.2 us  [the longest x1 0.1 us: per_device(): low = jnp.stack([own, fetch(own, 1, True)])]
    pallas_call x2 -> x1, Pallas kernels: 7.18 us -> 5.79 us  [project(): pl.pallas_call(functools.partial(projection_kernel, places), out_shape=(j...]
    all_to_all x1, blocking collectives: 21.4 us -> 22.7 us  [per_device(): mine = lax.all_to_all(attended, 'ctx', 0, 0, tiled=True)]
    ppermute x1, waiting for transfers between devices: 0.68 us -> 1.83 us  [per_device(): theirs = lax.ppermute(mine, 'ctx', swap)]
  transfers between devices with their start and end apart: 9 -> 10, of which waited for: 8 -> 7; matrix products, arithmetic and copies ran while one was open for 4% -> 6% of each run, Pallas kernels for 7% -> 10%
where the time goes in v5:
time: 96.3 us; the launch traced here: 96.1 us
  waiting for transfers between devices  28.4 us (29%)
  blocking collectives  22.7 us (24%)
  starting transfers between devices  19.9 us (21%)
  Pallas kernels  15.4 us (16%)
  other arithmetic  5.64 us (6%)
  local copies, waits for them, and re-layouts  3.91 us (4%)
    all_to_all x1, blocking collectives, per_device(): mine = lax.all_to_all(attended, 'ctx', 0, 0, tiled=True)  22.7 us
    ppermute x7, waiting for transfers between devices, fetch(): return lax.ppermute(piece, ('fsdp', 'ctx'), pairs)  21.1 us
    ppermute x7, starting transfers between devices, fetch(): return lax.ppermute(piece, ('fsdp', 'ctx'), pairs)  10.5 us
    all_to_all x1, starting transfers between devices, per_device(): lax.all_to_all(pack(queries, keys, values), 'ctx', 0, 0, tiled=True)  9.18 us
    pallas_call x1, Pallas kernels, head_attention(): pl.pallas_call(attention_kernel, out_shape=jax.ShapeDtypeStruct((blocks,...  7.17 us
    pallas_call x1, Pallas kernels, project(): pl.pallas_call(functools.partial(projection_kernel, places), out_shape=(j...  5.79 us
    all_to_all x1, waiting for transfers between devices, per_device(): lax.all_to_all(pack(queries, keys, values), 'ctx', 0, 0, tiled=True)  3.73 us
    pallas_call x1, Pallas kernels, pack(): pl.pallas_call(pack_kernel, out_shape=jax.ShapeDtypeStruct((heads, 3, row...  2.45 us
  transfers between devices with their start and end apart: 10, of which 7 were waited for; matrix products, arithmetic and copies ran while one was open for 6% of the time, Pallas kernels for 10%

profile of v5, /device:TPU:1, one launch (start us, length us, event | category | flops | bytes accessed | tf_op | source)
XLA Modules:
  0.0 96.1 jit_solution(4396415393855319582)
XLA Ops:
  0.0 0.0 copy-start
  0.0 1.2 %copy-done = bf16[128,4096]{1,0:T(8,128)(2,1)S(1)} copy-done((bf16[128,4096]{1,0:T(8,128)(2,1)S(1)}, bf16[128,4096]{1,0:T(8,128)(2,1)}, u32[]{:S(2)}) %copy-start) | copy-done | bytes 1048600
  1.2 0.8 constant_dynamic-slice_fusion
  2.1 3.6 %collective-permute-start = (bf16[128,2048]{1,0:T(8,128)(2,1)}, bf16[128,2048]{1,0:T(8,128)(2,1)S(1)}, u32[]{:S(2)}, u32[]{:S(2)}) collective-permute-start(bf16[128,2048]{1,0:T(8,128)(2,1)} %constant_dynamic-slice_fusion), channel_id=1, source_target_pairs={{16,0},{65,1},{18,2},{67,3},{20,4},{69,5},{22,6},{71,7},{24,8},{73... | collective-permute-start | bytes 1572872 | tf_op jit(solution)/shard_map/ppermute | solution.py:209
  5.6 2.4 %pack.1 = bf16[16,3,128,128]{3,2,1,0:T(8,128)(2,1)} custom-call(bf16[128,2048]{1,0:T(8,128)(2,1)} %queries_ref.1, bf16[128,2048]{1,0:T(8,128)(2,1)} %keys_ref.1, bf16[128,2048]{1,0:T(8,128)(2,1)} %values_ref.1), custom_call_target="tpu_custom_call" | custom-call | tf_op jit(solution)/shard_map/pack/pallas_call | solution.py:101
  8.1 9.2 %all-to-all-start = ((bf16[16,3,128,128]{3,2,1,0:T(8,128)(2,1)}), bf16[16,3,128,128]{3,2,1,0:T(8,128)(2,1)S(1)}, u32[]{:S(2)}, u32[]{:S(2)}) async-start(bf16[16,3,128,128]{3,2,1,0:T(8,128)(2,1)} %pack.1), calls=%async_computation | async-start | bytes 3145728 | tf_op jit(solution)/shard_map/all_to_all | solution.py:219
  17.3 2.9 %collective-permute-start.3 = (bf16[128,2048]{1,0:T(8,128)(2,1)}, bf16[128,2048]{1,0:T(8,128)(2,1)S(1)}, u32[]{:S(2)}, u32[]{:S(2)}) collective-permute-start(bf16[128,2048]{1,0:T(8,128)(2,1)} %constant_dynamic-slice_fusion), channel_id=1, source_target_pairs={{32,0},{129,1},{34,2},{131,3},{36,4},{133,5},{38,6},{135,7},{40,8}... | collective-permute-start | bytes 1572872 | tf_op jit(solution)/shard_map/ppermute | solution.py:209
  20.2 0.4 collective-permute-start.2
  20.6 0.0 collective-permute-done
  20.6 0.1 pad_maximum_fusion.2.rest_0_
  20.7 0.0 copy-start.1
  20.7 1.0 %copy-done.1 = bf16[2,128,2048]{2,1,0:T(8,128)(2,1)} copy-done((bf16[2,128,2048]{2,1,0:T(8,128)(2,1)}, bf16[2,128,2048]{2,1,0:T(8,128)(2,1)S(1)}, u32[]{:S(2)}) %copy-start.1) | copy-done | bytes 1048600
  21.7 0.5 collective-permute-start.1
  22.3 5.1 %collective-permute-done.3 = bf16[128,2048]{1,0:T(8,128)(2,1)S(1)} collective-permute-done((bf16[128,2048]{1,0:T(8,128)(2,1)}, bf16[128,2048]{1,0:T(8,128)(2,1)S(1)}, u32[]{:S(2)}, u32[]{:S(2)}) %collective-permute-start.3) | collective-permute-done | bytes 524320 | tf_op jit(solution)/shard_map/ppermute | solution.py:209
  27.3 5.6 %collective-permute-done.2 = bf16[128,2048]{1,0:T(8,128)(2,1)S(1)} collective-permute-done((bf16[128,2048]{1,0:T(8,128)(2,1)}, bf16[128,2048]{1,0:T(8,128)(2,1)S(1)}, u32[]{:S(2)}, u32[]{:S(2)}) %collective-permute-start.2) | collective-permute-done | bytes 524320 | tf_op jit(solution)/shard_map/ppermute | solution.py:209
  32.9 0.1 pad_maximum_fusion.3.rest_1_
  33.0 0.0 copy-start.2
  33.0 0.7 collective-permute-start.4
  33.7 4.9 %collective-permute-done.1.rest_2_ = bf16[2,128,2048]{2,1,0:T(8,128)(2,1)S(1)} collective-permute-done((bf16[2,128,2048]{2,1,0:T(8,128)(2,1)S(1)}, bf16[2,128,2048]{2,1,0:T(8,128)(2,1)S(1)}, u32[]{:S(2)}, u32[]{:S(2)}) %collective-permute-start.1) | collective-permute-done | bytes 1048608 | tf_op jit(solution)/shard_map/ppermute | solution.py:209
  38.7 0.0 copy-start.3
  38.7 1.7 %pad_maximum_fusion = bf16[4,128,2048]{2,1,0:T(8,128)(2,1)} fusion(bf16[2,128,2048]{2,1,0:T(8,128)(2,1)S(1)} %collective-permute-done.1.rest_2_, bf16[1,128,2048]{2,1,0:T(8,128)(2,1)S(1)} %bitcast.13, bf16[1,128,2048]{2,1,0:T(8,128)(2,1)S(1)} %bitcast.15), kind=kLoop, calls=%fused_computation | loop fusion | flops 2097152 | bytes 4194304 | tf_op jit(solution)/shard_map/concatenate | solution.py:227
  40.4 0.0 copy-done.2
  40.4 0.0 copy-done.3
  40.4 0.0 copy-start.5
  40.4 2.4 %collective-permute-start.6 = (bf16[4,128,2048]{2,1,0:T(8,128)(2,1)}, bf16[4,128,2048]{2,1,0:T(8,128)(2,1)}, u32[]{:S(2)}, u32[]{:S(2)}) collective-permute-start(bf16[4,128,2048]{2,1,0:T(8,128)(2,1)} %pad_maximum_fusion), channel_id=1, source_target_pairs={{64,0},{17,1},{66,2},{19,3},{68,4},{21,5},{70,6},{23,7},{72,8},{25... | collective-permute-start | bytes 6291464 | tf_op jit(solution)/shard_map/ppermute | solution.py:209
  42.8 5.5 %collective-permute-done.4.rest_3_ = bf16[2,128,2048]{2,1,0:T(8,128)(2,1)S(1)} collective-permute-done((bf16[2,128,2048]{2,1,0:T(8,128)(2,1)S(1)}, bf16[2,128,2048]{2,1,0:T(8,128)(2,1)S(1)}, u32[]{:S(2)}, u32[]{:S(2)}) %collective-permute-start.4) | collective-permute-done | bytes 1048608 | tf_op jit(solution)/shard_map/ppermute | solution.py:209
  48.3 0.0 copy-start.4
  48.3 1.7 %pad_maximum_fusion.1 = bf16[4,128,2048]{2,1,0:T(8,128)(2,1)} fusion(bf16[2,128,2048]{2,1,0:T(8,128)(2,1)S(1)} %collective-permute-done.4.rest_3_, bf16[1,128,2048]{2,1,0:T(8,128)(2,1)S(1)} %bitcast.11, bf16[1,128,2048]{2,1,0:T(8,128)(2,1)S(1)} %fusion.2), kind=kLoop, calls=%fused_computation.1 | loop fusion | flops 2097152 | bytes 4194304 | tf_op jit(solution)/shard_map/concatenate | solution.py:228
  49.9 0.0 collective-permute-start.7
  50.0 0.0 copy-done.5
  50.0 0.7 fusion
  50.6 0.0 copy-done.4
  50.6 1.3 %pad_add_fusion.1.bounds_ref = s32[2]{0:T(128)S(1)} fusion(s32[1]{0:T(128)} %bitcast.4, s32[1]{0:T(128)} %bitcast.3), kind=kLoop, calls=%fused_computation.9 | loop fusion | flops 2 | bytes 16 | tf_op jit(solution)/shard_map/stack | solution.py:215
  52.0 3.7 %all-to-all-done.packed_ref = bf16[16,3,128,128]{3,2,1,0:T(8,128)(2,1)S(1)} async-done(((bf16[16,3,128,128]{3,2,1,0:T(8,128)(2,1)}), bf16[16,3,128,128]{3,2,1,0:T(8,128)(2,1)S(1)}, u32[]{:S(2)}, u32[]{:S(2)}) %all-to-all-start) | async-done | bytes 1572896 | tf_op jit(solution)/shard_map/all_to_all | solution.py:219
  55.7 7.2 %head_attention.1 = bf16[16,128,128]{2,1,0:T(8,128)(2,1)S(1)} custom-call(s32[2]{0:T(128)S(1)} %pad_add_fusion.1.bounds_ref, bf16[16,3,128,128]{3,2,1,0:T(8,128)(2,1)S(1)} %all-to-all-done.packed_ref), custom_call_target="tpu_custom_call" | custom-call | tf_op jit(solution)/shard_map/head_attention/pallas_call | solution.py:114
  62.9 22.7 %all_to_all.10.mine_ref = bf16[16,128,128]{2,1,0:T(8,128)(2,1)S(1)} all-to-all(bf16[16,128,128]{2,1,0:T(8,128)(2,1)S(1)} %head_attention.1), channel_id=1, replica_groups=mesh['fsdp'=16,'ctx'=16] {'ctx'}, dimensions={0} | all-to-all | bytes 1048576 | tf_op jit(solution)/shard_map/all_to_all | solution.py:235
  85.5 0.0 collective-permute-start.5
  85.6 0.1 pad_add_fusion.place_ref
  85.6 0.0 collective-permute-done.6.rest_4_
  85.6 0.0 collective-permute-done.7.rest_5_
  85.6 1.8 %collective-permute-done.5.theirs_ref = bf16[16,128,128]{2,1,0:T(8,128)(2,1)S(1)} collective-permute-done((bf16[16,128,128]{2,1,0:T(8,128)(2,1)S(1)}, bf16[16,128,128]{2,1,0:T(8,128)(2,1)S(1)}, u32[]{:S(2)}, u32[]{:S(2)}) %collective-permute-start.5) | collective-permute-done | bytes 524320 | tf_op jit(solution)/shard_map/ppermute | solution.py:236
  87.5 5.8 %project.1 = (bf16[128,4096]{1,0:T(8,128)(2,1)}, bf16[128,2048]{1,0:T(8,128)(2,1)S(1)}) custom-call(s32[3]{0:T(128)S(1)} %pad_add_fusion.place_ref, bf16[16,128,128]{2,1,0:T(8,128)(2,1)S(1)} %all_to_all.10.mine_ref, bf16[16,128,128]{2,1,0:T(8,128)(2,1)S(1)} %collective-permute-done.5.theirs_ref, bf16[2,128,2048]{2,1,0:T(8,128)(2,1)} %copy-done.1, ...), custom_call_target="tpu_custom_call" | custom-call | tf_op jit(solution)/shard_map/project/pallas_call | solution.py:177
  93.3 0.2 collective-permute-start.8
  93.5 1.8 %collective-permute-done.8 = bf16[128,2048]{1,0:T(8,128)(2,1)S(1)} collective-permute-done((bf16[128,2048]{1,0:T(8,128)(2,1)S(1)}, bf16[128,2048]{1,0:T(8,128)(2,1)S(1)}, u32[]{:S(2)}, u32[]{:S(2)}) %collective-permute-start.8) | collective-permute-done | bytes 524320 | tf_op jit(solution)/shard_map/ppermute | solution.py:238
  95.3 0.8 constant_dynamic-update-slice_fusion
  (1 shorter events, 0.0 us)
Async XLA Ops:
  0.0 1.2 %copy-start = (bf16[128,4096]{1,0:T(8,128)(2,1)S(1)}, bf16[128,4096]{1,0:T(8,128)(2,1)}, u32[]{:S(2)}) copy-start(bf16[128,4096]{1,0:T(8,128)(2,1)} %param.8) | copy-start | bytes 3145732
  2.1 18.6 %collective-permute-start = (bf16[128,2048]{1,0:T(8,128)(2,1)}, bf16[128,2048]{1,0:T(8,128)(2,1)S(1)}, u32[]{:S(2)}, u32[]{:S(2)}) collective-permute-start(bf16[128,2048]{1,0:T(8,128)(2,1)} %constant_dynamic-slice_fusion), channel_id=1, source_target_pairs={{16,0},{65,1},{18,2},{67,3},{20,4},{69,5},{22,6},{71,7},{24,8},{73... | collective-permute-start | bytes 1572872 | tf_op jit(solution)/shard_map/ppermute | solution.py:209
  8.1 47.6 %all-to-all-start = ((bf16[16,3,128,128]{3,2,1,0:T(8,128)(2,1)}), bf16[16,3,128,128]{3,2,1,0:T(8,128)(2,1)S(1)}, u32[]{:S(2)}, u32[]{:S(2)}) async-start(bf16[16,3,128,128]{3,2,1,0:T(8,128)(2,1)} %pack.1), calls=%async_computation | async-start | bytes 3145728 | tf_op jit(solution)/shard_map/all_to_all | solution.py:219
  17.3 10.1 %collective-permute-start.3 = (bf16[128,2048]{1,0:T(8,128)(2,1)}, bf16[128,2048]{1,0:T(8,128)(2,1)S(1)}, u32[]{:S(2)}, u32[]{:S(2)}) collective-permute-start(bf16[128,2048]{1,0:T(8,128)(2,1)} %constant_dynamic-slice_fusion), channel_id=1, source_target_pairs={{32,0},{129,1},{34,2},{131,3},{36,4},{133,5},{38,6},{135,7},{40,8}... | collective-permute-start | bytes 1572872 | tf_op jit(solution)/shard_map/ppermute | solution.py:209
  20.2 12.7 %collective-permute-start.2 = (bf16[128,2048]{1,0:T(8,128)(2,1)}, bf16[128,2048]{1,0:T(8,128)(2,1)S(1)}, u32[]{:S(2)}, u32[]{:S(2)}) collective-permute-start(bf16[128,2048]{1,0:T(8,128)(2,1)} %constant_dynamic-slice_fusion), channel_id=1, source_target_pairs={{48,0},{193,1},{50,2},{195,3},{52,4},{197,5},{54,6},{199,7},{56,8}... | collective-permute-start | bytes 1572872 | tf_op jit(solution)/shard_map/ppermute | solution.py:209
  20.7 1.0 %copy-start.1 = (bf16[2,128,2048]{2,1,0:T(8,128)(2,1)}, bf16[2,128,2048]{2,1,0:T(8,128)(2,1)S(1)}, u32[]{:S(2)}) copy-start(bf16[2,128,2048]{2,1,0:T(8,128)(2,1)S(1)} %pad_maximum_fusion.2.rest_0_) | copy-start | bytes 3145732
  21.7 17.0 %collective-permute-start.1 = (bf16[2,128,2048]{2,1,0:T(8,128)(2,1)S(1)}, bf16[2,128,2048]{2,1,0:T(8,128)(2,1)S(1)}, u32[]{:S(2)}, u32[]{:S(2)}) collective-permute-start(bf16[2,128,2048]{2,1,0:T(8,128)(2,1)S(1)} %pad_maximum_fusion.2.rest_0_), channel_id=1, source_target_pairs={{64,0},{17,1},{66,2},{19,3},{68,4},{21,5},{70,6},{23,7},{72,8},{25... | collective-permute-start | bytes 3145736 | tf_op jit(solution)/shard_map/ppermute | solution.py:209
  33.0 7.4 %copy-start.2 = (bf16[2,128,2048]{2,1,0:T(8,128)(2,1)}, bf16[2,128,2048]{2,1,0:T(8,128)(2,1)S(1)}, u32[]{:S(2)}) copy-start(bf16[2,128,2048]{2,1,0:T(8,128)(2,1)S(1)} %pad_maximum_fusion.3.rest_1_) | copy-start | bytes 3145732
  33.0 15.2 %collective-permute-start.4 = (bf16[2,128,2048]{2,1,0:T(8,128)(2,1)S(1)}, bf16[2,128,2048]{2,1,0:T(8,128)(2,1)S(1)}, u32[]{:S(2)}, u32[]{:S(2)}) collective-permute-start(bf16[2,128,2048]{2,1,0:T(8,128)(2,1)S(1)} %pad_maximum_fusion.3.rest_1_), channel_id=1, source_target_pairs={{192,0},{49,1},{194,2},{51,3},{196,4},{53,5},{198,6},{55,7},{200,8... | collective-permute-start | bytes 3145736 | tf_op jit(solution)/shard_map/ppermute | solution.py:209
  38.7 1.7 %copy-start.3 = (bf16[2,128,2048]{2,1,0:T(8,128)(2,1)}, bf16[2,128,2048]{2,1,0:T(8,128)(2,1)S(1)}, u32[]{:S(2)}) copy-start(bf16[2,128,2048]{2,1,0:T(8,128)(2,1)S(1)} %collective-permute-done.1.rest_2_) | copy-start | bytes 3145732
  40.4 9.6 %copy-start.5 = (s32[1,2048]{1,0:T(1,128)S(1)}, s32[1,2048]{1,0:T(1,128)}, u32[]{:S(2)}) copy-start(s32[1,2048]{1,0:T(1,128)} %param.9) | copy-start | bytes 24580
  40.4 45.3 %collective-permute-start.6 = (bf16[4,128,2048]{2,1,0:T(8,128)(2,1)}, bf16[4,128,2048]{2,1,0:T(8,128)(2,1)}, u32[]{:S(2)}, u32[]{:S(2)}) collective-permute-start(bf16[4,128,2048]{2,1,0:T(8,128)(2,1)} %pad_maximum_fusion), channel_id=1, source_target_pairs={{64,0},{17,1},{66,2},{19,3},{68,4},{21,5},{70,6},{23,7},{72,8},{25... | collective-permute-start | bytes 6291464 | tf_op jit(solution)/shard_map/ppermute | solution.py:209
  48.3 2.4 %copy-start.4 = (bf16[2,128,2048]{2,1,0:T(8,128)(2,1)}, bf16[2,128,2048]{2,1,0:T(8,128)(2,1)S(1)}, u32[]{:S(2)}) copy-start(bf16[2,128,2048]{2,1,0:T(8,128)(2,1)S(1)} %collective-permute-done.4.rest_3_) | copy-start | bytes 3145732
  49.9 35.7 %collective-permute-start.7 = (bf16[4,128,2048]{2,1,0:T(8,128)(2,1)}, bf16[4,128,2048]{2,1,0:T(8,128)(2,1)}, u32[]{:S(2)}, u32[]{:S(2)}) collective-permute-start(bf16[4,128,2048]{2,1,0:T(8,128)(2,1)} %pad_maximum_fusion.1), channel_id=1, source_target_pairs={{192,0},{49,1},{194,2},{51,3},{196,4},{53,5},{198,6},{55,7},{200,8... | collective-permute-start | bytes 6291464 | tf_op jit(solution)/shard_map/ppermute | solution.py:209
  85.5 1.9 %collective-permute-start.5 = (bf16[16,128,128]{2,1,0:T(8,128)(2,1)S(1)}, bf16[16,128,128]{2,1,0:T(8,128)(2,1)S(1)}, u32[]{:S(2)}, u32[]{:S(2)}) collective-permute-start(bf16[16,128,128]{2,1,0:T(8,128)(2,1)S(1)} %all_to_all.10.mine_ref), channel_id=1, source_target_pairs={{0,1},{1,0},{2,3},{3,2},{4,5},{5,4},{6,7},{7,6},{8,9},{9,8},{10,11... | collective-permute-start | bytes 1572872 | tf_op jit(solution)/shard_map/ppermute | solution.py:236
  93.3 2.0 %collective-permute-start.8 = (bf16[128,2048]{1,0:T(8,128)(2,1)S(1)}, bf16[128,2048]{1,0:T(8,128)(2,1)S(1)}, u32[]{:S(2)}, u32[]{:S(2)}) collective-permute-start(bf16[128,2048]{1,0:T(8,128)(2,1)S(1)} %get-tuple-element.10), channel_id=1, source_target_pairs={{0,1},{1,0},{2,3},{3,2},{4,5},{5,4},{6,7},{7,6},{8,9},{9,8},{10,11... | collective-permute-start | bytes 1572872 | tf_op jit(solution)/shard_map/ppermute | solution.py:238

commit v6 on v5

--- a/solution.py
+++ b/solution.py
@@ -13,6 +13,7 @@
 CHAIN = 512
 MASKED = -1e30
 SIDE = 4
+NEAR = (0, 1, 3, 2)
 STRIP = 512
 
 
@@ -220,17 +221,10 @@
 
     half = out_weight.shape[1] // 2
     own = lax.dynamic_slice_in_dim(out_weight, core * half, half, 1)
-    low = jnp.stack([own, fetch(own, 1, True)])
-    high = jnp.stack([fetch(own, -1, True), fetch(own, 2, True)])
-    after = fetch(low, 1, False)
-    before = fetch(high, -1, False)
-    right = fetch(jnp.concatenate([high, after]), 1, False)
-    left = fetch(jnp.concatenate([low, before]), -1, False)
-    pieces = [low, high, after, before, right, left]
-    places = [(0, 0), (0, 1), (0, 3), (0, 2), (1, 0), (1, 1), (3, 3), (3, 2)]
-    places += [(1, 3), (1, 2), (2, 0), (2, 1), (3, 0), (3, 1), (2, 3), (2, 2)]
-    packed, *_ = lax.optimization_barrier((packed, after, before))
-
+    line = jnp.stack([own] + [fetch(own, step, True) for step in NEAR[1:]])
+    packed, _ = lax.optimization_barrier((packed, line))
+    pieces = [line] + [fetch(line, step, False) for step in NEAR[1:]]
+    places = [(far, near) for far in NEAR for near in NEAR]
     attended = head_attention(bounds, packed)
     mine = lax.all_to_all(attended, "ctx", 0, 0, tiled=True)
     theirs = lax.ppermute(mine, "ctx", swap)

time: 96.3 us -> 90.5 us (0.940)
  local copies, waits for them, and re-layouts: 3.91 us -> 0.91 us
  other arithmetic: 5.64 us -> 3.72 us
  blocking collectives: 22.7 us -> 21.4 us
    all_to_all x1, waiting for transfers between devices: 3.73 us -> 12.8 us  [per_device(): lax.all_to_all(pack(queries, keys, values), 'ctx', 0, 0, tiled=True)]
    ppermute x7 -> x6, waiting for transfers between devices: 21.1 us -> 12.6 us  [fetch(): return lax.ppermute(piece, ('fsdp', 'ctx'), pairs)]
    concatenate x2 -> x0, other arithmetic: 3.37 us -> none  [the longest x1 1.69 us: per_device(): left = fetch(jnp.concatenate([low, before]), -1, False)]
    unnamed x12 -> x4, local copies, waits for them, and re-layouts: 2.21 us -> 0.01 us
    another operation x2 -> x1, other arithmetic: 0.2 us -> 1.61 us  [per_device(): line = jnp.stack([own] + [fetch(own, step, True) for step in NEAR[1:]])]
    all_to_all x1, blocking collectives: 22.7 us -> 21.4 us  [per_device(): mine = lax.all_to_all(attended, 'ctx', 0, 0, tiled=True)]
    ppermute x7 -> x6, starting transfers between devices: 10.5 us -> 9.88 us  [fetch(): return lax.ppermute(piece, ('fsdp', 'ctx'), pairs)]
  transfers between devices with their start and end apart: 10 -> 9, of which waited for: 7 -> 8; matrix products, arithmetic and copies ran while one was open for 6% -> 4% of each run, Pallas kernels for 10% -> 8%
where the time goes in v6:
time: 90.5 us; the launch traced here: 90.3 us
  waiting for transfers between devices  28.2 us (31%)
  blocking collectives  21.4 us (24%)
  starting transfers between devices  20.6 us (23%)
  Pallas kernels  15.4 us (17%)
  other arithmetic  3.72 us (4%)
  local copies, waits for them, and re-layouts  0.91 us (1%)
    all_to_all x1, blocking collectives, per_device(): mine = lax.all_to_all(attended, 'ctx', 0, 0, tiled=True)  21.4 us
    all_to_all x1, waiting for transfers between devices, per_device(): lax.all_to_all(pack(queries, keys, values), 'ctx', 0, 0, tiled=True)  12.8 us
    ppermute x6, waiting for transfers between devices, fetch(): return lax.ppermute(piece, ('fsdp', 'ctx'), pairs)  12.6 us
    all_to_all x1, starting transfers between devices, per_device(): lax.all_to_all(pack(queries, keys, values), 'ctx', 0, 0, tiled=True)  9.98 us
    ppermute x6, starting transfers between devices, fetch(): return lax.ppermute(piece, ('fsdp', 'ctx'), pairs)  9.88 us
    pallas_call x1, Pallas kernels, head_attention(): pl.pallas_call(attention_kernel, out_shape=jax.ShapeDtypeStruct((blocks,...  7.17 us
    pallas_call x1, Pallas kernels, project(): pl.pallas_call(functools.partial(projection_kernel, places), out_shape=(j...  5.71 us
    pallas_call x1, Pallas kernels, pack(): pl.pallas_call(pack_kernel, out_shape=jax.ShapeDtypeStruct((heads, 3, row...  2.55 us
  transfers between devices with their start and end apart: 9, of which 8 were waited for; matrix products, arithmetic and copies ran while one was open for 4% of the time, Pallas kernels for 8%

profile of v6, /device:TPU:1, one launch (start us, length us, event | category | flops | bytes accessed | tf_op | source)
XLA Modules:
  0.0 90.3 jit_solution(1526823399898518353)
XLA Ops:
  0.0 0.0 copy-start
  0.0 2.5 %pack.1 = bf16[16,3,128,128]{3,2,1,0:T(8,128)(2,1)} custom-call(bf16[128,2048]{1,0:T(8,128)(2,1)} %queries_ref.1, bf16[128,2048]{1,0:T(8,128)(2,1)} %keys_ref.1, bf16[128,2048]{1,0:T(8,128)(2,1)} %values_ref.1), custom_call_target="tpu_custom_call" | custom-call | tf_op jit(solution)/shard_map/pack/pallas_call | solution.py:102
  2.5 10.0 %all-to-all-start = ((bf16[16,3,128,128]{3,2,1,0:T(8,128)(2,1)}), bf16[16,3,128,128]{3,2,1,0:T(8,128)(2,1)S(1)}, u32[]{:S(2)}, u32[]{:S(2)}) async-start(bf16[16,3,128,128]{3,2,1,0:T(8,128)(2,1)} %pack.1), calls=%async_computation | async-start | bytes 3145728 | tf_op jit(solution)/shard_map/all_to_all | solution.py:220
  12.5 0.0 copy-done
  12.6 1.4 %collective-permute-start.1 = (bf16[128,2048]{1,0:T(8,128)(2,1)S(1)}, bf16[128,2048]{1,0:T(8,128)(2,1)S(1)}, u32[]{:S(2)}, u32[]{:S(2)}) collective-permute-start(bf16[128,2048]{1,0:T(8,128)(2,1)S(1)} %constant_dynamic-slice_fusion), channel_id=1, source_target_pairs={{48,0},{193,1},{50,2},{195,3},{52,4},{197,5},{54,6},{199,7},{56,8}... | collective-permute-start | bytes 1572872 | tf_op jit(solution)/shard_map/ppermute | solution.py:210
  14.0 1.5 %collective-permute-start = (bf16[128,2048]{1,0:T(8,128)(2,1)S(1)}, bf16[128,2048]{1,0:T(8,128)(2,1)S(1)}, u32[]{:S(2)}, u32[]{:S(2)}) collective-permute-start(bf16[128,2048]{1,0:T(8,128)(2,1)S(1)} %constant_dynamic-slice_fusion), channel_id=1, source_target_pairs={{16,0},{65,1},{18,2},{67,3},{20,4},{69,5},{22,6},{71,7},{24,8},{73... | collective-permute-start | bytes 1572872 | tf_op jit(solution)/shard_map/ppermute | solution.py:210
  15.5 1.6 %collective-permute-start.2 = (bf16[128,2048]{1,0:T(8,128)(2,1)S(1)}, bf16[128,2048]{1,0:T(8,128)(2,1)S(1)}, u32[]{:S(2)}, u32[]{:S(2)}) collective-permute-start(bf16[128,2048]{1,0:T(8,128)(2,1)S(1)} %constant_dynamic-slice_fusion), channel_id=1, source_target_pairs={{32,0},{129,1},{34,2},{131,3},{36,4},{133,5},{38,6},{135,7},{40,8}... | collective-permute-start | bytes 1572872 | tf_op jit(solution)/shard_map/ppermute | solution.py:210
  17.1 5.2 %collective-permute-done.1 = bf16[128,2048]{1,0:T(8,128)(2,1)S(1)} collective-permute-done((bf16[128,2048]{1,0:T(8,128)(2,1)S(1)}, bf16[128,2048]{1,0:T(8,128)(2,1)S(1)}, u32[]{:S(2)}, u32[]{:S(2)}) %collective-permute-start.1) | collective-permute-done | bytes 524320 | tf_op jit(solution)/shard_map/ppermute | solution.py:210
  22.3 5.0 %collective-permute-done = bf16[128,2048]{1,0:T(8,128)(2,1)S(1)} collective-permute-done((bf16[128,2048]{1,0:T(8,128)(2,1)S(1)}, bf16[128,2048]{1,0:T(8,128)(2,1)S(1)}, u32[]{:S(2)}, u32[]{:S(2)}) %collective-permute-start) | collective-permute-done | bytes 524320 | tf_op jit(solution)/shard_map/ppermute | solution.py:210
  27.2 1.8 %collective-permute-done.2 = bf16[128,2048]{1,0:T(8,128)(2,1)S(1)} collective-permute-done((bf16[128,2048]{1,0:T(8,128)(2,1)S(1)}, bf16[128,2048]{1,0:T(8,128)(2,1)S(1)}, u32[]{:S(2)}, u32[]{:S(2)}) %collective-permute-start.2) | collective-permute-done | bytes 524320 | tf_op jit(solution)/shard_map/ppermute | solution.py:210
  29.1 0.0 copy-start.1
  29.1 1.6 %pad_maximum_fusion.rest_0_ = bf16[4,128,2048]{2,1,0:T(8,128)(2,1)} fusion(bf16[1,128,2048]{2,1,0:T(8,128)(2,1)S(1)} %bitcast.12, bf16[1,128,2048]{2,1,0:T(8,128)(2,1)S(1)} %bitcast.10, bf16[1,128,2048]{2,1,0:T(8,128)(2,1)S(1)} %bitcast.11, bf16[1,128,2048]{2,1,0:T(8,128)(2,1)S(1)} %fusion.2), kind=kLoop, calls=%fused_computation | loop fusion | flops 3145728 | bytes 4194304 | tf_op jit(solution)/shard_map/stack | solution.py:224
  30.7 2.7 %collective-permute-start.6 = (bf16[4,128,2048]{2,1,0:T(8,128)(2,1)}, bf16[4,128,2048]{2,1,0:T(8,128)(2,1)}, u32[]{:S(2)}, u32[]{:S(2)}) collective-permute-start(bf16[4,128,2048]{2,1,0:T(8,128)(2,1)} %pad_maximum_fusion.rest_0_), channel_id=1, source_target_pairs={{128,0},{33,1},{130,2},{35,3},{132,4},{37,5},{134,6},{39,7},{136,8... | collective-permute-start | bytes 6291464 | tf_op jit(solution)/shard_map/ppermute | solution.py:210
  33.4 0.3 collective-permute-start.5
  33.7 2.4 %collective-permute-start.4 = (bf16[4,128,2048]{2,1,0:T(8,128)(2,1)}, bf16[4,128,2048]{2,1,0:T(8,128)(2,1)}, u32[]{:S(2)}, u32[]{:S(2)}) collective-permute-start(bf16[4,128,2048]{2,1,0:T(8,128)(2,1)} %pad_maximum_fusion.rest_0_), channel_id=1, source_target_pairs={{64,0},{17,1},{66,2},{19,3},{68,4},{21,5},{70,6},{23,7},{72,8},{25... | collective-permute-start | bytes 6291464 | tf_op jit(solution)/shard_map/ppermute | solution.py:210
  36.1 0.0 copy-done.1
  36.1 0.7 fusion
  36.8 1.4 %pad_add_fusion.1.bounds_ref = s32[2]{0:T(128)S(1)} fusion(s32[1]{0:T(128)} %bitcast.4, s32[1]{0:T(128)} %bitcast.3), kind=kLoop, calls=%fused_computation.6 | loop fusion | flops 2 | bytes 16 | tf_op jit(solution)/shard_map/stack | solution.py:216
  38.1 12.8 %all-to-all-done.packed_ref = bf16[16,3,128,128]{3,2,1,0:T(8,128)(2,1)S(1)} async-done(((bf16[16,3,128,128]{3,2,1,0:T(8,128)(2,1)}), bf16[16,3,128,128]{3,2,1,0:T(8,128)(2,1)S(1)}, u32[]{:S(2)}, u32[]{:S(2)}) %all-to-all-start) | async-done | bytes 1572896 | tf_op jit(solution)/shard_map/all_to_all | solution.py:220
  51.0 7.2 %head_attention.1 = bf16[16,128,128]{2,1,0:T(8,128)(2,1)S(1)} custom-call(s32[2]{0:T(128)S(1)} %pad_add_fusion.1.bounds_ref, bf16[16,3,128,128]{3,2,1,0:T(8,128)(2,1)S(1)} %all-to-all-done.packed_ref), custom_call_target="tpu_custom_call" | custom-call | tf_op jit(solution)/shard_map/head_attention/pallas_call | solution.py:115
  58.1 21.4 %all_to_all.10.mine_ref = bf16[16,128,128]{2,1,0:T(8,128)(2,1)S(1)} all-to-all(bf16[16,128,128]{2,1,0:T(8,128)(2,1)S(1)} %head_attention.1), channel_id=1, replica_groups=mesh['fsdp'=16,'ctx'=16] {'ctx'}, dimensions={0} | all-to-all | bytes 1048576 | tf_op jit(solution)/shard_map/all_to_all | solution.py:229
  79.5 0.0 collective-permute-start.3
  79.5 0.1 pad_add_fusion.place_ref
  79.6 0.0 collective-permute-done.6.rest_3_
  79.6 0.5 collective-permute-done.5.rest_2_
  80.1 0.1 collective-permute-done.4.rest_1_
  80.3 1.2 %collective-permute-done.3.theirs_ref = bf16[16,128,128]{2,1,0:T(8,128)(2,1)S(1)} collective-permute-done((bf16[16,128,128]{2,1,0:T(8,128)(2,1)S(1)}, bf16[16,128,128]{2,1,0:T(8,128)(2,1)S(1)}, u32[]{:S(2)}, u32[]{:S(2)}) %collective-permute-start.3) | collective-permute-done | bytes 524320 | tf_op jit(solution)/shard_map/ppermute | solution.py:230
  81.4 5.7 %project.1 = (bf16[128,4096]{1,0:T(8,128)(2,1)}, bf16[128,2048]{1,0:T(8,128)(2,1)S(1)}) custom-call(s32[3]{0:T(128)S(1)} %pad_add_fusion.place_ref, bf16[16,128,128]{2,1,0:T(8,128)(2,1)S(1)} %all_to_all.10.mine_ref, bf16[16,128,128]{2,1,0:T(8,128)(2,1)S(1)} %collective-permute-done.3.theirs_ref, bf16[4,128,2048]{2,1,0:T(8,128)(2,1)} %pad_maximum_fusion.rest_0_, ...), custom_call_target="tpu_custom_call" | custom-call | tf_op jit(solution)/shard_map/project/pallas_call | solution.py:178
  87.1 0.8 collective-permute-start.7
  87.9 1.5 %collective-permute-done.7 = bf16[128,2048]{1,0:T(8,128)(2,1)S(1)} collective-permute-done((bf16[128,2048]{1,0:T(8,128)(2,1)S(1)}, bf16[128,2048]{1,0:T(8,128)(2,1)S(1)}, u32[]{:S(2)}, u32[]{:S(2)}) %collective-permute-start.7) | collective-permute-done | bytes 524320 | tf_op jit(solution)/shard_map/ppermute | solution.py:232
  89.4 0.8 constant_dynamic-update-slice_fusion
  (2 shorter events, 0.1 us)
Async XLA Ops:
  0.0 12.5 %copy-start = (bf16[128,4096]{1,0:T(8,128)(2,1)S(1)}, bf16[128,4096]{1,0:T(8,128)(2,1)}, u32[]{:S(2)}) copy-start(bf16[128,4096]{1,0:T(8,128)(2,1)} %param.8) | copy-start | bytes 3145732
  2.5 48.4 %all-to-all-start = ((bf16[16,3,128,128]{3,2,1,0:T(8,128)(2,1)}), bf16[16,3,128,128]{3,2,1,0:T(8,128)(2,1)S(1)}, u32[]{:S(2)}, u32[]{:S(2)}) async-start(bf16[16,3,128,128]{3,2,1,0:T(8,128)(2,1)} %pack.1), calls=%async_computation | async-start | bytes 3145728 | tf_op jit(solution)/shard_map/all_to_all | solution.py:220
  12.6 9.7 %collective-permute-start.1 = (bf16[128,2048]{1,0:T(8,128)(2,1)S(1)}, bf16[128,2048]{1,0:T(8,128)(2,1)S(1)}, u32[]{:S(2)}, u32[]{:S(2)}) collective-permute-start(bf16[128,2048]{1,0:T(8,128)(2,1)S(1)} %constant_dynamic-slice_fusion), channel_id=1, source_target_pairs={{48,0},{193,1},{50,2},{195,3},{52,4},{197,5},{54,6},{199,7},{56,8}... | collective-permute-start | bytes 1572872 | tf_op jit(solution)/shard_map/ppermute | solution.py:210
  14.0 13.3 %collective-permute-start = (bf16[128,2048]{1,0:T(8,128)(2,1)S(1)}, bf16[128,2048]{1,0:T(8,128)(2,1)S(1)}, u32[]{:S(2)}, u32[]{:S(2)}) collective-permute-start(bf16[128,2048]{1,0:T(8,128)(2,1)S(1)} %constant_dynamic-slice_fusion), channel_id=1, source_target_pairs={{16,0},{65,1},{18,2},{67,3},{20,4},{69,5},{22,6},{71,7},{24,8},{73... | collective-permute-start | bytes 1572872 | tf_op jit(solution)/shard_map/ppermute | solution.py:210
  15.5 13.6 %collective-permute-start.2 = (bf16[128,2048]{1,0:T(8,128)(2,1)S(1)}, bf16[128,2048]{1,0:T(8,128)(2,1)S(1)}, u32[]{:S(2)}, u32[]{:S(2)}) collective-permute-start(bf16[128,2048]{1,0:T(8,128)(2,1)S(1)} %constant_dynamic-slice_fusion), channel_id=1, source_target_pairs={{32,0},{129,1},{34,2},{131,3},{36,4},{133,5},{38,6},{135,7},{40,8}... | collective-permute-start | bytes 1572872 | tf_op jit(solution)/shard_map/ppermute | solution.py:210
  29.1 7.0 %copy-start.1 = (s32[1,2048]{1,0:T(1,128)S(1)}, s32[1,2048]{1,0:T(1,128)}, u32[]{:S(2)}) copy-start(s32[1,2048]{1,0:T(1,128)} %param.9) | copy-start | bytes 24580
  30.7 48.9 %collective-permute-start.6 = (bf16[4,128,2048]{2,1,0:T(8,128)(2,1)}, bf16[4,128,2048]{2,1,0:T(8,128)(2,1)}, u32[]{:S(2)}, u32[]{:S(2)}) collective-permute-start(bf16[4,128,2048]{2,1,0:T(8,128)(2,1)} %pad_maximum_fusion.rest_0_), channel_id=1, source_target_pairs={{128,0},{33,1},{130,2},{35,3},{132,4},{37,5},{134,6},{39,7},{136,8... | collective-permute-start | bytes 6291464 | tf_op jit(solution)/shard_map/ppermute | solution.py:210
  33.4 46.7 %collective-permute-start.5 = (bf16[4,128,2048]{2,1,0:T(8,128)(2,1)}, bf16[4,128,2048]{2,1,0:T(8,128)(2,1)}, u32[]{:S(2)}, u32[]{:S(2)}) collective-permute-start(bf16[4,128,2048]{2,1,0:T(8,128)(2,1)} %pad_maximum_fusion.rest_0_), channel_id=1, source_target_pairs={{192,0},{49,1},{194,2},{51,3},{196,4},{53,5},{198,6},{55,7},{200,8... | collective-permute-start | bytes 6291464 | tf_op jit(solution)/shard_map/ppermute | solution.py:210
  33.7 46.5 %collective-permute-start.4 = (bf16[4,128,2048]{2,1,0:T(8,128)(2,1)}, bf16[4,128,2048]{2,1,0:T(8,128)(2,1)}, u32[]{:S(2)}, u32[]{:S(2)}) collective-permute-start(bf16[4,128,2048]{2,1,0:T(8,128)(2,1)} %pad_maximum_fusion.rest_0_), channel_id=1, source_target_pairs={{64,0},{17,1},{66,2},{19,3},{68,4},{21,5},{70,6},{23,7},{72,8},{25... | collective-permute-start | bytes 6291464 | tf_op jit(solution)/shard_map/ppermute | solution.py:210
  79.5 1.9 %collective-permute-start.3 = (bf16[16,128,128]{2,1,0:T(8,128)(2,1)S(1)}, bf16[16,128,128]{2,1,0:T(8,128)(2,1)S(1)}, u32[]{:S(2)}, u32[]{:S(2)}) collective-permute-start(bf16[16,128,128]{2,1,0:T(8,128)(2,1)S(1)} %all_to_all.10.mine_ref), channel_id=1, source_target_pairs={{0,1},{1,0},{2,3},{3,2},{4,5},{5,4},{6,7},{7,6},{8,9},{9,8},{10,11... | collective-permute-start | bytes 1572872 | tf_op jit(solution)/shard_map/ppermute | solution.py:230
  87.1 2.3 %collective-permute-start.7 = (bf16[128,2048]{1,0:T(8,128)(2,1)S(1)}, bf16[128,2048]{1,0:T(8,128)(2,1)S(1)}, u32[]{:S(2)}, u32[]{:S(2)}) collective-permute-start(bf16[128,2048]{1,0:T(8,128)(2,1)S(1)} %get-tuple-element.10), channel_id=1, source_target_pairs={{0,1},{1,0},{2,3},{3,2},{4,5},{5,4},{6,7},{7,6},{8,9},{9,8},{10,11... | collective-permute-start | bytes 1572872 | tf_op jit(solution)/shard_map/ppermute | solution.py:232

commit v7 on v6

--- a/solution.py
+++ b/solution.py
@@ -10,7 +10,7 @@
 
 HDIM = 128
 TILE = 512
-CHAIN = 512
+HALF = TILE // 2
 MASKED = -1e30
 SIDE = 4
 NEAR = (0, 1, 3, 2)
@@ -22,7 +22,6 @@
     slab = blocks * rows
     first, second = bounds_ref[0], bounds_ref[1]
     factor = math.log2(math.e) / math.sqrt(HDIM)
-    chains = TILE // CHAIN
 
     def start_of(position):
         return jnp.where(position >= second, second, jnp.where(position >= first, first, 0))
@@ -55,38 +54,52 @@
 
     for tile in range(slab // TILE):
         base = tile * TILE
-        queries, positions, starts, states = [], [], [], []
-        for chain in range(chains):
-            at = base + chain * CHAIN
-            queries.append(tokens(0, at, CHAIN))
-            position = at + lax.broadcasted_iota(jnp.int32, (1, CHAIN), 1)
-            starts.append(start_of(position))
-            count = (chain + 1) * CHAIN
-            key_pos = base + lax.broadcasted_iota(jnp.int32, (count, 1), 0)
-            mask = (key_pos <= position) & (key_pos >= starts[-1])
-            states.append(attend(None, queries[-1], tokens(1, base, count), values_t(base, count), mask))
+        query = tokens(0, base, TILE)
+        position = base + lax.broadcasted_iota(jnp.int32, (1, TILE), 1)
+        starts = start_of(position)
+        key_pos = base + lax.broadcasted_iota(jnp.int32, (TILE, 1), 0)
+        mask = (key_pos <= position) & (key_pos >= starts)
+        state = attend(None, query, tokens(1, base, TILE), values_t(base, TILE), mask)
         if tile:
-            low = start_of(jnp.int32(base)) // TILE
+            begin = start_of(jnp.int32(base))
+            low = begin // TILE
             full = jnp.minimum((start_of(jnp.int32(base + TILE - 1)) + TILE - 1) // TILE, tile)
-
-            def step(masked, j, states):
+            ends = jnp.minimum(
+                jnp.where(first > base, first, slab), jnp.where(second > base, second, slab)
+            )
+            narrow = ends - base <= HALF
+            short = jnp.logical_not(narrow) & (low < full) & (begin - low * TILE >= HALF)
+            short = short.astype(jnp.int32)
+
+            def masked(state, query, start, count, starts):
+                mask = start + lax.broadcasted_iota(jnp.int32, (count, 1), 0) >= starts
+                return attend(state, query, tokens(1, start, count), values_t(start, count), mask)
+
+            def whole(j, state):
                 start = pl.multiple_of(j * TILE, TILE)
-                keys, v_t = tokens(1, start, TILE), values_t(start, TILE)
-                out = []
-                for chain in range(chains):
-                    mask = None
-                    if masked:
-                        mask = start + lax.broadcasted_iota(jnp.int32, (TILE, 1), 0) >= starts[chain]
-                    out.append(attend(states[chain], queries[chain], keys, v_t, mask))
-                return tuple(out)
-
-            states = lax.fori_loop(full, tile, lambda j, s: step(False, j, s), tuple(states))
-            states = lax.fori_loop(low, full, lambda j, s: step(True, j, s), states)
-        for chain in range(chains):
-            _, total, accum = states[chain]
-            finished = jnp.transpose((accum / total).astype(jnp.bfloat16))
-            at = (base + chain * CHAIN) // rows
-            out_ref[at:at + CHAIN // rows] = finished.reshape(CHAIN // rows, rows, HDIM)
+                return attend(state, query, tokens(1, start, TILE), values_t(start, TILE), None)
+
+            def wide(j, state):
+                return masked(state, query, pl.multiple_of(j * TILE, TILE), TILE, starts)
+
+            def second_half(_, state):
+                return masked(state, query, pl.multiple_of(low * TILE + HALF, HALF), HALF, starts)
+
+            def first_queries(j, state):
+                part = tuple(item[:, :HALF] for item in state)
+                start = pl.multiple_of(j * TILE, TILE)
+                part = masked(part, query[:HALF], start, TILE, starts[:, :HALF])
+                return tuple(
+                    jnp.concatenate([new, old[:, HALF:]], axis=1) for new, old in zip(part, state)
+                )
+
+            state = lax.fori_loop(full, tile, whole, state)
+            state = lax.fori_loop(low + short, jnp.where(narrow, low, full), wide, state)
+            state = lax.fori_loop(0, short, second_half, state)
+            state = lax.fori_loop(low, jnp.where(narrow, full, low), first_queries, state)
+        _, total, accum = state
+        finished = jnp.transpose((accum / total).astype(jnp.bfloat16))
+        out_ref[base // rows:(base + TILE) // rows] = finished.reshape(TILE // rows, rows, HDIM)
 
 
 def pack_kernel(queries_ref, keys_ref, values_ref, out_ref):
@@ -221,11 +234,16 @@
 
     half = out_weight.shape[1] // 2
     own = lax.dynamic_slice_in_dim(out_weight, core * half, half, 1)
-    line = jnp.stack([own] + [fetch(own, step, True) for step in NEAR[1:]])
-    packed, _ = lax.optimization_barrier((packed, line))
-    pieces = [line] + [fetch(line, step, False) for step in NEAR[1:]]
-    places = [(far, near) for far in NEAR for near in NEAR]
+    own = own[None]
+    across = fetch(own, 2, False)
+    near = [fetch(own, step, True) for step in (1, 3, 2)]
+    line = jnp.concatenate([own] + near)
+    near = jnp.concatenate(near)
+    packed, *_ = lax.optimization_barrier((packed, line, near))
+    pieces = [line, fetch(line, 1, False), fetch(line, 3, False), across, fetch(near, 2, False)]
+    places = [(far, step) for far in NEAR for step in NEAR]
     attended = head_attention(bounds, packed)
+    attended, _ = lax.optimization_barrier((attended, across))
     mine = lax.all_to_all(attended, "ctx", 0, 0, tiled=True)
     theirs = lax.ppermute(mine, "ctx", swap)
     part, sent = project(place, mine, theirs, pieces, places)

time: 90.5 us -> 90.7 us (level)
  waiting for transfers between devices: 28.2 us -> 22.5 us
  starting transfers between devices: 20.6 us -> 25.8 us
  local copies, waits for them, and re-layouts: 0.91 us -> 3.38 us
  Pallas kernels: 15.4 us -> 13.6 us
    all_to_all x1, waiting for transfers between devices: 12.8 us -> 7.18 us  [per_device(): lax.all_to_all(pack(queries, keys, values), 'ctx', 0, 0, tiled=True)]
    ppermute x6 -> x7, starting transfers between devices: 9.88 us -> 13.8 us  [fetch(): return lax.ppermute(piece, ('fsdp', 'ctx'), pairs)]
    pallas_call x1, Pallas kernels: 7.17 us -> 5.36 us  [head_attention(): pl.pallas_call(attention_kernel, out_shape=jax.ShapeDtypeStruct((blocks,...]
    unnamed x4 -> x6, local copies, waits for them, and re-layouts: 0.01 us -> 1.66 us
    another operation x1 -> x0, other arithmetic: 1.61 us -> none  [per_device(): line = jnp.stack([own] + [fetch(own, step, True) for step in NEAR[1:]])]
    concatenate x0 -> x1, other arithmetic: none -> 1.6 us  [per_device(): line = jnp.concatenate([own] + near)]
    ppermute x1, waiting for transfers between devices: 1.16 us -> 0.01 us  [per_device(): theirs = lax.ppermute(mine, 'ctx', swap)]
    ppermute x1, starting transfers between devices: 0.76 us -> 1.92 us  [per_device(): got = lax.ppermute(sent, 'ctx', swap)]
  transfers between devices with their start and end apart: 9 -> 10, of which waited for: 8 -> 6; matrix products, arithmetic and copies ran while one was open for 4% -> 7% of each run, Pallas kernels for 8% -> 6%
where the time goes in v7:
time: 90.7 us; the launch traced here: 90.4 us
  starting transfers between devices  25.8 us (28%)
  waiting for transfers between devices  22.5 us (25%)
  blocking collectives  21.4 us (24%)
  Pallas kernels  13.6 us (15%)
  other arithmetic  3.73 us (4%)
  local copies, waits for them, and re-layouts  3.38 us (4%)
    all_to_all x1, blocking collectives, per_device(): mine = lax.all_to_all(attended, 'ctx', 0, 0, tiled=True)  21.4 us
    ppermute x7, starting transfers between devices, fetch(): return lax.ppermute(piece, ('fsdp', 'ctx'), pairs)  13.8 us
    ppermute x7, waiting for transfers between devices, fetch(): return lax.ppermute(piece, ('fsdp', 'ctx'), pairs)  13.7 us
    all_to_all x1, starting transfers between devices, per_device(): lax.all_to_all(pack(queries, keys, values), 'ctx', 0, 0, tiled=True)  10.1 us
    all_to_all x1, waiting for transfers between devices, per_device(): lax.all_to_all(pack(queries, keys, values), 'ctx', 0, 0, tiled=True)  7.18 us
    pallas_call x1, Pallas kernels, project(): pl.pallas_call(functools.partial(projection_kernel, places), out_shape=(j...  5.75 us
    pallas_call x1, Pallas kernels, head_attention(): pl.pallas_call(attention_kernel, out_shape=jax.ShapeDtypeStruct((blocks,...  5.36 us
    pallas_call x1, Pallas kernels, pack(): pl.pallas_call(pack_kernel, out_shape=jax.ShapeDtypeStruct((heads, 3, row...  2.49 us
  transfers between devices with their start and end apart: 10, of which 6 were waited for; matrix products, arithmetic and copies ran while one was open for 7% of the time, Pallas kernels for 6%

profile of v7, /device:TPU:1, one launch (start us, length us, event | category | flops | bytes accessed | tf_op | source)
XLA Modules:
  0.0 90.4 jit_solution(15212688053558923894)
XLA Ops:
  0.0 0.0 copy-start
  0.0 2.5 %pack.1 = bf16[16,3,128,128]{3,2,1,0:T(8,128)(2,1)} custom-call(bf16[128,2048]{1,0:T(8,128)(2,1)} %queries_ref.1, bf16[128,2048]{1,0:T(8,128)(2,1)} %keys_ref.1, bf16[128,2048]{1,0:T(8,128)(2,1)} %values_ref.1), custom_call_target="tpu_custom_call" | custom-call | tf_op jit(solution)/shard_map/pack/pallas_call | solution.py:115
  2.5 0.0 copy-start.1
  2.5 10.1 %all-to-all-start = ((bf16[16,3,128,128]{3,2,1,0:T(8,128)(2,1)}), bf16[16,3,128,128]{3,2,1,0:T(8,128)(2,1)S(1)}, u32[]{:S(2)}, u32[]{:S(2)}) async-start(bf16[16,3,128,128]{3,2,1,0:T(8,128)(2,1)} %pack.1), calls=%async_computation | async-start | bytes 3145728 | tf_op jit(solution)/shard_map/all_to_all | solution.py:233
  12.6 0.0 copy-done
  12.7 3.0 %collective-permute-start.2 = (bf16[1,128,2048]{2,1,0:T(8,128)(2,1)S(1)}, bf16[1,128,2048]{2,1,0:T(8,128)(2,1)S(1)}, u32[]{:S(2)}, u32[]{:S(2)}) collective-permute-start(bf16[1,128,2048]{2,1,0:T(8,128)(2,1)S(1)} %dynamic-slice_bitcast_fusion), channel_id=1, source_target_pairs={{32,0},{129,1},{34,2},{131,3},{36,4},{133,5},{38,6},{135,7},{40,8}... | collective-permute-start | bytes 1572872 | tf_op jit(solution)/shard_map/ppermute | solution.py:223
  15.7 0.4 collective-permute-start.1
  16.1 2.3 %collective-permute-start = (bf16[1,128,2048]{2,1,0:T(8,128)(2,1)S(1)}, bf16[1,128,2048]{2,1,0:T(8,128)(2,1)S(1)}, u32[]{:S(2)}, u32[]{:S(2)}) collective-permute-start(bf16[1,128,2048]{2,1,0:T(8,128)(2,1)S(1)} %dynamic-slice_bitcast_fusion), channel_id=1, source_target_pairs={{16,0},{65,1},{18,2},{67,3},{20,4},{69,5},{22,6},{71,7},{24,8},{73... | collective-permute-start | bytes 1572872 | tf_op jit(solution)/shard_map/ppermute | solution.py:223
  18.3 2.7 %collective-permute-start.3 = (bf16[1,128,2048]{2,1,0:T(8,128)(2,1)S(1)}, bf16[1,128,2048]{2,1,0:T(8,128)(2,1)}, u32[]{:S(2)}, u32[]{:S(2)}) collective-permute-start(bf16[1,128,2048]{2,1,0:T(8,128)(2,1)S(1)} %dynamic-slice_bitcast_fusion), channel_id=1, source_target_pairs={{128,0},{33,1},{130,2},{35,3},{132,4},{37,5},{134,6},{39,7},{136,8... | collective-permute-start | bytes 1572872 | tf_op jit(solution)/shard_map/ppermute | solution.py:223
  21.1 0.0 copy-done.1
  21.1 0.7 fusion
  21.8 0.8 collective-permute-done.2
  22.6 10.0 %collective-permute-done.1 = bf16[1,128,2048]{2,1,0:T(8,128)(2,1)S(1)} collective-permute-done((bf16[1,128,2048]{2,1,0:T(8,128)(2,1)S(1)}, bf16[1,128,2048]{2,1,0:T(8,128)(2,1)S(1)}, u32[]{:S(2)}, u32[]{:S(2)}) %collective-permute-start.1) | collective-permute-done | bytes 524320 | tf_op jit(solution)/shard_map/ppermute | solution.py:223
  32.6 0.4 collective-permute-done
  33.1 1.6 %pad_maximum_fusion.rest_0_ = bf16[4,128,2048]{2,1,0:T(8,128)(2,1)} fusion(bf16[1,128,2048]{2,1,0:T(8,128)(2,1)S(1)} %collective-permute-done.2, bf16[1,128,2048]{2,1,0:T(8,128)(2,1)S(1)} %collective-permute-done.1, bf16[1,128,2048]{2,1,0:T(8,128)(2,1)S(1)} %collective-permute-done, bf16[1,128,2048]{2,1,0:T(8,128)(2,1)S(1)} %dynamic-slice_bitcast_fusion), kind=kLoop, calls=%fused_computation | loop fusion | flops 3145728 | bytes 4194304 | tf_op jit(solution)/shard_map/concatenate | solution.py:240
  34.7 2.4 %collective-permute-start.6 = (bf16[4,128,2048]{2,1,0:T(8,128)(2,1)}, bf16[4,128,2048]{2,1,0:T(8,128)(2,1)}, u32[]{:S(2)}, u32[]{:S(2)}) collective-permute-start(bf16[4,128,2048]{2,1,0:T(8,128)(2,1)} %pad_maximum_fusion.rest_0_), channel_id=1, source_target_pairs={{192,0},{49,1},{194,2},{51,3},{196,4},{53,5},{198,6},{55,7},{200,8... | collective-permute-start | bytes 6291464 | tf_op jit(solution)/shard_map/ppermute | solution.py:223
  37.0 1.3 %collective-permute-start.5 = (bf16[4,128,2048]{2,1,0:T(8,128)(2,1)}, bf16[4,128,2048]{2,1,0:T(8,128)(2,1)}, u32[]{:S(2)}, u32[]{:S(2)}) collective-permute-start(bf16[4,128,2048]{2,1,0:T(8,128)(2,1)} %pad_maximum_fusion.rest_0_), channel_id=1, source_target_pairs={{64,0},{17,1},{66,2},{19,3},{68,4},{21,5},{70,6},{23,7},{72,8},{25... | collective-permute-start | bytes 6291464 | tf_op jit(solution)/shard_map/ppermute | solution.py:223
  38.3 0.8 constant_dynamic-update-slice_fusion.2
  39.1 0.8 constant_dynamic-update-slice_fusion.1
  39.9 0.9 constant_dynamic-update-slice_fusion
  40.8 1.7 %collective-permute-start.7 = (bf16[3,128,2048]{2,1,0:T(8,128)(2,1)}, bf16[3,128,2048]{2,1,0:T(8,128)(2,1)}, u32[]{:S(2)}, u32[]{:S(2)}) collective-permute-start(bf16[3,128,2048]{2,1,0:T(8,128)(2,1)} %constant_dynamic-update-slice_fusion), channel_id=1, source_target_pairs={{128,0},{33,1},{130,2},{35,3},{132,4},{37,5},{134,6},{39,7},{136,8... | collective-permute-start | bytes 4718600 | tf_op jit(solution)/shard_map/ppermute | solution.py:223
  42.5 1.3 %pad_add_fusion.1.bounds_ref = s32[2]{0:T(128)S(1)} fusion(s32[1]{0:T(128)} %bitcast.4, s32[1]{0:T(128)} %bitcast.3), kind=kLoop, calls=%fused_computation.10 | loop fusion | flops 2 | bytes 16 | tf_op jit(solution)/shard_map/stack | solution.py:229
  43.9 7.2 %all-to-all-done.packed_ref = bf16[16,3,128,128]{3,2,1,0:T(8,128)(2,1)S(1)} async-done(((bf16[16,3,128,128]{3,2,1,0:T(8,128)(2,1)}), bf16[16,3,128,128]{3,2,1,0:T(8,128)(2,1)S(1)}, u32[]{:S(2)}, u32[]{:S(2)}) %all-to-all-start) | async-done | bytes 1572896 | tf_op jit(solution)/shard_map/all_to_all | solution.py:233
  51.0 5.4 %head_attention.1 = bf16[16,128,128]{2,1,0:T(8,128)(2,1)S(1)} custom-call(s32[2]{0:T(128)S(1)} %pad_add_fusion.1.bounds_ref, bf16[16,3,128,128]{3,2,1,0:T(8,128)(2,1)S(1)} %all-to-all-done.packed_ref), custom_call_target="tpu_custom_call" | custom-call | tf_op jit(solution)/shard_map/head_attention/pallas_call | solution.py:128
  56.4 0.0 collective-permute-done.3.rest_3_
  56.4 21.4 %all_to_all.10.mine_ref = bf16[16,128,128]{2,1,0:T(8,128)(2,1)S(1)} all-to-all(bf16[16,128,128]{2,1,0:T(8,128)(2,1)S(1)} %head_attention.1), channel_id=1, replica_groups=mesh['fsdp'=16,'ctx'=16] {'ctx'}, dimensions={0} | all-to-all | bytes 1048576 | tf_op jit(solution)/shard_map/all_to_all | solution.py:247
  77.8 0.0 collective-permute-start.4
  77.8 0.1 pad_add_fusion.place_ref
  77.9 2.5 %collective-permute-done.7.rest_4_ = bf16[3,128,2048]{2,1,0:T(8,128)(2,1)} collective-permute-done((bf16[3,128,2048]{2,1,0:T(8,128)(2,1)}, bf16[3,128,2048]{2,1,0:T(8,128)(2,1)}, u32[]{:S(2)}, u32[]{:S(2)}) %collective-permute-start.7) | collective-permute-done | bytes 1572896 | tf_op jit(solution)/shard_map/ppermute | solution.py:223
  80.3 0.0 collective-permute-done.6.rest_2_
  80.4 0.0 collective-permute-done.5.rest_1_
  80.4 0.0 collective-permute-done.4.theirs_ref
  80.4 5.7 %project.1 = (bf16[128,4096]{1,0:T(8,128)(2,1)}, bf16[128,2048]{1,0:T(8,128)(2,1)S(1)}) custom-call(s32[3]{0:T(128)S(1)} %pad_add_fusion.place_ref, bf16[16,128,128]{2,1,0:T(8,128)(2,1)S(1)} %all_to_all.10.mine_ref, bf16[16,128,128]{2,1,0:T(8,128)(2,1)S(1)} %collective-permute-done.4.theirs_ref, bf16[4,128,2048]{2,1,0:T(8,128)(2,1)} %pad_maximum_fusion.rest_0_, ...), custom_call_target="tpu_custom_call" | custom-call | tf_op jit(solution)/shard_map/project/pallas_call | solution.py:191
  86.1 1.9 %collective-permute-start.8 = (bf16[128,2048]{1,0:T(8,128)(2,1)S(1)}, bf16[128,2048]{1,0:T(8,128)(2,1)S(1)}, u32[]{:S(2)}, u32[]{:S(2)}) collective-permute-start(bf16[128,2048]{1,0:T(8,128)(2,1)S(1)} %get-tuple-element.12), channel_id=1, source_target_pairs={{0,1},{1,0},{2,3},{3,2},{4,5},{5,4},{6,7},{7,6},{8,9},{9,8},{10,11... | collective-permute-start | bytes 1572872 | tf_op jit(solution)/shard_map/ppermute | solution.py:250
  88.0 1.5 %collective-permute-done.8 = bf16[128,2048]{1,0:T(8,128)(2,1)S(1)} collective-permute-done((bf16[128,2048]{1,0:T(8,128)(2,1)S(1)}, bf16[128,2048]{1,0:T(8,128)(2,1)S(1)}, u32[]{:S(2)}, u32[]{:S(2)}) %collective-permute-start.8) | collective-permute-done | bytes 524320 | tf_op jit(solution)/shard_map/ppermute | solution.py:250
  89.6 0.8 constant_dynamic-update-slice_fusion.3
  (1 shorter events, 0.0 us)
Async XLA Ops:
  0.0 12.6 %copy-start = (bf16[128,4096]{1,0:T(8,128)(2,1)S(1)}, bf16[128,4096]{1,0:T(8,128)(2,1)}, u32[]{:S(2)}) copy-start(bf16[128,4096]{1,0:T(8,128)(2,1)} %param.8) | copy-start | bytes 3145732
  2.5 18.6 %copy-start.1 = (s32[1,2048]{1,0:T(1,128)S(1)}, s32[1,2048]{1,0:T(1,128)}, u32[]{:S(2)}) copy-start(s32[1,2048]{1,0:T(1,128)} %param.9) | copy-start | bytes 24580
  2.5 48.5 %all-to-all-start = ((bf16[16,3,128,128]{3,2,1,0:T(8,128)(2,1)}), bf16[16,3,128,128]{3,2,1,0:T(8,128)(2,1)S(1)}, u32[]{:S(2)}, u32[]{:S(2)}) async-start(bf16[16,3,128,128]{3,2,1,0:T(8,128)(2,1)} %pack.1), calls=%async_computation | async-start | bytes 3145728 | tf_op jit(solution)/shard_map/all_to_all | solution.py:233
  12.7 10.0 %collective-permute-start.2 = (bf16[1,128,2048]{2,1,0:T(8,128)(2,1)S(1)}, bf16[1,128,2048]{2,1,0:T(8,128)(2,1)S(1)}, u32[]{:S(2)}, u32[]{:S(2)}) collective-permute-start(bf16[1,128,2048]{2,1,0:T(8,128)(2,1)S(1)} %dynamic-slice_bitcast_fusion), channel_id=1, source_target_pairs={{32,0},{129,1},{34,2},{131,3},{36,4},{133,5},{38,6},{135,7},{40,8}... | collective-permute-start | bytes 1572872 | tf_op jit(solution)/shard_map/ppermute | solution.py:223
  15.7 17.0 %collective-permute-start.1 = (bf16[1,128,2048]{2,1,0:T(8,128)(2,1)S(1)}, bf16[1,128,2048]{2,1,0:T(8,128)(2,1)S(1)}, u32[]{:S(2)}, u32[]{:S(2)}) collective-permute-start(bf16[1,128,2048]{2,1,0:T(8,128)(2,1)S(1)} %dynamic-slice_bitcast_fusion), channel_id=1, source_target_pairs={{48,0},{193,1},{50,2},{195,3},{52,4},{197,5},{54,6},{199,7},{56,8}... | collective-permute-start | bytes 1572872 | tf_op jit(solution)/shard_map/ppermute | solution.py:223
  16.1 17.0 %collective-permute-start = (bf16[1,128,2048]{2,1,0:T(8,128)(2,1)S(1)}, bf16[1,128,2048]{2,1,0:T(8,128)(2,1)S(1)}, u32[]{:S(2)}, u32[]{:S(2)}) collective-permute-start(bf16[1,128,2048]{2,1,0:T(8,128)(2,1)S(1)} %dynamic-slice_bitcast_fusion), channel_id=1, source_target_pairs={{16,0},{65,1},{18,2},{67,3},{20,4},{69,5},{22,6},{71,7},{24,8},{73... | collective-permute-start | bytes 1572872 | tf_op jit(solution)/shard_map/ppermute | solution.py:223
  18.3 38.1 %collective-permute-start.3 = (bf16[1,128,2048]{2,1,0:T(8,128)(2,1)S(1)}, bf16[1,128,2048]{2,1,0:T(8,128)(2,1)}, u32[]{:S(2)}, u32[]{:S(2)}) collective-permute-start(bf16[1,128,2048]{2,1,0:T(8,128)(2,1)S(1)} %dynamic-slice_bitcast_fusion), channel_id=1, source_target_pairs={{128,0},{33,1},{130,2},{35,3},{132,4},{37,5},{134,6},{39,7},{136,8... | collective-permute-start | bytes 1572872 | tf_op jit(solution)/shard_map/ppermute | solution.py:223
  34.7 45.7 %collective-permute-start.6 = (bf16[4,128,2048]{2,1,0:T(8,128)(2,1)}, bf16[4,128,2048]{2,1,0:T(8,128)(2,1)}, u32[]{:S(2)}, u32[]{:S(2)}) collective-permute-start(bf16[4,128,2048]{2,1,0:T(8,128)(2,1)} %pad_maximum_fusion.rest_0_), channel_id=1, source_target_pairs={{192,0},{49,1},{194,2},{51,3},{196,4},{53,5},{198,6},{55,7},{200,8... | collective-permute-start | bytes 6291464 | tf_op jit(solution)/shard_map/ppermute | solution.py:223
  37.0 43.3 %collective-permute-start.5 = (bf16[4,128,2048]{2,1,0:T(8,128)(2,1)}, bf16[4,128,2048]{2,1,0:T(8,128)(2,1)}, u32[]{:S(2)}, u32[]{:S(2)}) collective-permute-start(bf16[4,128,2048]{2,1,0:T(8,128)(2,1)} %pad_maximum_fusion.rest_0_), channel_id=1, source_target_pairs={{64,0},{17,1},{66,2},{19,3},{68,4},{21,5},{70,6},{23,7},{72,8},{25... | collective-permute-start | bytes 6291464 | tf_op jit(solution)/shard_map/ppermute | solution.py:223
  40.8 39.6 %collective-permute-start.7 = (bf16[3,128,2048]{2,1,0:T(8,128)(2,1)}, bf16[3,128,2048]{2,1,0:T(8,128)(2,1)}, u32[]{:S(2)}, u32[]{:S(2)}) collective-permute-start(bf16[3,128,2048]{2,1,0:T(8,128)(2,1)} %constant_dynamic-update-slice_fusion), channel_id=1, source_target_pairs={{128,0},{33,1},{130,2},{35,3},{132,4},{37,5},{134,6},{39,7},{136,8... | collective-permute-start | bytes 4718600 | tf_op jit(solution)/shard_map/ppermute | solution.py:223
  77.8 2.6 %collective-permute-start.4 = (bf16[16,128,128]{2,1,0:T(8,128)(2,1)S(1)}, bf16[16,128,128]{2,1,0:T(8,128)(2,1)S(1)}, u32[]{:S(2)}, u32[]{:S(2)}) collective-permute-start(bf16[16,128,128]{2,1,0:T(8,128)(2,1)S(1)} %all_to_all.10.mine_ref), channel_id=1, source_target_pairs={{0,1},{1,0},{2,3},{3,2},{4,5},{5,4},{6,7},{7,6},{8,9},{9,8},{10,11... | collective-permute-start | bytes 1572872 | tf_op jit(solution)/shard_map/ppermute | solution.py:248
  86.1 3.5 %collective-permute-start.8 = (bf16[128,2048]{1,0:T(8,128)(2,1)S(1)}, bf16[128,2048]{1,0:T(8,128)(2,1)S(1)}, u32[]{:S(2)}, u32[]{:S(2)}) collective-permute-start(bf16[128,2048]{1,0:T(8,128)(2,1)S(1)} %get-tuple-element.12), channel_id=1, source_target_pairs={{0,1},{1,0},{2,3},{3,2},{4,5},{5,4},{6,7},{7,6},{8,9},{9,8},{10,11... | collective-permute-start | bytes 1572872 | tf_op jit(solution)/shard_map/ppermute | solution.py:250

commit v8 on v7

--- a/solution.py
+++ b/solution.py
@@ -17,7 +17,7 @@
 STRIP = 512
 
 
-def attention_kernel(bounds_ref, packed_ref, out_ref, vt_ref):
+def attention_kernel(bounds_ref, packed_ref, out_ref):
     blocks, _, rows, _ = packed_ref.shape
     slab = blocks * rows
     first, second = bounds_ref[0], bounds_ref[1]
@@ -29,11 +29,8 @@
     def tokens(index, start, count):
         return packed_ref[pl.ds(start // rows, count // rows), index].reshape(count, HDIM)
 
-    for block in range(blocks):
-        vt_ref[block] = jnp.transpose(packed_ref[block, 2])
-
     def values_t(start, count):
-        part = vt_ref[pl.ds(start // rows, count // rows)]
+        part = packed_ref[pl.ds(start // rows, count // rows), 2]
         return jnp.concatenate([part[i] for i in range(count // rows)], axis=1)
 
     def attend(state, query, keys, v_t, mask):
@@ -103,9 +100,11 @@
 
 
 def pack_kernel(queries_ref, keys_ref, values_ref, out_ref):
-    for index, ref in enumerate((queries_ref, keys_ref, values_ref)):
-        for head in range(out_ref.shape[0]):
-            out_ref[head, index] = ref[:, head * HDIM:(head + 1) * HDIM]
+    for head in range(out_ref.shape[0]):
+        columns = slice(head * HDIM, (head + 1) * HDIM)
+        out_ref[head, 0] = queries_ref[:, columns]
+        out_ref[head, 1] = keys_ref[:, columns]
+        out_ref[head, 2] = jnp.transpose(values_ref[:, columns])
 
 
 def pack(queries, keys, values):
@@ -130,7 +129,6 @@
         out_shape=jax.ShapeDtypeStruct((blocks, rows, HDIM), jnp.bfloat16),
         in_specs=[pl.BlockSpec(memory_space=pltpu.SMEM), vmem],
         out_specs=vmem,
-        scratch_shapes=[pltpu.VMEM((blocks, HDIM, rows), jnp.bfloat16)],
         compiler_params=pltpu.CompilerParams(vmem_limit_bytes=16 << 20),
         name="head_attention",
     )(bounds, packed)
@@ -234,16 +232,11 @@
 
     half = out_weight.shape[1] // 2
     own = lax.dynamic_slice_in_dim(out_weight, core * half, half, 1)
-    own = own[None]
-    across = fetch(own, 2, False)
-    near = [fetch(own, step, True) for step in (1, 3, 2)]
-    line = jnp.concatenate([own] + near)
-    near = jnp.concatenate(near)
-    packed, *_ = lax.optimization_barrier((packed, line, near))
-    pieces = [line, fetch(line, 1, False), fetch(line, 3, False), across, fetch(near, 2, False)]
-    places = [(far, step) for far in NEAR for step in NEAR]
+    line = jnp.stack([own] + [fetch(own, step, True) for step in NEAR[1:]])
+    packed, _ = lax.optimization_barrier((packed, line))
+    pieces = [line] + [fetch(line, step, False) for step in NEAR[1:]]
+    places = [(far, near) for far in NEAR for near in NEAR]
     attended = head_attention(bounds, packed)
-    attended, _ = lax.optimization_barrier((attended, across))
     mine = lax.all_to_all(attended, "ctx", 0, 0, tiled=True)
     theirs = lax.ppermute(mine, "ctx", swap)
     part, sent = project(place, mine, theirs, pieces, places)

time: 90.7 us -> 90.5 us (level)
  waiting for transfers between devices: 22.5 us -> 28.2 us
  starting transfers between devices: 25.8 us -> 20.8 us
  local copies, waits for them, and re-layouts: 3.38 us -> 0.91 us
  Pallas kernels: 13.6 us -> 15 us
    all_to_all x1, waiting for transfers between devices: 7.18 us -> 12.8 us  [per_device(): lax.all_to_all(pack(queries, keys, values), 'ctx', 0, 0, tiled=True)]
    ppermute x7 -> x6, starting transfers between devices: 13.8 us -> 9.88 us  [fetch(): return lax.ppermute(piece, ('fsdp', 'ctx'), pairs)]
    unnamed x6 -> x4, local copies, waits for them, and re-layouts: 1.66 us -> 0.01 us
    another operation x0 -> x1, other arithmetic: none -> 1.61 us  [per_device(): line = jnp.stack([own] + [fetch(own, step, True) for step in NEAR[1:]])]
    concatenate x1 -> x0, other arithmetic: 1.6 us -> none  [per_device(): line = jnp.concatenate([own] + near)]
    pallas_call x1, Pallas kernels: 5.36 us -> 6.78 us  [head_attention(): pl.pallas_call(attention_kernel, out_shape=jax.ShapeDtypeStruct((blocks,...]
    ppermute x1, waiting for transfers between devices: 0.01 us -> 0.96 us  [per_device(): theirs = lax.ppermute(mine, 'ctx', swap)]
    ppermute x1, starting transfers between devices: 1.92 us -> 0.96 us  [per_device(): got = lax.ppermute(sent, 'ctx', swap)]
  transfers between devices with their start and end apart: 10 -> 9, of which waited for: 6 -> 8; matrix products, arithmetic and copies ran while one was open for 7% -> 4% of each run, Pallas kernels for 6% -> 8%
where the time goes in v8:
time: 90.5 us; the launch traced here: 90.3 us
  waiting for transfers between devices  28.2 us (31%)
  blocking collectives  21.6 us (24%)
  starting transfers between devices  20.8 us (23%)
  Pallas kernels  15 us (17%)
  other arithmetic  3.72 us (4%)
  local copies, waits for them, and re-layouts  0.91 us (1%)
    all_to_all x1, blocking collectives, per_device(): mine = lax.all_to_all(attended, 'ctx', 0, 0, tiled=True)  21.6 us
    ppermute x6, waiting for transfers between devices, fetch(): return lax.ppermute(piece, ('fsdp', 'ctx'), pairs)  12.8 us
    all_to_all x1, waiting for transfers between devices, per_device(): lax.all_to_all(pack(queries, keys, values), 'ctx', 0, 0, tiled=True)  12.8 us
    all_to_all x1, starting transfers between devices, per_device(): lax.all_to_all(pack(queries, keys, values), 'ctx', 0, 0, tiled=True)  9.98 us
    ppermute x6, starting transfers between devices, fetch(): return lax.ppermute(piece, ('fsdp', 'ctx'), pairs)  9.88 us
    pallas_call x1, Pallas kernels, head_attention(): pl.pallas_call(attention_kernel, out_shape=jax.ShapeDtypeStruct((blocks,...  6.78 us
    pallas_call x1, Pallas kernels, project(): pl.pallas_call(functools.partial(projection_kernel, places), out_shape=(j...  5.71 us
    pallas_call x1, Pallas kernels, pack(): pl.pallas_call(pack_kernel, out_shape=jax.ShapeDtypeStruct((heads, 3, row...  2.55 us
  transfers between devices with their start and end apart: 9, of which 8 were waited for; matrix products, arithmetic and copies ran while one was open for 4% of the time, Pallas kernels for 8%

profile of v8, /device:TPU:1, one launch (start us, length us, event | category | flops | bytes accessed | tf_op | source)
XLA Modules:
  0.0 90.3 jit_solution(8966409817873804690)
XLA Ops:
  0.0 0.0 copy-start
  0.0 2.5 %pack.1 = bf16[16,3,128,128]{3,2,1,0:T(8,128)(2,1)} custom-call(bf16[128,2048]{1,0:T(8,128)(2,1)} %queries_ref.1, bf16[128,2048]{1,0:T(8,128)(2,1)} %keys_ref.1, bf16[128,2048]{1,0:T(8,128)(2,1)} %values_ref.1), custom_call_target="tpu_custom_call" | custom-call | tf_op jit(solution)/shard_map/pack/pallas_call | solution.py:114
  2.6 10.0 %all-to-all-start = ((bf16[16,3,128,128]{3,2,1,0:T(8,128)(2,1)}), bf16[16,3,128,128]{3,2,1,0:T(8,128)(2,1)S(1)}, u32[]{:S(2)}, u32[]{:S(2)}) async-start(bf16[16,3,128,128]{3,2,1,0:T(8,128)(2,1)} %pack.1), calls=%async_computation | async-start | bytes 3145728 | tf_op jit(solution)/shard_map/all_to_all | solution.py:231
  12.5 0.0 copy-done
  12.6 1.4 %collective-permute-start.1 = (bf16[128,2048]{1,0:T(8,128)(2,1)S(1)}, bf16[128,2048]{1,0:T(8,128)(2,1)S(1)}, u32[]{:S(2)}, u32[]{:S(2)}) collective-permute-start(bf16[128,2048]{1,0:T(8,128)(2,1)S(1)} %constant_dynamic-slice_fusion), channel_id=1, source_target_pairs={{48,0},{193,1},{50,2},{195,3},{52,4},{197,5},{54,6},{199,7},{56,8}... | collective-permute-start | bytes 1572872 | tf_op jit(solution)/shard_map/ppermute | solution.py:221
  14.0 1.5 %collective-permute-start = (bf16[128,2048]{1,0:T(8,128)(2,1)S(1)}, bf16[128,2048]{1,0:T(8,128)(2,1)S(1)}, u32[]{:S(2)}, u32[]{:S(2)}) collective-permute-start(bf16[128,2048]{1,0:T(8,128)(2,1)S(1)} %constant_dynamic-slice_fusion), channel_id=1, source_target_pairs={{16,0},{65,1},{18,2},{67,3},{20,4},{69,5},{22,6},{71,7},{24,8},{73... | collective-permute-start | bytes 1572872 | tf_op jit(solution)/shard_map/ppermute | solution.py:221
  15.5 1.6 %collective-permute-start.2 = (bf16[128,2048]{1,0:T(8,128)(2,1)S(1)}, bf16[128,2048]{1,0:T(8,128)(2,1)S(1)}, u32[]{:S(2)}, u32[]{:S(2)}) collective-permute-start(bf16[128,2048]{1,0:T(8,128)(2,1)S(1)} %constant_dynamic-slice_fusion), channel_id=1, source_target_pairs={{32,0},{129,1},{34,2},{131,3},{36,4},{133,5},{38,6},{135,7},{40,8}... | collective-permute-start | bytes 1572872 | tf_op jit(solution)/shard_map/ppermute | solution.py:221
  17.1 5.2 %collective-permute-done.1 = bf16[128,2048]{1,0:T(8,128)(2,1)S(1)} collective-permute-done((bf16[128,2048]{1,0:T(8,128)(2,1)S(1)}, bf16[128,2048]{1,0:T(8,128)(2,1)S(1)}, u32[]{:S(2)}, u32[]{:S(2)}) %collective-permute-start.1) | collective-permute-done | bytes 524320 | tf_op jit(solution)/shard_map/ppermute | solution.py:221
  22.3 5.0 %collective-permute-done = bf16[128,2048]{1,0:T(8,128)(2,1)S(1)} collective-permute-done((bf16[128,2048]{1,0:T(8,128)(2,1)S(1)}, bf16[128,2048]{1,0:T(8,128)(2,1)S(1)}, u32[]{:S(2)}, u32[]{:S(2)}) %collective-permute-start) | collective-permute-done | bytes 524320 | tf_op jit(solution)/shard_map/ppermute | solution.py:221
  27.2 1.8 %collective-permute-done.2 = bf16[128,2048]{1,0:T(8,128)(2,1)S(1)} collective-permute-done((bf16[128,2048]{1,0:T(8,128)(2,1)S(1)}, bf16[128,2048]{1,0:T(8,128)(2,1)S(1)}, u32[]{:S(2)}, u32[]{:S(2)}) %collective-permute-start.2) | collective-permute-done | bytes 524320 | tf_op jit(solution)/shard_map/ppermute | solution.py:221
  29.1 0.0 copy-start.1
  29.1 1.6 %pad_maximum_fusion.rest_0_ = bf16[4,128,2048]{2,1,0:T(8,128)(2,1)} fusion(bf16[1,128,2048]{2,1,0:T(8,128)(2,1)S(1)} %bitcast.12, bf16[1,128,2048]{2,1,0:T(8,128)(2,1)S(1)} %bitcast.10, bf16[1,128,2048]{2,1,0:T(8,128)(2,1)S(1)} %bitcast.11, bf16[1,128,2048]{2,1,0:T(8,128)(2,1)S(1)} %fusion.2), kind=kLoop, calls=%fused_computation | loop fusion | flops 3145728 | bytes 4194304 | tf_op jit(solution)/shard_map/stack | solution.py:235
  30.7 2.7 %collective-permute-start.6 = (bf16[4,128,2048]{2,1,0:T(8,128)(2,1)}, bf16[4,128,2048]{2,1,0:T(8,128)(2,1)}, u32[]{:S(2)}, u32[]{:S(2)}) collective-permute-start(bf16[4,128,2048]{2,1,0:T(8,128)(2,1)} %pad_maximum_fusion.rest_0_), channel_id=1, source_target_pairs={{128,0},{33,1},{130,2},{35,3},{132,4},{37,5},{134,6},{39,7},{136,8... | collective-permute-start | bytes 6291464 | tf_op jit(solution)/shard_map/ppermute | solution.py:221
  33.4 0.3 collective-permute-start.5
  33.7 2.4 %collective-permute-start.4 = (bf16[4,128,2048]{2,1,0:T(8,128)(2,1)}, bf16[4,128,2048]{2,1,0:T(8,128)(2,1)}, u32[]{:S(2)}, u32[]{:S(2)}) collective-permute-start(bf16[4,128,2048]{2,1,0:T(8,128)(2,1)} %pad_maximum_fusion.rest_0_), channel_id=1, source_target_pairs={{64,0},{17,1},{66,2},{19,3},{68,4},{21,5},{70,6},{23,7},{72,8},{25... | collective-permute-start | bytes 6291464 | tf_op jit(solution)/shard_map/ppermute | solution.py:221
  36.1 0.0 copy-done.1
  36.1 0.7 fusion
  36.8 1.4 %pad_add_fusion.1.bounds_ref = s32[2]{0:T(128)S(1)} fusion(s32[1]{0:T(128)} %bitcast.4, s32[1]{0:T(128)} %bitcast.3), kind=kLoop, calls=%fused_computation.6 | loop fusion | flops 2 | bytes 16 | tf_op jit(solution)/shard_map/stack | solution.py:227
  38.1 12.8 %all-to-all-done.packed_ref = bf16[16,3,128,128]{3,2,1,0:T(8,128)(2,1)S(1)} async-done(((bf16[16,3,128,128]{3,2,1,0:T(8,128)(2,1)}), bf16[16,3,128,128]{3,2,1,0:T(8,128)(2,1)S(1)}, u32[]{:S(2)}, u32[]{:S(2)}) %all-to-all-start) | async-done | bytes 1572896 | tf_op jit(solution)/shard_map/all_to_all | solution.py:231
  51.0 6.8 %head_attention.1 = bf16[16,128,128]{2,1,0:T(8,128)(2,1)S(1)} custom-call(s32[2]{0:T(128)S(1)} %pad_add_fusion.1.bounds_ref, bf16[16,3,128,128]{3,2,1,0:T(8,128)(2,1)S(1)} %all-to-all-done.packed_ref), custom_call_target="tpu_custom_call" | custom-call | tf_op jit(solution)/shard_map/head_attention/pallas_call | solution.py:127
  57.8 21.6 %all_to_all.10.mine_ref = bf16[16,128,128]{2,1,0:T(8,128)(2,1)S(1)} all-to-all(bf16[16,128,128]{2,1,0:T(8,128)(2,1)S(1)} %head_attention.1), channel_id=1, replica_groups=mesh['fsdp'=16,'ctx'=16] {'ctx'}, dimensions={0} | all-to-all | bytes 1048576 | tf_op jit(solution)/shard_map/all_to_all | solution.py:240
  79.3 0.0 collective-permute-start.3
  79.3 0.1 pad_add_fusion.place_ref
  79.4 0.0 collective-permute-done.6.rest_3_
  79.4 0.7 collective-permute-done.5.rest_2_
  80.1 0.1 collective-permute-done.4.rest_1_
  80.3 1.0 %collective-permute-done.3.theirs_ref = bf16[16,128,128]{2,1,0:T(8,128)(2,1)S(1)} collective-permute-done((bf16[16,128,128]{2,1,0:T(8,128)(2,1)S(1)}, bf16[16,128,128]{2,1,0:T(8,128)(2,1)S(1)}, u32[]{:S(2)}, u32[]{:S(2)}) %collective-permute-start.3) | collective-permute-done | bytes 524320 | tf_op jit(solution)/shard_map/ppermute | solution.py:241
  81.2 5.7 %project.1 = (bf16[128,4096]{1,0:T(8,128)(2,1)}, bf16[128,2048]{1,0:T(8,128)(2,1)S(1)}) custom-call(s32[3]{0:T(128)S(1)} %pad_add_fusion.place_ref, bf16[16,128,128]{2,1,0:T(8,128)(2,1)S(1)} %all_to_all.10.mine_ref, bf16[16,128,128]{2,1,0:T(8,128)(2,1)S(1)} %collective-permute-done.3.theirs_ref, bf16[4,128,2048]{2,1,0:T(8,128)(2,1)} %pad_maximum_fusion.rest_0_, ...), custom_call_target="tpu_custom_call" | custom-call | tf_op jit(solution)/shard_map/project/pallas_call | solution.py:189
  87.0 1.0 %collective-permute-start.7 = (bf16[128,2048]{1,0:T(8,128)(2,1)S(1)}, bf16[128,2048]{1,0:T(8,128)(2,1)S(1)}, u32[]{:S(2)}, u32[]{:S(2)}) collective-permute-start(bf16[128,2048]{1,0:T(8,128)(2,1)S(1)} %get-tuple-element.10), channel_id=1, source_target_pairs={{0,1},{1,0},{2,3},{3,2},{4,5},{5,4},{6,7},{7,6},{8,9},{9,8},{10,11... | collective-permute-start | bytes 1572872 | tf_op jit(solution)/shard_map/ppermute | solution.py:243
  87.9 1.5 %collective-permute-done.7 = bf16[128,2048]{1,0:T(8,128)(2,1)S(1)} collective-permute-done((bf16[128,2048]{1,0:T(8,128)(2,1)S(1)}, bf16[128,2048]{1,0:T(8,128)(2,1)S(1)}, u32[]{:S(2)}, u32[]{:S(2)}) %collective-permute-start.7) | collective-permute-done | bytes 524320 | tf_op jit(solution)/shard_map/ppermute | solution.py:243
  89.4 0.8 constant_dynamic-update-slice_fusion
  (2 shorter events, 0.1 us)
Async XLA Ops:
  0.0 12.5 %copy-start = (bf16[128,4096]{1,0:T(8,128)(2,1)S(1)}, bf16[128,4096]{1,0:T(8,128)(2,1)}, u32[]{:S(2)}) copy-start(bf16[128,4096]{1,0:T(8,128)(2,1)} %param.8) | copy-start | bytes 3145732
  2.6 48.4 %all-to-all-start = ((bf16[16,3,128,128]{3,2,1,0:T(8,128)(2,1)}), bf16[16,3,128,128]{3,2,1,0:T(8,128)(2,1)S(1)}, u32[]{:S(2)}, u32[]{:S(2)}) async-start(bf16[16,3,128,128]{3,2,1,0:T(8,128)(2,1)} %pack.1), calls=%async_computation | async-start | bytes 3145728 | tf_op jit(solution)/shard_map/all_to_all | solution.py:231
  12.6 9.7 %collective-permute-start.1 = (bf16[128,2048]{1,0:T(8,128)(2,1)S(1)}, bf16[128,2048]{1,0:T(8,128)(2,1)S(1)}, u32[]{:S(2)}, u32[]{:S(2)}) collective-permute-start(bf16[128,2048]{1,0:T(8,128)(2,1)S(1)} %constant_dynamic-slice_fusion), channel_id=1, source_target_pairs={{48,0},{193,1},{50,2},{195,3},{52,4},{197,5},{54,6},{199,7},{56,8}... | collective-permute-start | bytes 1572872 | tf_op jit(solution)/shard_map/ppermute | solution.py:221
  14.0 13.3 %collective-permute-start = (bf16[128,2048]{1,0:T(8,128)(2,1)S(1)}, bf16[128,2048]{1,0:T(8,128)(2,1)S(1)}, u32[]{:S(2)}, u32[]{:S(2)}) collective-permute-start(bf16[128,2048]{1,0:T(8,128)(2,1)S(1)} %constant_dynamic-slice_fusion), channel_id=1, source_target_pairs={{16,0},{65,1},{18,2},{67,3},{20,4},{69,5},{22,6},{71,7},{24,8},{73... | collective-permute-start | bytes 1572872 | tf_op jit(solution)/shard_map/ppermute | solution.py:221
  15.5 13.6 %collective-permute-start.2 = (bf16[128,2048]{1,0:T(8,128)(2,1)S(1)}, bf16[128,2048]{1,0:T(8,128)(2,1)S(1)}, u32[]{:S(2)}, u32[]{:S(2)}) collective-permute-start(bf16[128,2048]{1,0:T(8,128)(2,1)S(1)} %constant_dynamic-slice_fusion), channel_id=1, source_target_pairs={{32,0},{129,1},{34,2},{131,3},{36,4},{133,5},{38,6},{135,7},{40,8}... | collective-permute-start | bytes 1572872 | tf_op jit(solution)/shard_map/ppermute | solution.py:221
  29.1 7.0 %copy-start.1 = (s32[1,2048]{1,0:T(1,128)S(1)}, s32[1,2048]{1,0:T(1,128)}, u32[]{:S(2)}) copy-start(s32[1,2048]{1,0:T(1,128)} %param.9) | copy-start | bytes 24580
  30.7 48.7 %collective-permute-start.6 = (bf16[4,128,2048]{2,1,0:T(8,128)(2,1)}, bf16[4,128,2048]{2,1,0:T(8,128)(2,1)}, u32[]{:S(2)}, u32[]{:S(2)}) collective-permute-start(bf16[4,128,2048]{2,1,0:T(8,128)(2,1)} %pad_maximum_fusion.rest_0_), channel_id=1, source_target_pairs={{128,0},{33,1},{130,2},{35,3},{132,4},{37,5},{134,6},{39,7},{136,8... | collective-permute-start | bytes 6291464 | tf_op jit(solution)/shard_map/ppermute | solution.py:221
  33.4 46.7 %collective-permute-start.5 = (bf16[4,128,2048]{2,1,0:T(8,128)(2,1)}, bf16[4,128,2048]{2,1,0:T(8,128)(2,1)}, u32[]{:S(2)}, u32[]{:S(2)}) collective-permute-start(bf16[4,128,2048]{2,1,0:T(8,128)(2,1)} %pad_maximum_fusion.rest_0_), channel_id=1, source_target_pairs={{192,0},{49,1},{194,2},{51,3},{196,4},{53,5},{198,6},{55,7},{200,8... | collective-permute-start | bytes 6291464 | tf_op jit(solution)/shard_map/ppermute | solution.py:221
  33.7 46.5 %collective-permute-start.4 = (bf16[4,128,2048]{2,1,0:T(8,128)(2,1)}, bf16[4,128,2048]{2,1,0:T(8,128)(2,1)}, u32[]{:S(2)}, u32[]{:S(2)}) collective-permute-start(bf16[4,128,2048]{2,1,0:T(8,128)(2,1)} %pad_maximum_fusion.rest_0_), channel_id=1, source_target_pairs={{64,0},{17,1},{66,2},{19,3},{68,4},{21,5},{70,6},{23,7},{72,8},{25... | collective-permute-start | bytes 6291464 | tf_op jit(solution)/shard_map/ppermute | solution.py:221
  79.3 1.9 %collective-permute-start.3 = (bf16[16,128,128]{2,1,0:T(8,128)(2,1)S(1)}, bf16[16,128,128]{2,1,0:T(8,128)(2,1)S(1)}, u32[]{:S(2)}, u32[]{:S(2)}) collective-permute-start(bf16[16,128,128]{2,1,0:T(8,128)(2,1)S(1)} %all_to_all.10.mine_ref), channel_id=1, source_target_pairs={{0,1},{1,0},{2,3},{3,2},{4,5},{5,4},{6,7},{7,6},{8,9},{9,8},{10,11... | collective-permute-start | bytes 1572872 | tf_op jit(solution)/shard_map/ppermute | solution.py:241
  87.0 2.5 %collective-permute-start.7 = (bf16[128,2048]{1,0:T(8,128)(2,1)S(1)}, bf16[128,2048]{1,0:T(8,128)(2,1)S(1)}, u32[]{:S(2)}, u32[]{:S(2)}) collective-permute-start(bf16[128,2048]{1,0:T(8,128)(2,1)S(1)} %get-tuple-element.10), channel_id=1, source_target_pairs={{0,1},{1,0},{2,3},{3,2},{4,5},{5,4},{6,7},{7,6},{8,9},{9,8},{10,11... | collective-permute-start | bytes 1572872 | tf_op jit(solution)/shard_map/ppermute | solution.py:243

commit v9 on v8

--- a/solution.py
+++ b/solution.py
@@ -151,8 +151,8 @@
             at += count
     y, x, core = place_ref[0], place_ref[1], place_ref[2]
     for i, (far, near) in enumerate(places):
-        dy = jnp.where(core == 0, far, near)
-        dx = jnp.where(core == 0, near, far)
+        dy = jnp.where(core == 1, far, near)
+        dx = jnp.where(core == 1, near, far)
         head = ((y + dy) % SIDE) * SIDE + (x + dx) % SIDE
         left_ref[:rows, i * HDIM:(i + 1) * HDIM] = mine_ref[head]
         left_ref[rows:, i * HDIM:(i + 1) * HDIM] = theirs_ref[head]
@@ -212,7 +212,7 @@
     for y in range(SIDE):
         for x in range(SIDE):
             for place in range(count):
-                along_x = (place % 2 == 0) == near
+                along_x = (place % 2 == 1) == near
                 source_y = y if along_x else (y + step) % SIDE
                 source_x = (x + step) % SIDE if along_x else x
                 pairs.append(

time: 90.5 us -> 90.5 us (level)
  transfers between devices with their start and end apart: 9 -> 9, of which waited for: 8 -> 7; matrix products, arithmetic and copies ran while one was open for 4% -> 4% of each run, Pallas kernels for 8% -> 7%
where the time goes in v9:
time: 90.5 us; the launch traced here: 90.3 us
  waiting for transfers between devices  28.2 us (31%)
  blocking collectives  21.6 us (24%)
  starting transfers between devices  20.9 us (23%)
  Pallas kernels  15 us (17%)
  other arithmetic  3.72 us (4%)
  local copies, waits for them, and re-layouts  0.91 us (1%)
    all_to_all x1, blocking collectives, per_device(): mine = lax.all_to_all(attended, 'ctx', 0, 0, tiled=True)  21.6 us
    all_to_all x1, waiting for transfers between devices, per_device(): lax.all_to_all(pack(queries, keys, values), 'ctx', 0, 0, tiled=True)  12.9 us
    ppermute x6, waiting for transfers between devices, fetch(): return lax.ppermute(piece, ('fsdp', 'ctx'), pairs)  12.8 us
    all_to_all x1, starting transfers between devices, per_device(): lax.all_to_all(pack(queries, keys, values), 'ctx', 0, 0, tiled=True)  9.98 us
    ppermute x6, starting transfers between devices, fetch(): return lax.ppermute(piece, ('fsdp', 'ctx'), pairs)  9.88 us
    pallas_call x1, Pallas kernels, head_attention(): pl.pallas_call(attention_kernel, out_shape=jax.ShapeDtypeStruct((blocks,...  6.71 us
    pallas_call x1, Pallas kernels, project(): pl.pallas_call(functools.partial(projection_kernel, places), out_shape=(j...  5.71 us
    pallas_call x1, Pallas kernels, pack(): pl.pallas_call(pack_kernel, out_shape=jax.ShapeDtypeStruct((heads, 3, row...  2.55 us
  transfers between devices with their start and end apart: 9, of which 7 were waited for; matrix products, arithmetic and copies ran while one was open for 4% of the time, Pallas kernels for 7%

profile of v9, /device:TPU:1, one launch (start us, length us, event | category | flops | bytes accessed | tf_op | source)
XLA Modules:
  0.0 90.3 jit_solution(10617358033590407475)
XLA Ops:
  0.0 0.0 copy-start
  0.0 2.5 %pack.1 = bf16[16,3,128,128]{3,2,1,0:T(8,128)(2,1)} custom-call(bf16[128,2048]{1,0:T(8,128)(2,1)} %queries_ref.1, bf16[128,2048]{1,0:T(8,128)(2,1)} %keys_ref.1, bf16[128,2048]{1,0:T(8,128)(2,1)} %values_ref.1), custom_call_target="tpu_custom_call" | custom-call | tf_op jit(solution)/shard_map/pack/pallas_call | solution.py:114
  2.6 10.0 %all-to-all-start = ((bf16[16,3,128,128]{3,2,1,0:T(8,128)(2,1)}), bf16[16,3,128,128]{3,2,1,0:T(8,128)(2,1)S(1)}, u32[]{:S(2)}, u32[]{:S(2)}) async-start(bf16[16,3,128,128]{3,2,1,0:T(8,128)(2,1)} %pack.1), calls=%async_computation | async-start | bytes 3145728 | tf_op jit(solution)/shard_map/all_to_all | solution.py:231
  12.5 0.0 copy-done
  12.6 1.3 %collective-permute-start.1 = (bf16[128,2048]{1,0:T(8,128)(2,1)S(1)}, bf16[128,2048]{1,0:T(8,128)(2,1)S(1)}, u32[]{:S(2)}, u32[]{:S(2)}) collective-permute-start(bf16[128,2048]{1,0:T(8,128)(2,1)S(1)} %constant_dynamic-slice_fusion), channel_id=1, source_target_pairs={{192,0},{49,1},{194,2},{51,3},{196,4},{53,5},{198,6},{55,7},{200,8... | collective-permute-start | bytes 1572872 | tf_op jit(solution)/shard_map/ppermute | solution.py:221
  13.9 1.5 %collective-permute-start = (bf16[128,2048]{1,0:T(8,128)(2,1)S(1)}, bf16[128,2048]{1,0:T(8,128)(2,1)S(1)}, u32[]{:S(2)}, u32[]{:S(2)}) collective-permute-start(bf16[128,2048]{1,0:T(8,128)(2,1)S(1)} %constant_dynamic-slice_fusion), channel_id=1, source_target_pairs={{64,0},{17,1},{66,2},{19,3},{68,4},{21,5},{70,6},{23,7},{72,8},{25... | collective-permute-start | bytes 1572872 | tf_op jit(solution)/shard_map/ppermute | solution.py:221
  15.3 1.5 %collective-permute-start.2 = (bf16[128,2048]{1,0:T(8,128)(2,1)S(1)}, bf16[128,2048]{1,0:T(8,128)(2,1)S(1)}, u32[]{:S(2)}, u32[]{:S(2)}) collective-permute-start(bf16[128,2048]{1,0:T(8,128)(2,1)S(1)} %constant_dynamic-slice_fusion), channel_id=1, source_target_pairs={{128,0},{33,1},{130,2},{35,3},{132,4},{37,5},{134,6},{39,7},{136,8... | collective-permute-start | bytes 1572872 | tf_op jit(solution)/shard_map/ppermute | solution.py:221
  16.9 5.3 %collective-permute-done.1 = bf16[128,2048]{1,0:T(8,128)(2,1)S(1)} collective-permute-done((bf16[128,2048]{1,0:T(8,128)(2,1)S(1)}, bf16[128,2048]{1,0:T(8,128)(2,1)S(1)}, u32[]{:S(2)}, u32[]{:S(2)}) %collective-permute-start.1) | collective-permute-done | bytes 524320 | tf_op jit(solution)/shard_map/ppermute | solution.py:221
  22.2 0.0 collective-permute-done
  22.2 6.6 %collective-permute-done.2 = bf16[128,2048]{1,0:T(8,128)(2,1)S(1)} collective-permute-done((bf16[128,2048]{1,0:T(8,128)(2,1)S(1)}, bf16[128,2048]{1,0:T(8,128)(2,1)S(1)}, u32[]{:S(2)}, u32[]{:S(2)}) %collective-permute-start.2) | collective-permute-done | bytes 524320 | tf_op jit(solution)/shard_map/ppermute | solution.py:221
  28.8 0.0 copy-start.1
  28.8 1.6 %pad_maximum_fusion.rest_0_ = bf16[4,128,2048]{2,1,0:T(8,128)(2,1)} fusion(bf16[1,128,2048]{2,1,0:T(8,128)(2,1)S(1)} %bitcast.12, bf16[1,128,2048]{2,1,0:T(8,128)(2,1)S(1)} %bitcast.10, bf16[1,128,2048]{2,1,0:T(8,128)(2,1)S(1)} %bitcast.11, bf16[1,128,2048]{2,1,0:T(8,128)(2,1)S(1)} %fusion.2), kind=kLoop, calls=%fused_computation | loop fusion | flops 3145728 | bytes 4194304 | tf_op jit(solution)/shard_map/stack | solution.py:235
  30.4 2.9 %collective-permute-start.6 = (bf16[4,128,2048]{2,1,0:T(8,128)(2,1)}, bf16[4,128,2048]{2,1,0:T(8,128)(2,1)}, u32[]{:S(2)}, u32[]{:S(2)}) collective-permute-start(bf16[4,128,2048]{2,1,0:T(8,128)(2,1)} %pad_maximum_fusion.rest_0_), channel_id=1, source_target_pairs={{32,0},{129,1},{34,2},{131,3},{36,4},{133,5},{38,6},{135,7},{40,8}... | collective-permute-start | bytes 6291464 | tf_op jit(solution)/shard_map/ppermute | solution.py:221
  33.3 0.4 collective-permute-start.5
  33.7 2.3 %collective-permute-start.4 = (bf16[4,128,2048]{2,1,0:T(8,128)(2,1)}, bf16[4,128,2048]{2,1,0:T(8,128)(2,1)}, u32[]{:S(2)}, u32[]{:S(2)}) collective-permute-start(bf16[4,128,2048]{2,1,0:T(8,128)(2,1)} %pad_maximum_fusion.rest_0_), channel_id=1, source_target_pairs={{16,0},{65,1},{18,2},{67,3},{20,4},{69,5},{22,6},{71,7},{24,8},{73... | collective-permute-start | bytes 6291464 | tf_op jit(solution)/shard_map/ppermute | solution.py:221
  36.0 0.0 copy-done.1
  36.0 0.7 fusion
  36.7 1.4 %pad_add_fusion.1.bounds_ref = s32[2]{0:T(128)S(1)} fusion(s32[1]{0:T(128)} %bitcast.4, s32[1]{0:T(128)} %bitcast.3), kind=kLoop, calls=%fused_computation.6 | loop fusion | flops 2 | bytes 16 | tf_op jit(solution)/shard_map/stack | solution.py:227
  38.0 12.9 %all-to-all-done.packed_ref = bf16[16,3,128,128]{3,2,1,0:T(8,128)(2,1)S(1)} async-done(((bf16[16,3,128,128]{3,2,1,0:T(8,128)(2,1)}), bf16[16,3,128,128]{3,2,1,0:T(8,128)(2,1)S(1)}, u32[]{:S(2)}, u32[]{:S(2)}) %all-to-all-start) | async-done | bytes 1572896 | tf_op jit(solution)/shard_map/all_to_all | solution.py:231
  51.0 6.7 %head_attention.1 = bf16[16,128,128]{2,1,0:T(8,128)(2,1)S(1)} custom-call(s32[2]{0:T(128)S(1)} %pad_add_fusion.1.bounds_ref, bf16[16,3,128,128]{3,2,1,0:T(8,128)(2,1)S(1)} %all-to-all-done.packed_ref), custom_call_target="tpu_custom_call" | custom-call | tf_op jit(solution)/shard_map/head_attention/pallas_call | solution.py:127
  57.7 21.6 %all_to_all.10.mine_ref = bf16[16,128,128]{2,1,0:T(8,128)(2,1)S(1)} all-to-all(bf16[16,128,128]{2,1,0:T(8,128)(2,1)S(1)} %head_attention.1), channel_id=1, replica_groups=mesh['fsdp'=16,'ctx'=16] {'ctx'}, dimensions={0} | all-to-all | bytes 1048576 | tf_op jit(solution)/shard_map/all_to_all | solution.py:240
  79.2 0.0 collective-permute-start.3
  79.2 0.1 pad_add_fusion.place_ref
  79.3 0.0 collective-permute-done.6.rest_3_
  79.3 0.6 collective-permute-done.5.rest_2_
  79.9 0.4 collective-permute-done.4.rest_1_
  80.3 0.9 collective-permute-done.3.theirs_ref
  81.2 5.7 %project.1 = (bf16[128,4096]{1,0:T(8,128)(2,1)}, bf16[128,2048]{1,0:T(8,128)(2,1)S(1)}) custom-call(s32[3]{0:T(128)S(1)} %pad_add_fusion.place_ref, bf16[16,128,128]{2,1,0:T(8,128)(2,1)S(1)} %all_to_all.10.mine_ref, bf16[16,128,128]{2,1,0:T(8,128)(2,1)S(1)} %collective-permute-done.3.theirs_ref, bf16[4,128,2048]{2,1,0:T(8,128)(2,1)} %pad_maximum_fusion.rest_0_, ...), custom_call_target="tpu_custom_call" | custom-call | tf_op jit(solution)/shard_map/project/pallas_call | solution.py:189
  86.9 1.0 %collective-permute-start.7 = (bf16[128,2048]{1,0:T(8,128)(2,1)S(1)}, bf16[128,2048]{1,0:T(8,128)(2,1)S(1)}, u32[]{:S(2)}, u32[]{:S(2)}) collective-permute-start(bf16[128,2048]{1,0:T(8,128)(2,1)S(1)} %get-tuple-element.10), channel_id=1, source_target_pairs={{0,1},{1,0},{2,3},{3,2},{4,5},{5,4},{6,7},{7,6},{8,9},{9,8},{10,11... | collective-permute-start | bytes 1572872 | tf_op jit(solution)/shard_map/ppermute | solution.py:243
  87.9 1.5 %collective-permute-done.7 = bf16[128,2048]{1,0:T(8,128)(2,1)S(1)} collective-permute-done((bf16[128,2048]{1,0:T(8,128)(2,1)S(1)}, bf16[128,2048]{1,0:T(8,128)(2,1)S(1)}, u32[]{:S(2)}, u32[]{:S(2)}) %collective-permute-start.7) | collective-permute-done | bytes 524320 | tf_op jit(solution)/shard_map/ppermute | solution.py:243
  89.4 0.8 constant_dynamic-update-slice_fusion
  (2 shorter events, 0.1 us)
Async XLA Ops:
  0.0 12.5 %copy-start = (bf16[128,4096]{1,0:T(8,128)(2,1)S(1)}, bf16[128,4096]{1,0:T(8,128)(2,1)}, u32[]{:S(2)}) copy-start(bf16[128,4096]{1,0:T(8,128)(2,1)} %param.8) | copy-start | bytes 3145732
  2.6 48.4 %all-to-all-start = ((bf16[16,3,128,128]{3,2,1,0:T(8,128)(2,1)}), bf16[16,3,128,128]{3,2,1,0:T(8,128)(2,1)S(1)}, u32[]{:S(2)}, u32[]{:S(2)}) async-start(bf16[16,3,128,128]{3,2,1,0:T(8,128)(2,1)} %pack.1), calls=%async_computation | async-start | bytes 3145728 | tf_op jit(solution)/shard_map/all_to_all | solution.py:231
  12.6 9.6 %collective-permute-start.1 = (bf16[128,2048]{1,0:T(8,128)(2,1)S(1)}, bf16[128,2048]{1,0:T(8,128)(2,1)S(1)}, u32[]{:S(2)}, u32[]{:S(2)}) collective-permute-start(bf16[128,2048]{1,0:T(8,128)(2,1)S(1)} %constant_dynamic-slice_fusion), channel_id=1, source_target_pairs={{192,0},{49,1},{194,2},{51,3},{196,4},{53,5},{198,6},{55,7},{200,8... | collective-permute-start | bytes 1572872 | tf_op jit(solution)/shard_map/ppermute | solution.py:221
  13.9 8.3 %collective-permute-start = (bf16[128,2048]{1,0:T(8,128)(2,1)S(1)}, bf16[128,2048]{1,0:T(8,128)(2,1)S(1)}, u32[]{:S(2)}, u32[]{:S(2)}) collective-permute-start(bf16[128,2048]{1,0:T(8,128)(2,1)S(1)} %constant_dynamic-slice_fusion), channel_id=1, source_target_pairs={{64,0},{17,1},{66,2},{19,3},{68,4},{21,5},{70,6},{23,7},{72,8},{25... | collective-permute-start | bytes 1572872 | tf_op jit(solution)/shard_map/ppermute | solution.py:221
  15.3 13.5 %collective-permute-start.2 = (bf16[128,2048]{1,0:T(8,128)(2,1)S(1)}, bf16[128,2048]{1,0:T(8,128)(2,1)S(1)}, u32[]{:S(2)}, u32[]{:S(2)}) collective-permute-start(bf16[128,2048]{1,0:T(8,128)(2,1)S(1)} %constant_dynamic-slice_fusion), channel_id=1, source_target_pairs={{128,0},{33,1},{130,2},{35,3},{132,4},{37,5},{134,6},{39,7},{136,8... | collective-permute-start | bytes 1572872 | tf_op jit(solution)/shard_map/ppermute | solution.py:221
  28.8 7.2 %copy-start.1 = (s32[1,2048]{1,0:T(1,128)S(1)}, s32[1,2048]{1,0:T(1,128)}, u32[]{:S(2)}) copy-start(s32[1,2048]{1,0:T(1,128)} %param.9) | copy-start | bytes 24580
  30.4 48.9 %collective-permute-start.6 = (bf16[4,128,2048]{2,1,0:T(8,128)(2,1)}, bf16[4,128,2048]{2,1,0:T(8,128)(2,1)}, u32[]{:S(2)}, u32[]{:S(2)}) collective-permute-start(bf16[4,128,2048]{2,1,0:T(8,128)(2,1)} %pad_maximum_fusion.rest_0_), channel_id=1, source_target_pairs={{32,0},{129,1},{34,2},{131,3},{36,4},{133,5},{38,6},{135,7},{40,8}... | collective-permute-start | bytes 6291464 | tf_op jit(solution)/shard_map/ppermute | solution.py:221
  33.3 46.6 %collective-permute-start.5 = (bf16[4,128,2048]{2,1,0:T(8,128)(2,1)}, bf16[4,128,2048]{2,1,0:T(8,128)(2,1)}, u32[]{:S(2)}, u32[]{:S(2)}) collective-permute-start(bf16[4,128,2048]{2,1,0:T(8,128)(2,1)} %pad_maximum_fusion.rest_0_), channel_id=1, source_target_pairs={{48,0},{193,1},{50,2},{195,3},{52,4},{197,5},{54,6},{199,7},{56,8}... | collective-permute-start | bytes 6291464 | tf_op jit(solution)/shard_map/ppermute | solution.py:221
  33.7 46.5 %collective-permute-start.4 = (bf16[4,128,2048]{2,1,0:T(8,128)(2,1)}, bf16[4,128,2048]{2,1,0:T(8,128)(2,1)}, u32[]{:S(2)}, u32[]{:S(2)}) collective-permute-start(bf16[4,128,2048]{2,1,0:T(8,128)(2,1)} %pad_maximum_fusion.rest_0_), channel_id=1, source_target_pairs={{16,0},{65,1},{18,2},{67,3},{20,4},{69,5},{22,6},{71,7},{24,8},{73... | collective-permute-start | bytes 6291464 | tf_op jit(solution)/shard_map/ppermute | solution.py:221
  79.2 1.9 %collective-permute-start.3 = (bf16[16,128,128]{2,1,0:T(8,128)(2,1)S(1)}, bf16[16,128,128]{2,1,0:T(8,128)(2,1)S(1)}, u32[]{:S(2)}, u32[]{:S(2)}) collective-permute-start(bf16[16,128,128]{2,1,0:T(8,128)(2,1)S(1)} %all_to_all.10.mine_ref), channel_id=1, source_target_pairs={{0,1},{1,0},{2,3},{3,2},{4,5},{5,4},{6,7},{7,6},{8,9},{9,8},{10,11... | collective-permute-start | bytes 1572872 | tf_op jit(solution)/shard_map/ppermute | solution.py:241
  86.9 2.6 %collective-permute-start.7 = (bf16[128,2048]{1,0:T(8,128)(2,1)S(1)}, bf16[128,2048]{1,0:T(8,128)(2,1)S(1)}, u32[]{:S(2)}, u32[]{:S(2)}) collective-permute-start(bf16[128,2048]{1,0:T(8,128)(2,1)S(1)} %get-tuple-element.10), channel_id=1, source_target_pairs={{0,1},{1,0},{2,3},{3,2},{4,5},{5,4},{6,7},{7,6},{8,9},{9,8},{10,11... | collective-permute-start | bytes 1572872 | tf_op jit(solution)/shard_map/ppermute | solution.py:243

commit v10 on v8

--- a/solution.py
+++ b/solution.py
@@ -13,7 +13,7 @@
 HALF = TILE // 2
 MASKED = -1e30
 SIDE = 4
-NEAR = (0, 1, 3, 2)
+NEAR = (0, 1, 2, 3)
 STRIP = 512
 
 

time: 90.5 us -> 90.5 us (level)
  Pallas kernels: 15 us -> 13.4 us
  waiting for transfers between devices: 28.2 us -> 29.5 us
    pallas_call x1, Pallas kernels: 6.78 us -> 5.16 us  [head_attention(): pl.pallas_call(attention_kernel, out_shape=jax.ShapeDtypeStruct((blocks,...]
    all_to_all x1, waiting for transfers between devices: 12.8 us -> 14 us  [per_device(): lax.all_to_all(pack(queries, keys, values), 'ctx', 0, 0, tiled=True)]
    ppermute x6, waiting for transfers between devices: 12.8 us -> 13.9 us  [fetch(): return lax.ppermute(piece, ('fsdp', 'ctx'), pairs)]
    ppermute x1, starting transfers between devices: 0.96 us -> 1.92 us  [per_device(): got = lax.ppermute(sent, 'ctx', swap)]
    ppermute x1, waiting for transfers between devices: 0.96 us -> 0.01 us  [per_device(): theirs = lax.ppermute(mine, 'ctx', swap)]
  transfers between devices with their start and end apart: 9 -> 9, of which waited for: 8 -> 5; matrix products, arithmetic and copies ran while one was open for 4% -> 4% of each run, Pallas kernels for 8% -> 6%
where the time goes in v10:
time: 90.5 us; the launch traced here: 90.3 us
  waiting for transfers between devices  29.5 us (33%)
  blocking collectives  21.6 us (24%)
  starting transfers between devices  21.2 us (23%)
  Pallas kernels  13.4 us (15%)
  other arithmetic  3.72 us (4%)
  local copies, waits for them, and re-layouts  0.91 us (1%)
    all_to_all x1, blocking collectives, per_device(): mine = lax.all_to_all(attended, 'ctx', 0, 0, tiled=True)  21.6 us
    all_to_all x1, waiting for transfers between devices, per_device(): lax.all_to_all(pack(queries, keys, values), 'ctx', 0, 0, tiled=True)  14 us
    ppermute x6, waiting for transfers between devices, fetch(): return lax.ppermute(piece, ('fsdp', 'ctx'), pairs)  13.9 us
    all_to_all x1, starting transfers between devices, per_device(): lax.all_to_all(pack(queries, keys, values), 'ctx', 0, 0, tiled=True)  9.98 us
    ppermute x6, starting transfers between devices, fetch(): return lax.ppermute(piece, ('fsdp', 'ctx'), pairs)  9.28 us
    pallas_call x1, Pallas kernels, project(): pl.pallas_call(functools.partial(projection_kernel, places), out_shape=(j...  5.71 us
    pallas_call x1, Pallas kernels, head_attention(): pl.pallas_call(attention_kernel, out_shape=jax.ShapeDtypeStruct((blocks,...  5.16 us
    pallas_call x1, Pallas kernels, pack(): pl.pallas_call(pack_kernel, out_shape=jax.ShapeDtypeStruct((heads, 3, row...  2.55 us
  transfers between devices with their start and end apart: 9, of which 5 were waited for; matrix products, arithmetic and copies ran while one was open for 4% of the time, Pallas kernels for 6%

profile of v10, /device:TPU:1, one launch (start us, length us, event | category | flops | bytes accessed | tf_op | source)
XLA Modules:
  0.0 90.3 jit_solution(15073343869062001949)
XLA Ops:
  0.0 0.0 copy-start
  0.0 2.5 %pack.1 = bf16[16,3,128,128]{3,2,1,0:T(8,128)(2,1)} custom-call(bf16[128,2048]{1,0:T(8,128)(2,1)} %queries_ref.1, bf16[128,2048]{1,0:T(8,128)(2,1)} %keys_ref.1, bf16[128,2048]{1,0:T(8,128)(2,1)} %values_ref.1), custom_call_target="tpu_custom_call" | custom-call | tf_op jit(solution)/shard_map/pack/pallas_call | solution.py:114
  2.6 10.0 %all-to-all-start = ((bf16[16,3,128,128]{3,2,1,0:T(8,128)(2,1)}), bf16[16,3,128,128]{3,2,1,0:T(8,128)(2,1)S(1)}, u32[]{:S(2)}, u32[]{:S(2)}) async-start(bf16[16,3,128,128]{3,2,1,0:T(8,128)(2,1)} %pack.1), calls=%async_computation | async-start | bytes 3145728 | tf_op jit(solution)/shard_map/all_to_all | solution.py:231
  12.5 0.0 copy-done
  12.6 3.0 %collective-permute-start.1 = (bf16[128,2048]{1,0:T(8,128)(2,1)S(1)}, bf16[128,2048]{1,0:T(8,128)(2,1)S(1)}, u32[]{:S(2)}, u32[]{:S(2)}) collective-permute-start(bf16[128,2048]{1,0:T(8,128)(2,1)S(1)} %constant_dynamic-slice_fusion), channel_id=1, source_target_pairs={{32,0},{129,1},{34,2},{131,3},{36,4},{133,5},{38,6},{135,7},{40,8}... | collective-permute-start | bytes 1572872 | tf_op jit(solution)/shard_map/ppermute | solution.py:221
  15.6 0.8 collective-permute-start
  16.4 0.7 collective-permute-start.2
  17.1 5.5 %collective-permute-done.1 = bf16[128,2048]{1,0:T(8,128)(2,1)S(1)} collective-permute-done((bf16[128,2048]{1,0:T(8,128)(2,1)S(1)}, bf16[128,2048]{1,0:T(8,128)(2,1)S(1)}, u32[]{:S(2)}, u32[]{:S(2)}) %collective-permute-start.1) | collective-permute-done | bytes 524320 | tf_op jit(solution)/shard_map/ppermute | solution.py:221
  22.6 6.0 %collective-permute-done = bf16[128,2048]{1,0:T(8,128)(2,1)S(1)} collective-permute-done((bf16[128,2048]{1,0:T(8,128)(2,1)S(1)}, bf16[128,2048]{1,0:T(8,128)(2,1)S(1)}, u32[]{:S(2)}, u32[]{:S(2)}) %collective-permute-start) | collective-permute-done | bytes 524320 | tf_op jit(solution)/shard_map/ppermute | solution.py:221
  28.5 0.0 collective-permute-done.2
  28.5 0.0 copy-start.1
  28.5 1.6 %pad_maximum_fusion.rest_0_ = bf16[4,128,2048]{2,1,0:T(8,128)(2,1)} fusion(bf16[1,128,2048]{2,1,0:T(8,128)(2,1)S(1)} %bitcast.12, bf16[1,128,2048]{2,1,0:T(8,128)(2,1)S(1)} %bitcast.10, bf16[1,128,2048]{2,1,0:T(8,128)(2,1)S(1)} %bitcast.11, bf16[1,128,2048]{2,1,0:T(8,128)(2,1)S(1)} %fusion.2), kind=kLoop, calls=%fused_computation | loop fusion | flops 3145728 | bytes 4194304 | tf_op jit(solution)/shard_map/stack | solution.py:235
  30.1 1.2 %collective-permute-start.6 = (bf16[4,128,2048]{2,1,0:T(8,128)(2,1)}, bf16[4,128,2048]{2,1,0:T(8,128)(2,1)}, u32[]{:S(2)}, u32[]{:S(2)}) collective-permute-start(bf16[4,128,2048]{2,1,0:T(8,128)(2,1)} %pad_maximum_fusion.rest_0_), channel_id=1, source_target_pairs={{192,0},{49,1},{194,2},{51,3},{196,4},{53,5},{198,6},{55,7},{200,8... | collective-permute-start | bytes 6291464 | tf_op jit(solution)/shard_map/ppermute | solution.py:221
  31.3 2.5 %collective-permute-start.5 = (bf16[4,128,2048]{2,1,0:T(8,128)(2,1)}, bf16[4,128,2048]{2,1,0:T(8,128)(2,1)}, u32[]{:S(2)}, u32[]{:S(2)}) collective-permute-start(bf16[4,128,2048]{2,1,0:T(8,128)(2,1)} %pad_maximum_fusion.rest_0_), channel_id=1, source_target_pairs={{128,0},{33,1},{130,2},{35,3},{132,4},{37,5},{134,6},{39,7},{136,8... | collective-permute-start | bytes 6291464 | tf_op jit(solution)/shard_map/ppermute | solution.py:221
  33.8 1.2 %collective-permute-start.4 = (bf16[4,128,2048]{2,1,0:T(8,128)(2,1)}, bf16[4,128,2048]{2,1,0:T(8,128)(2,1)}, u32[]{:S(2)}, u32[]{:S(2)}) collective-permute-start(bf16[4,128,2048]{2,1,0:T(8,128)(2,1)} %pad_maximum_fusion.rest_0_), channel_id=1, source_target_pairs={{64,0},{17,1},{66,2},{19,3},{68,4},{21,5},{70,6},{23,7},{72,8},{25... | collective-permute-start | bytes 6291464 | tf_op jit(solution)/shard_map/ppermute | solution.py:221
  34.9 0.0 copy-done.1
  34.9 0.7 fusion
  35.6 1.4 %pad_add_fusion.1.bounds_ref = s32[2]{0:T(128)S(1)} fusion(s32[1]{0:T(128)} %bitcast.4, s32[1]{0:T(128)} %bitcast.3), kind=kLoop, calls=%fused_computation.6 | loop fusion | flops 2 | bytes 16 | tf_op jit(solution)/shard_map/stack | solution.py:227
  37.0 14.0 %all-to-all-done.packed_ref = bf16[16,3,128,128]{3,2,1,0:T(8,128)(2,1)S(1)} async-done(((bf16[16,3,128,128]{3,2,1,0:T(8,128)(2,1)}), bf16[16,3,128,128]{3,2,1,0:T(8,128)(2,1)S(1)}, u32[]{:S(2)}, u32[]{:S(2)}) %all-to-all-start) | async-done | bytes 1572896 | tf_op jit(solution)/shard_map/all_to_all | solution.py:231
  51.0 5.2 %head_attention.1 = bf16[16,128,128]{2,1,0:T(8,128)(2,1)S(1)} custom-call(s32[2]{0:T(128)S(1)} %pad_add_fusion.1.bounds_ref, bf16[16,3,128,128]{3,2,1,0:T(8,128)(2,1)S(1)} %all-to-all-done.packed_ref), custom_call_target="tpu_custom_call" | custom-call | tf_op jit(solution)/shard_map/head_attention/pallas_call | solution.py:127
  56.1 21.6 %all_to_all.10.mine_ref = bf16[16,128,128]{2,1,0:T(8,128)(2,1)S(1)} all-to-all(bf16[16,128,128]{2,1,0:T(8,128)(2,1)S(1)} %head_attention.1), channel_id=1, replica_groups=mesh['fsdp'=16,'ctx'=16] {'ctx'}, dimensions={0} | all-to-all | bytes 1048576 | tf_op jit(solution)/shard_map/all_to_all | solution.py:240
  77.7 0.0 collective-permute-start.3
  77.7 0.1 pad_add_fusion.place_ref
  77.8 0.0 collective-permute-done.6.rest_3_
  77.8 2.5 %collective-permute-done.5.rest_2_ = bf16[4,128,2048]{2,1,0:T(8,128)(2,1)} collective-permute-done((bf16[4,128,2048]{2,1,0:T(8,128)(2,1)}, bf16[4,128,2048]{2,1,0:T(8,128)(2,1)}, u32[]{:S(2)}, u32[]{:S(2)}) %collective-permute-start.5) | collective-permute-done | bytes 2097184 | tf_op jit(solution)/shard_map/ppermute | solution.py:221
  80.3 0.0 collective-permute-done.4.rest_1_
  80.3 0.0 collective-permute-done.3.theirs_ref
  80.3 5.7 %project.1 = (bf16[128,4096]{1,0:T(8,128)(2,1)}, bf16[128,2048]{1,0:T(8,128)(2,1)S(1)}) custom-call(s32[3]{0:T(128)S(1)} %pad_add_fusion.place_ref, bf16[16,128,128]{2,1,0:T(8,128)(2,1)S(1)} %all_to_all.10.mine_ref, bf16[16,128,128]{2,1,0:T(8,128)(2,1)S(1)} %collective-permute-done.3.theirs_ref, bf16[4,128,2048]{2,1,0:T(8,128)(2,1)} %pad_maximum_fusion.rest_0_, ...), custom_call_target="tpu_custom_call" | custom-call | tf_op jit(solution)/shard_map/project/pallas_call | solution.py:189
  86.0 1.9 %collective-permute-start.7 = (bf16[128,2048]{1,0:T(8,128)(2,1)S(1)}, bf16[128,2048]{1,0:T(8,128)(2,1)S(1)}, u32[]{:S(2)}, u32[]{:S(2)}) collective-permute-start(bf16[128,2048]{1,0:T(8,128)(2,1)S(1)} %get-tuple-element.10), channel_id=1, source_target_pairs={{0,1},{1,0},{2,3},{3,2},{4,5},{5,4},{6,7},{7,6},{8,9},{9,8},{10,11... | collective-permute-start | bytes 1572872 | tf_op jit(solution)/shard_map/ppermute | solution.py:243
  87.9 1.5 %collective-permute-done.7 = bf16[128,2048]{1,0:T(8,128)(2,1)S(1)} collective-permute-done((bf16[128,2048]{1,0:T(8,128)(2,1)S(1)}, bf16[128,2048]{1,0:T(8,128)(2,1)S(1)}, u32[]{:S(2)}, u32[]{:S(2)}) %collective-permute-start.7) | collective-permute-done | bytes 524320 | tf_op jit(solution)/shard_map/ppermute | solution.py:243
  89.5 0.8 constant_dynamic-update-slice_fusion
  (2 shorter events, 0.1 us)
Async XLA Ops:
  0.0 12.5 %copy-start = (bf16[128,4096]{1,0:T(8,128)(2,1)S(1)}, bf16[128,4096]{1,0:T(8,128)(2,1)}, u32[]{:S(2)}) copy-start(bf16[128,4096]{1,0:T(8,128)(2,1)} %param.8) | copy-start | bytes 3145732
  2.6 48.4 %all-to-all-start = ((bf16[16,3,128,128]{3,2,1,0:T(8,128)(2,1)}), bf16[16,3,128,128]{3,2,1,0:T(8,128)(2,1)S(1)}, u32[]{:S(2)}, u32[]{:S(2)}) async-start(bf16[16,3,128,128]{3,2,1,0:T(8,128)(2,1)} %pack.1), calls=%async_computation | async-start | bytes 3145728 | tf_op jit(solution)/shard_map/all_to_all | solution.py:231
  12.6 10.0 %collective-permute-start.1 = (bf16[128,2048]{1,0:T(8,128)(2,1)S(1)}, bf16[128,2048]{1,0:T(8,128)(2,1)S(1)}, u32[]{:S(2)}, u32[]{:S(2)}) collective-permute-start(bf16[128,2048]{1,0:T(8,128)(2,1)S(1)} %constant_dynamic-slice_fusion), channel_id=1, source_target_pairs={{32,0},{129,1},{34,2},{131,3},{36,4},{133,5},{38,6},{135,7},{40,8}... | collective-permute-start | bytes 1572872 | tf_op jit(solution)/shard_map/ppermute | solution.py:221
  15.6 12.9 %collective-permute-start = (bf16[128,2048]{1,0:T(8,128)(2,1)S(1)}, bf16[128,2048]{1,0:T(8,128)(2,1)S(1)}, u32[]{:S(2)}, u32[]{:S(2)}) collective-permute-start(bf16[128,2048]{1,0:T(8,128)(2,1)S(1)} %constant_dynamic-slice_fusion), channel_id=1, source_target_pairs={{16,0},{65,1},{18,2},{67,3},{20,4},{69,5},{22,6},{71,7},{24,8},{73... | collective-permute-start | bytes 1572872 | tf_op jit(solution)/shard_map/ppermute | solution.py:221
  16.4 12.1 %collective-permute-start.2 = (bf16[128,2048]{1,0:T(8,128)(2,1)S(1)}, bf16[128,2048]{1,0:T(8,128)(2,1)S(1)}, u32[]{:S(2)}, u32[]{:S(2)}) collective-permute-start(bf16[128,2048]{1,0:T(8,128)(2,1)S(1)} %constant_dynamic-slice_fusion), channel_id=1, source_target_pairs={{48,0},{193,1},{50,2},{195,3},{52,4},{197,5},{54,6},{199,7},{56,8}... | collective-permute-start | bytes 1572872 | tf_op jit(solution)/shard_map/ppermute | solution.py:221
  28.5 6.4 %copy-start.1 = (s32[1,2048]{1,0:T(1,128)S(1)}, s32[1,2048]{1,0:T(1,128)}, u32[]{:S(2)}) copy-start(s32[1,2048]{1,0:T(1,128)} %param.9) | copy-start | bytes 24580
  30.1 47.7 %collective-permute-start.6 = (bf16[4,128,2048]{2,1,0:T(8,128)(2,1)}, bf16[4,128,2048]{2,1,0:T(8,128)(2,1)}, u32[]{:S(2)}, u32[]{:S(2)}) collective-permute-start(bf16[4,128,2048]{2,1,0:T(8,128)(2,1)} %pad_maximum_fusion.rest_0_), channel_id=1, source_target_pairs={{192,0},{49,1},{194,2},{51,3},{196,4},{53,5},{198,6},{55,7},{200,8... | collective-permute-start | bytes 6291464 | tf_op jit(solution)/shard_map/ppermute | solution.py:221
  31.3 48.9 %collective-permute-start.5 = (bf16[4,128,2048]{2,1,0:T(8,128)(2,1)}, bf16[4,128,2048]{2,1,0:T(8,128)(2,1)}, u32[]{:S(2)}, u32[]{:S(2)}) collective-permute-start(bf16[4,128,2048]{2,1,0:T(8,128)(2,1)} %pad_maximum_fusion.rest_0_), channel_id=1, source_target_pairs={{128,0},{33,1},{130,2},{35,3},{132,4},{37,5},{134,6},{39,7},{136,8... | collective-permute-start | bytes 6291464 | tf_op jit(solution)/shard_map/ppermute | solution.py:221
  33.8 46.5 %collective-permute-start.4 = (bf16[4,128,2048]{2,1,0:T(8,128)(2,1)}, bf16[4,128,2048]{2,1,0:T(8,128)(2,1)}, u32[]{:S(2)}, u32[]{:S(2)}) collective-permute-start(bf16[4,128,2048]{2,1,0:T(8,128)(2,1)} %pad_maximum_fusion.rest_0_), channel_id=1, source_target_pairs={{64,0},{17,1},{66,2},{19,3},{68,4},{21,5},{70,6},{23,7},{72,8},{25... | collective-permute-start | bytes 6291464 | tf_op jit(solution)/shard_map/ppermute | solution.py:221
  77.7 2.6 %collective-permute-start.3 = (bf16[16,128,128]{2,1,0:T(8,128)(2,1)S(1)}, bf16[16,128,128]{2,1,0:T(8,128)(2,1)S(1)}, u32[]{:S(2)}, u32[]{:S(2)}) collective-permute-start(bf16[16,128,128]{2,1,0:T(8,128)(2,1)S(1)} %all_to_all.10.mine_ref), channel_id=1, source_target_pairs={{0,1},{1,0},{2,3},{3,2},{4,5},{5,4},{6,7},{7,6},{8,9},{9,8},{10,11... | collective-permute-start | bytes 1572872 | tf_op jit(solution)/shard_map/ppermute | solution.py:241
  86.0 3.5 %collective-permute-start.7 = (bf16[128,2048]{1,0:T(8,128)(2,1)S(1)}, bf16[128,2048]{1,0:T(8,128)(2,1)S(1)}, u32[]{:S(2)}, u32[]{:S(2)}) collective-permute-start(bf16[128,2048]{1,0:T(8,128)(2,1)S(1)} %get-tuple-element.10), channel_id=1, source_target_pairs={{0,1},{1,0},{2,3},{3,2},{4,5},{5,4},{6,7},{7,6},{8,9},{9,8},{10,11... | collective-permute-start | bytes 1572872 | tf_op jit(solution)/shard_map/ppermute | solution.py:243
